TPU v7x, 32 devices: a whole 2x2x4 slice. The times are simulated.
32 devices in a mesh: grp: 4 (over y, x), sec: 8 (over z, core).
Axes of the slice: x: 2, y: 2, z: 4, core: 2. Of those that a mesh axis runs over, the one named last changes fastest.
Arguments:
- fields: bfloat16 [8, 32, 32, 192], P('grp', None, 'sec'), may hold values from -6 to 6
- valid_rows: int32 [8], P('grp'), may hold values from 8 to 32, as said below
- w_embed: bfloat16 [3, 192, 1024], replicated, may hold values from -0.25 to 0.25
- ln1_gain: bfloat16 [1024], replicated, may hold values from 0.25 to 1.75
- w_qkv: bfloat16 [1024, 3072], replicated, may hold values from -0.1875 to 0.1875
- w_out: bfloat16 [1024, 1024], replicated, may hold values from -6 to 6
- ln2_gain: bfloat16 [1024], replicated, may hold values from 0.25 to 1.75
- w_up: bfloat16 [1024, 4096], replicated, may hold values from -0.1875 to 0.1875
- b_up: bfloat16 [4096], replicated, may hold values from -3 to 3
- w_down: bfloat16 [4096, 1024], replicated, may hold values from -0.09375 to 0.09375
- w_head: bfloat16 [3, 1024, 192], replicated, may hold values from -0.109375 to 0.109375
- cotangent: bfloat16 [8, 32, 32, 192], P('grp', None, 'sec'), may hold values from -6 to 6
Outputs:
- head_output: float32 [8, 32, 32, 192], P('grp', None, 'sec')
- input_grad: float32 [8, 32, 32, 192], P('grp', None, 'sec')
- embed_grad: float32 [3, 192, 1024], P(None, None, 'sec')
- gain_one_grad: float32 [1024], P('sec')
- qkv_grad: float32 [1024, 3072], P('sec')
- out_grad: float32 [1024, 1024], P('sec')
- gain_two_grad: float32 [1024], P('sec')
- up_grad: float32 [1024, 4096], P('sec')
- bias_grad: float32 [4096], P('sec')
- down_grad: float32 [4096, 1024], P('sec')
- head_grad: float32 [3, 1024, 192], P(None, 'sec')
Inputs may be any that keep to these rules, and one draw needn't show every extreme that they name: Rows 0 to valid_rows - 1 of a sample are data, the rest padding; at least 8 rows (one at least) are data, and some sample has all 32 rows.
All inputs are finite; a program needn't handle non-finite values.
Results may differ from a plain program's by a relative error of at most 0.022.
Values may be sent and summed in bfloat16 or wider, within the bound.
No kernel may reach another device: no remote copies, remote signals or barrier semaphores. Data moves between devices by JAX's collectives and lax.ppermute only.
A program may use at most 192 MiB of HBM per device.

v0:
```python
import jax
import jax.numpy as jnp
import numpy as np
from jax import lax
from jax.experimental import pallas as pl
from jax.experimental.pallas import tpu as pltpu
from jax.sharding import PartitionSpec as P

HEAD_DIM = 64
HEADS = 16
LANES = 128
KEY_CHUNK = 512
VMEM_LIMIT = 127 * 512 * 1024
BF = jnp.bfloat16
F32 = jnp.float32

NN = ((1,), (0,))
NT = ((1,), (1,))
TN = ((0,), (0,))

MICROS = {
    "embed_qkv": 9.6,
    "cotangent_grad": 6.1,
    "attention_fwd": 9.2,
    "mlp": 17.0,
    "trunk_part": 4.0,
    "norm_two_back": 4.9,
    "attention_bwd": 13.3,
    "norm_one_grad": 11.7,
    "trunk_head": 7.0,
    "embed_back": 9.0,
    "mlp_weight_grads": 11.5,
    "attention_weight_grads": 9.0,
    "pick_team": 3.4,
    "pick_member": 2.5,
    "mlp_grads_out": 4.7,
    "attention_grads_out": 3.5,
    "edge_grads_out": 2.8,
}

TEAM, ME, GRP, VALID = range(4)


def dot(a, b, dims):
    return lax.dot_general(a, b, (dims, ((), ())), preferred_element_type=F32)


def swap(x, axis, bit):
    n = lax.axis_size(axis)
    return lax.ppermute(x, axis, [(i, i ^ bit) for i in range(n)])


def kernel(body, name, scalars, grid, ins, outs, scratch=(), aliases=None):
    micros = MICROS[name]
    scalars, chain = scalars
    values = lax.optimization_barrier((scalars, *chain))[0] if chain else scalars
    def spec(block, index):
        if block is None:
            return pl.BlockSpec(memory_space=pl.ANY)
        return pl.BlockSpec(block, index)

    results = pl.pallas_call(
        body,
        grid_spec=pltpu.PrefetchScalarGridSpec(
            num_scalar_prefetch=1,
            grid=grid,
            in_specs=[spec(block, index) for _, block, index in ins],
            out_specs=[spec(block, index) for _, _, block, index in outs],
            scratch_shapes=list(scratch),
        ),
        out_shape=[jax.ShapeDtypeStruct(shape, kind) for shape, kind, _, _ in outs],
        input_output_aliases=aliases or {},
        compiler_params=pltpu.CompilerParams(vmem_limit_bytes=VMEM_LIMIT),
        cost_estimate=pl.CostEstimate(
            flops=int(micros * 1.15e9), transcendentals=0, bytes_accessed=int(micros * 3.6e6)
        ),
        name=name,
    )(values, *[array for array, _, _ in ins])
    chain[:] = [results[-1]]
    return results


def hold(scalars, *values):
    scalars[1].extend(values)


def whole(array):
    rank = len(array.shape)
    return (array, array.shape, lambda *_: (0,) * rank)


def whole_out(shape, kind):
    rank = len(shape)
    return (shape, kind, shape, lambda *_: (0,) * rank)


class Sizes:
    def __init__(self, fields, w_qkv, w_up):
        self.teams, self.lat, self.cols, self.chan = fields.shape
        self.sectors = lax.axis_size("sec")
        self.members = self.sectors // self.teams
        self.group = lax.axis_size("grp")
        self.d = w_qkv.shape[0]
        self.ff = w_up.shape[1]
        self.sec_tokens = self.lat * self.cols
        self.tokens = self.sectors * self.sec_tokens
        self.heads = HEADS // self.members
        self.width = self.heads * HEAD_DIM
        self.db = self.d // self.sectors
        self.fb = self.ff // self.sectors
        self.dn = self.teams * self.db
        self.fn = self.teams * self.fb
        self.own = self.tokens // self.members
        self.half = self.tokens // 2


def line_up(s, scalars, pieces, canon):
    for j, piece in enumerate(pieces):
        for k in range(s.teams):
            at = (scalars[TEAM] ^ k) * s.members + (scalars[ME] ^ j)
            canon[at] = piece[k]


def beside(s, canon, sector):
    mid = canon[sector].astype(F32)
    before = canon[lax.rem(sector + s.sectors - 1, s.sectors)].astype(F32)
    after = canon[lax.rem(sector + 1, s.sectors)].astype(F32)
    col = lax.rem(lax.broadcasted_iota(jnp.int32, mid.shape, 0), s.cols)
    rows = s.sec_tokens
    west = jnp.where(col == 0, pltpu.roll(before, rows - (s.cols - 1), 0), pltpu.roll(mid, 1, 0))
    east = jnp.where(col == s.cols - 1, pltpu.roll(after, s.cols - 1, 0), pltpu.roll(mid, rows - 1, 0))
    return west, mid, east


def row_stats(rows):
    mean = jnp.mean(rows, axis=-1, keepdims=True)
    center = rows - mean
    return mean, lax.rsqrt(jnp.mean(center * center, axis=-1, keepdims=True) + 1e-05)


def normed_rows(rows):
    mean, rstd = row_stats(rows)
    return (rows - mean) * rstd, rstd


def embed_qkv(s, scalars, pieces, w_embed, gain, w_qkv):
    rows = s.half
    per = rows // s.sec_tokens
    chunk = s.sec_tokens

    def body(sc, *refs):
        parts = refs[: s.members]
        we, g, wq, wk, wv = refs[s.members : s.members + 5]
        cat_ref, hid_ref, norm_ref, qkv_ref, stat_ref, canon = refs[s.members + 5 :]
        i = pl.program_id(0)

        @pl.when(i == 0)
        def _():
            line_up(s, sc, parts, canon)

        for p in range(per):
            at = slice(p * chunk, (p + 1) * chunk)
            west, mid, east = beside(s, canon, i * per + p)
            cat_ref[at, :] = jnp.concatenate([west, mid, east], axis=1).astype(BF)
        hid_ref[...] = dot(cat_ref[...], we[...], NN)
        lane = lax.broadcasted_iota(jnp.int32, (chunk, LANES), 1)
        for p in range(per):
            at = slice(p * chunk, (p + 1) * chunk)
            value = hid_ref[at, :]
            mean, rstd = row_stats(value)
            norm_ref[at, :] = ((value - mean) * rstd * g[...]).astype(BF)
            stat_ref[at, :] = jnp.where(lane == 0, mean, rstd)
        for k, w in enumerate((wq, wk, wv)):
            qkv_ref[:, k * s.width : (k + 1) * s.width] = dot(norm_ref[...], w[...], NN).astype(BF)

    def third(k):
        return (w_qkv, (s.d, s.width), lambda i, sc: (0, k * s.members + sc[ME]))

    row = lambda i, sc: (i, 0)
    return kernel(
        body,
        "embed_qkv",
        scalars,
        (s.tokens // rows,),
        [whole(p) for p in pieces] + [whole(w_embed), whole(gain), third(0), third(1), third(2)],
        [
            ((s.tokens, 3 * s.chan), BF, (rows, 3 * s.chan), row),
            ((s.tokens, s.d), F32, (rows, s.d), row),
            ((s.tokens, s.d), BF, (rows, s.d), row),
            ((s.tokens, 3 * s.width), BF, (rows, 3 * s.width), row),
            ((s.tokens, LANES), F32, (rows, LANES), row),
        ],
        [pltpu.VMEM((s.sectors, s.sec_tokens, s.chan), BF)],
    )


def cotangent_grad(s, scalars, pieces, w_head):
    rows = s.half
    per = rows // s.sec_tokens

    def body(sc, *refs):
        parts = refs[: s.members]
        wh, cat_ref, grad_ref, canon = refs[s.members :]
        i = pl.program_id(0)

        @pl.when(i == 0)
        def _():
            line_up(s, sc, parts, canon)

        for p in range(per):
            at = slice(p * s.sec_tokens, (p + 1) * s.sec_tokens)
            west, mid, east = beside(s, canon, i * per + p)
            cat_ref[at, :] = jnp.concatenate([east, mid, west], axis=1).astype(BF)
        grad_ref[...] = dot(cat_ref[...], wh[...], NN).astype(BF)

    row = lambda i, sc: (i, 0)
    return kernel(
        body,
        "cotangent_grad",
        scalars,
        (s.tokens // rows,),
        [whole(p) for p in pieces] + [whole(w_head)],
        [
            ((s.tokens, 3 * s.chan), BF, (rows, 3 * s.chan), row),
            ((s.tokens, s.d), BF, (rows, s.d), row),
        ],
        [pltpu.VMEM((s.sectors, s.sec_tokens, s.chan), BF)],
    )


def side_of(s, sc, far):
    own = sc[ME] // (s.members // 2)
    return own ^ 1 if far else own


def lanes_of(value, side):
    lane = lax.broadcasted_iota(jnp.int32, value.shape, 1)
    return jnp.where(lane // HEAD_DIM == side, value, jnp.zeros_like(value))


def attention_fwd(s, scalars, qkv, far):
    rows = s.own
    steps = s.half // rows
    chunk = KEY_CHUNK

    def body(sc, q_ref, kv_ref, att_ref, weight_ref, inv_ref, bias, values, buf_a, buf_b, top_a, top_b, outs, invs):
        @pl.when(pl.program_id(0) == 0)
        def _():
            key = lax.broadcasted_iota(jnp.int32, (s.tokens, LANES), 0)
            bias[...] = jnp.where(lax.rem(key, s.sec_tokens) // s.cols < sc[VALID], 0.0, -1e30)
            values[...] = jnp.transpose(kv_ref[:, 2 * s.width :].astype(F32)).astype(BF)
            invs[...] = jnp.zeros_like(invs)

        def score(p, side, buf, tops):
            at = pl.ds(pl.multiple_of(p * LANES, LANES), LANES)
            kat = pl.ds(pl.multiple_of(s.width + p * LANES, LANES), LANES)
            query = lanes_of(q_ref[:, at] * jnp.asarray(0.125, BF), side)
            top = None
            for c in range(0, s.tokens, chunk):
                rows_at = slice(c, c + chunk)
                wide = jnp.concatenate([bias[rows_at, :]] * (rows // LANES), axis=1)
                scores = dot(kv_ref[rows_at, kat], query, NT) + wide
                buf[rows_at, :] = scores
                peak = jnp.max(scores, axis=0, keepdims=True)
                top = peak if top is None else jnp.maximum(top, peak)
            tops[...] = jnp.broadcast_to(top, tops.shape)

        def weigh(p, side, buf, tops):
            h = 2 * p + side
            heads_at = pl.ds(pl.multiple_of(h * HEAD_DIM, HEAD_DIM), HEAD_DIM)
            top = tops[0:1, :]
            total = None
            out = None
            for c in range(0, s.tokens, chunk):
                at = slice(c, c + chunk)
                weights = jnp.exp(buf[at, :] - top)
                part = jnp.sum(weights, axis=0, keepdims=True)
                low = weights.astype(BF)
                weight_ref[h, 0, at, :] = low
                more = dot(values[heads_at, at], low, NN)
                total = part if total is None else total + part
                out = more if out is None else out + more
            inv = 1.0 / total
            invs[pl.ds(pl.multiple_of(h * 8, 8), 8), :] = jnp.broadcast_to(inv, (8, rows))
            outs[heads_at, :] = out * inv

        score(0, 0, buf_a, top_a)

        def pair_step(p, carry):
            weigh(p, 0, buf_a, top_a)
            score(p, 1, buf_b, top_b)

            @pl.when(p >= 0)
            def _():
                weigh(p, 1, buf_b, top_b)
                score(jnp.minimum(p + 1, s.heads // 2 - 1), 0, buf_a, top_a)

            return carry

        lax.fori_loop(0, s.heads // 2, pair_step, 0)
        att_ref[...] = jnp.transpose(outs[...]).astype(BF)
        inv_ref[...] = jnp.transpose(invs[...])

    row = lambda i, sc: (i, 0)
    return kernel(
        body,
        "attention_fwd",
        scalars,
        (steps,),
        [
            (qkv, (rows, 3 * s.width), lambda i, sc: (side_of(s, sc, far) * steps + i, 0)),
            whole(qkv),
        ],
        [
            ((s.half, s.width), BF, (rows, s.width), row),
            ((s.heads, steps, s.tokens, rows), BF, (s.heads, 1, s.tokens, rows), lambda i, sc: (0, i, 0, 0)),
            ((s.half, LANES), F32, (rows, LANES), row),
        ],
        [
            pltpu.VMEM((s.tokens, LANES), F32),
            pltpu.VMEM((s.width, s.tokens), BF),
            pltpu.VMEM((s.tokens, rows), F32),
            pltpu.VMEM((s.tokens, rows), F32),
            pltpu.VMEM((8, rows), F32),
            pltpu.VMEM((8, rows), F32),
            pltpu.VMEM((s.width, rows), F32),
            pltpu.VMEM((LANES, rows), F32),
        ],
    )


def mlp(s, scalars, att, hidden0, grad_mlp, w_out, gain, w_up, b_up, w_down, far):
    chunk = 64
    rows = s.half
    count = len(att)

    def body(sc, *refs):
        parts = refs[:count]
        h0, gm, g, bias, wo_hbm, wu_hbm, wd_hbm = refs[count : count + 7]
        outs = refs[count + 7 :]
        att_ref, n2_ref, act_ref, gpre_ref, gkeep, gsend, gsum_ref, hown, bsum, h1_ref = outs[:10]
        wo, wu, wd, pre, gact, means, rstds, sem = outs[10:]
        me = sc[ME]

        copies = [pltpu.make_async_copy(wo_hbm, wo, sem.at[0])]
        for k in range(s.teams):
            at = pl.multiple_of((k * s.members + me) * s.fb, s.fb)
            copies.append(
                pltpu.make_async_copy(
                    wu_hbm.at[:, pl.ds(at, s.fb)], wu.at[:, pl.ds(k * s.fb, s.fb)], sem.at[1 + k]
                )
            )
        for k in range(s.teams):
            at = pl.multiple_of((k * s.members + me) * s.fb, s.fb)
            copies.append(
                pltpu.make_async_copy(
                    wd_hbm.at[pl.ds(at, s.fb), :],
                    wd.at[pl.ds(k * s.fb, s.fb), :],
                    sem.at[1 + s.teams + k],
                )
            )
        for copy in copies:
            copy.start()
        for j in range(count):
            at = pl.multiple_of((me ^ j) * s.width, s.width)
            att_ref[:, pl.ds(at, s.width)] = parts[j][...]
        copies[0].wait()
        span = 512

        def by_columns(size, one):
            def step(n, carry):
                one(pl.ds(pl.multiple_of(n * span, span), span))
                return carry

            lax.fori_loop(0, size // span, step, 0)

        def attention_out(cols):
            h1_ref[:, cols] = h0[:, cols] + dot(att_ref[...], wo[:, cols], NN)

        by_columns(s.d, attention_out)

        def norm_chunk(c, carry):
            at = pl.ds(pl.multiple_of(c * chunk, chunk), chunk)
            value = h1_ref[at, :]
            mean, rstd = row_stats(value)
            n2_ref[at, :] = ((value - mean) * rstd * g[...]).astype(BF)
            means[at, :] = jnp.broadcast_to(mean, (chunk, LANES))
            rstds[at, :] = jnp.broadcast_to(rstd, (chunk, LANES))
            return carry

        lax.fori_loop(0, rows // chunk, norm_chunk, 0)
        for k in range(s.teams):
            at = pl.multiple_of((k * s.members + me) * s.db, s.db)
            hown[:, k * s.db : (k + 1) * s.db] = h1_ref[:, pl.ds(at, s.db)]
        for copy in copies[1 : 1 + s.teams]:
            copy.wait()

        def up_out(cols):
            pre[:, cols] = dot(n2_ref[...], wu[:, cols], NN)

        by_columns(s.fn, up_out)
        for copy in copies[1 + s.teams :]:
            copy.wait()

        def down_back(cols):
            gact[:, cols] = dot(gm[...], wd[cols, :], NT)

        by_columns(s.fn, down_back)

        def gelu_chunk(c, total):
            at = pl.ds(pl.multiple_of(c * chunk, chunk), chunk)
            u = pre[at, :] + bias[...]
            cdf = 0.5 * (1.0 + lax.erf(u * np.float32(2**-0.5)))
            act_ref[at, :] = (u * cdf).astype(BF)
            slope = cdf + u * jnp.exp(-0.5 * u * u) * np.float32((2 * np.pi) ** -0.5)
            low = (gact[at, :] * slope).astype(BF)
            gpre_ref[at, :] = low
            return total + jnp.sum(low.astype(F32), axis=0, keepdims=True)

        bsum[...] = lax.fori_loop(0, rows // chunk, gelu_chunk, jnp.zeros((1, s.fn), F32))

        def up_back(cols):
            pre[:, cols] = dot(gpre_ref[...], wu[cols, :], NT)

        by_columns(s.d, up_back)

        def gain_chunk(c, total):
            at = pl.ds(pl.multiple_of(c * chunk, chunk), chunk)
            mean, rstd = means[at, :], rstds[at, :]
            sums = []
            for n in range(s.d // LANES):
                cols = slice(n * LANES, (n + 1) * LANES)
                xhat = (h1_ref[at, cols] - mean) * rstd
                sums.append(jnp.sum(pre[at, cols] * xhat, axis=0, keepdims=True))
            return total + jnp.concatenate(sums, axis=1)

        gsum = lax.fori_loop(0, rows // chunk, gain_chunk, jnp.zeros((1, s.d), F32))
        mine = lax.rem(me, 2)
        keep_at = pl.ds(pl.multiple_of(mine * s.own, s.own), s.own)
        send_at = pl.ds(pl.multiple_of((1 - mine) * s.own, s.own), s.own)
        gkeep[...] = pre[keep_at, :].astype(BF)
        gsend[...] = pre[send_at, :].astype(BF)
        gsum_ref[...] = gsum

    index = lambda i, sc: (side_of(s, sc, far), 0)
    bias_own = jnp.concatenate(
        [
            lax.dynamic_slice_in_dim(b_up, (k * s.members + scalars[0][ME]) * s.fb, s.fb, 0)
            for k in range(s.teams)
        ]
    ).astype(F32)[None]
    return kernel(
        body,
        "mlp",
        scalars,
        (1,),
        [whole(a) for a in att]
        + [
            (hidden0, (rows, s.d), index),
            (grad_mlp, (rows, s.d), index),
            whole(gain),
            whole(bias_own),
            (w_out, None, None),
            (w_up, None, None),
            (w_down, None, None),
        ],
        [
            whole_out((rows, s.d), BF),
            whole_out((rows, s.d), BF),
            whole_out((rows, s.fn), BF),
            whole_out((rows, s.fn), BF),
            whole_out((s.own, s.d), BF),
            whole_out((s.own, s.d), BF),
            whole_out((1, s.d), F32),
            whole_out((rows, s.dn), F32),
            whole_out((1, s.fn), F32),
            whole_out((rows, s.d), F32),
        ],
        [
            pltpu.VMEM((s.d, s.d), BF),
            pltpu.VMEM((s.d, s.fn), BF),
            pltpu.VMEM((s.fn, s.d), BF),
            pltpu.VMEM((rows, s.fn), F32),
            pltpu.VMEM((rows, s.fn), F32),
            pltpu.VMEM((rows, LANES), F32),
            pltpu.VMEM((rows, LANES), F32),
            pltpu.SemaphoreType.DMA((1 + 2 * s.teams,)),
        ],
    )


def trunk_part(s, scalars, parts, w_down):
    extra = 16
    rows = s.half

    def body(sc, act0, gs0, act1, gs1, *refs):
        downs, (keep, send, out, both, sums) = refs[: s.teams], refs[s.teams :]
        both[0], both[1] = act0[...], act1[...]
        sums[0], sums[1] = gs0[...], gs1[...]

        def one_half(half, carry):
            total = dot(both[half, :, : s.fb], downs[0][...], NN)
            for k in range(1, s.teams):
                total += dot(both[half, :, k * s.fb : (k + 1) * s.fb], downs[k][...], NN)
            out[:rows] = total
            out[rows:] = jnp.broadcast_to(sums[half], (extra, s.d))
            for odd, ref in ((0, keep), (1, send)):
                for n in range(s.members // 2):
                    m = sc[ME] ^ (2 * n + odd)
                    for k in range(s.teams):
                        cols = pl.ds(pl.multiple_of((k * s.members + m) * s.db, s.db), s.db)
                        ref[n, half, :, k * s.db : (k + 1) * s.db] = out[:, cols].astype(BF)
            return carry

        lax.fori_loop(0, 2, one_half, 0)

    pair = (s.members // 2, 2, rows + extra, s.dn)
    return kernel(
        body,
        "trunk_part",
        scalars,
        (1,),
        [whole(x) for part in parts for x in part]
        + [
            (w_down, (s.fb, s.d), lambda i, sc, k=k: (k * s.members + sc[ME], 0))
            for k in range(s.teams)
        ],
        [whole_out(pair, BF), whole_out(pair, BF)],
        [
            pltpu.VMEM((rows + extra, s.d), F32),
            pltpu.VMEM((2, rows, s.fn), BF),
            pltpu.VMEM((2, 1, s.d), F32),
        ],
    )


def norm_two_back(s, scalars, parts, hidden1, grad_mlp, gain):
    chunk = 64
    count = len(parts)

    def body(sc, *refs):
        h1, gm, g, out_ref = refs[count:]

        def rows_chunk(c, carry):
            at = pl.ds(pl.multiple_of(c * chunk, chunk), chunk)
            xhat, rstd = normed_rows(h1[at, :])
            grad = refs[0][at, :].astype(F32)
            for ref in refs[1:count]:
                grad += ref[at, :].astype(F32)
            grad *= g[...]
            back = grad - jnp.mean(grad, axis=-1, keepdims=True)
            back -= xhat * jnp.mean(grad * xhat, axis=-1, keepdims=True)
            out_ref[at, :] = (gm[at, :].astype(F32) + rstd * back).astype(BF)
            return carry

        lax.fori_loop(0, s.own // chunk, rows_chunk, 0)

    return kernel(
        body,
        "norm_two_back",
        scalars,
        (1,),
        [whole(p) for p in parts]
        + [
            (hidden1, (s.own, s.d), lambda i, sc: (lax.rem(sc[ME], 2), 0)),
            (grad_mlp, (s.own, s.d), lambda i, sc: (sc[ME], 0)),
            whole(gain),
        ],
        [whole_out((s.own, s.d), BF)],
    )[0]


def attention_bwd(s, scalars, qkv, saved, grads, w_out, far, before=None):
    base = s.members // 2 if far else 0
    rows = s.own
    last = before is not None
    attended, weights, inverse = saved

    def body(sc, *refs):
        q_ref, kv_ref, att_ref, weight_ref, inv_ref, first, second, wo = refs[:8]
        if last:
            old_ref = refs[10]
            dq_ref, own_ref, out_ref, gh, acc, keys = refs[11:]
        else:
            dq_ref, own_ref, out_ref, gh, acc, keys = refs[8:]
        i = pl.program_id(0)

        @pl.when(i == 0)
        def _():
            if last:
                acc[...] = old_ref[...]
            else:
                acc[...] = jnp.zeros_like(acc)
            keys[...] = jnp.transpose(kv_ref[:, s.width : 2 * s.width].astype(F32)).astype(BF)

        for step, piece in enumerate((first, second)):

            @pl.when(i == step)
            def _():
                gh[...] = dot(piece[...], wo[...], NT)
                for k in range(s.teams):
                    at = pl.multiple_of((k * s.members + sc[ME]) * s.db, s.db)
                    own_ref[:, k * s.db : (k + 1) * s.db] = piece[:, pl.ds(at, s.db)]

        def pair_step(p, carry):
            pair = pl.ds(pl.multiple_of(p * LANES, LANES), LANES)
            value_at = pl.ds(pl.multiple_of(2 * s.width + p * LANES, LANES), LANES)
            dv_at = pl.ds(pl.multiple_of(s.width + p * LANES, LANES), LANES)
            inv = inv_ref[...]
            wide = lax.broadcasted_iota(jnp.int32, inv.shape, 1)
            outs = []
            means = jnp.zeros((rows, LANES), F32)
            for side in range(2):
                h = 2 * p + side
                one = jnp.sum(jnp.where(wide == 8 * h, inv, 0.0), axis=-1, keepdims=True)
                out = (lanes_of(gh[:, pair], side) * one).astype(BF)
                mean = jnp.sum(out.astype(F32) * att_ref[:, pair].astype(F32), axis=-1, keepdims=True)
                means = jnp.where(wide == side, mean, means)
                outs.append(out)
            means = jnp.transpose(means)
            turned = [None, None]
            units = [(c, side) for c in range(0, s.tokens, KEY_CHUNK) for side in range(2)]

            def first_dot(unit):
                c, side = unit
                return dot(kv_ref[c : c + KEY_CHUNK, value_at], outs[side], NT)

            ahead = first_dot(units[0])
            for n, (c, side) in enumerate(units):
                at = slice(c, c + KEY_CHUNK)
                h = 2 * p + side
                gprob = ahead - means[side : side + 1, :]
                if n + 1 < len(units):
                    ahead = first_dot(units[n + 1])
                weight = weight_ref[h, 0, at, :]
                gscore = (weight.astype(F32) * gprob).astype(BF)
                key_rows = pl.ds(pl.multiple_of(h * HEAD_DIM, HEAD_DIM), HEAD_DIM)
                dq = dot(keys[key_rows, at], gscore, NN)
                turned[side] = dq if turned[side] is None else turned[side] + dq
                one = dot(gscore, lanes_of(q_ref[:, pair], side), NN)
                two = dot(weight, outs[side], NN)
                if side == 0:
                    dk, dv = one, two
                else:
                    acc[at, pair] += dk + one
                    acc[at, dv_at] += dv + two
            dq_ref[:, pair] = (jnp.transpose(jnp.concatenate(turned, axis=0)) * 0.125).astype(BF)
            return carry

        lax.fori_loop(0, s.heads // 2, pair_step, 0)

        @pl.when(i == pl.num_programs(0) - 1)
        def _():
            if last:
                out_ref[:, : s.width] = (acc[:, : s.width] * 0.125).astype(BF)
                out_ref[:, s.width :] = acc[:, s.width :].astype(BF)
            else:
                out_ref[...] = acc[...]

    member = lambda i, sc: (sc[ME] ^ (base + i), 0)
    side = lambda i, sc: lax.rem(sc[ME] ^ i, s.members // 2)
    ins = [
        (qkv, (rows, 3 * s.width), member),
        whole(qkv),
        (attended, (rows, s.width), lambda i, sc: (side(i, sc), 0)),
        (weights, (s.heads, 1, s.tokens, rows), lambda i, sc: (0, side(i, sc), 0, 0)),
        (inverse, (rows, LANES), lambda i, sc: (side(i, sc), 0)),
        whole(grads[0]),
        whole(grads[1]),
        (w_out, (s.width, s.d), lambda i, sc: (sc[ME], 0)),
    ]
    aliases = None
    if last:
        ins += [(before[0], None, None), (before[1], None, None), whole(before[2])]
        aliases = {9: 0, 10: 1}
    return kernel(
        body,
        "attention_bwd",
        scalars,
        (2,),
        ins,
        [
            ((s.tokens, s.width), BF, (rows, s.width), member),
            ((s.tokens, s.dn), BF, (rows, s.dn), member),
            whole_out((s.tokens, 2 * s.width), BF if last else F32),
        ],
        [
            pltpu.VMEM((rows, s.width), F32),
            pltpu.VMEM((s.tokens, 2 * s.width), F32),
            pltpu.VMEM((s.width, s.tokens), BF),
        ],
        aliases,
    )


def norm_one_grad(s, scalars, qkv, dq, dkv, w_qkv, gain):
    rows = s.half

    def body(sc, qkv_ref, dq_ref, dkv_ref, wq, wk, wv, g, keep, send, grad, stat, lines):
        me = sc[ME]
        total = dot(dq_ref[...], wq[...], NT)
        total += dot(dkv_ref[:, : s.width], wk[...], NT)
        grad[...] = total + dot(dkv_ref[:, s.width :], wv[...], NT)
        gain8 = jnp.broadcast_to(g[...], (8, s.d)).astype(BF)
        parts = ((dq_ref[...], wq), (dkv_ref[:, : s.width], wk), (dkv_ref[:, s.width :], wv))
        one = jnp.zeros((rows, s.width), F32)
        two = jnp.zeros((rows, s.width), F32)
        for k, (value, w) in enumerate(parts):
            value = value.astype(F32)
            one += value * dot(gain8, w[...], NN)[0:1, :]
            two += value * qkv_ref[:, k * s.width : (k + 1) * s.width].astype(F32)
        one = jnp.sum(one, axis=-1, keepdims=True)
        two = jnp.sum(two, axis=-1, keepdims=True)
        lane = lax.broadcasted_iota(jnp.int32, (rows, LANES), 1)
        stat[...] = jnp.where(lane == 0, one, two)
        turned = jnp.transpose(stat[...])
        count = s.tokens // s.dn
        for kind in range(2):
            for n in range(rows // s.dn):
                at = kind * count + n
                step = rows // s.dn
                line = turned[kind : kind + 1, n * s.dn : (n + 1) * s.dn].astype(BF).astype(F32)
                for i in range(s.tokens // rows):

                    @pl.when(pl.program_id(0) == i)
                    def _():
                        lines[at + i * step : at + i * step + 1, :] = line
        at = pl.ds(pl.multiple_of(pl.program_id(0) * rows, rows), rows)
        for odd, ref in ((0, keep), (1, send)):
            for n in range(s.members // 2):
                m = me ^ (2 * n + odd)
                for k in range(s.teams):
                    cols = pl.ds(pl.multiple_of((k * s.members + m) * s.db, s.db), s.db)
                    ref[n, at, k * s.db : (k + 1) * s.db] = grad[:, cols].astype(BF)
                ref[n, s.tokens :, :] = lines[...].astype(BF)

    def third(k):
        return (w_qkv, (s.d, s.width), lambda i, sc: (0, k * s.members + sc[ME]))

    row = lambda i, sc: (i, 0)
    pair = (s.members // 2, s.tokens + 16, s.dn)
    return kernel(
        body,
        "norm_one_grad",
        scalars,
        (s.tokens // rows,),
        [
            (qkv, (rows, 3 * s.width), row),
            (dq, (rows, s.width), row),
            (dkv, (rows, 2 * s.width), row),
            third(0),
            third(1),
            third(2),
            whole(gain),
        ],
        [
            whole_out(pair, BF),
            whole_out(pair, BF),
        ],
        [
            pltpu.VMEM((rows, s.d), F32),
            pltpu.VMEM((rows, LANES), F32),
            pltpu.VMEM((16, s.dn), F32),
        ],
    )


def shift_all(s, parts, out_ref):
    west_ref, mid_ref, east_ref = parts
    rows = s.sec_tokens
    col = lax.rem(lax.broadcasted_iota(jnp.int32, (rows, s.chan), 0), s.cols)

    def one(sector, carry):
        before = west_ref[lax.rem(sector + s.sectors - 1, s.sectors)]
        after = east_ref[lax.rem(sector + 1, s.sectors)]
        west = jnp.where(
            col == 0, pltpu.roll(before, rows - (s.cols - 1), 0), pltpu.roll(west_ref[sector], 1, 0)
        )
        east = jnp.where(
            col == s.cols - 1,
            pltpu.roll(after, s.cols - 1, 0),
            pltpu.roll(east_ref[sector], rows - 1, 0),
        )
        out_ref[sector] = (west + mid_ref[sector] + east).astype(BF)
        return carry

    lax.fori_loop(0, s.sectors, one, 0)


def group_blocks(s, sc, color):
    half = s.group // 2
    for side in range(2):
        for slot in range(half):
            j = 2 * slot + side if color == 0 else side * half + slot
            yield side, slot, sc[GRP] ^ j


def trunk_head(s, scalars, hown, terms, w_head, cot_cat):
    rows = s.half

    def body(sc, near, far, a, b, c, wh0, wh1, cat, home_ref, grad_ref, gain_ref, h2, y0, y1, y2):
        own = sc[ME] // (s.members // 2)
        gains = []
        for half, h1 in enumerate((near, far)):
            side = own ^ half
            total = three_terms(a[0, half, :rows, :], b[0, half, :rows, :], c[0, 1 - half, :rows, :])
            h2[pl.ds(pl.multiple_of(side * rows, rows), rows), :] = (h1[...] + total).astype(BF)
            at = slice(rows, rows + 8)
            gains.append(three_terms(a[0, half, at, :], b[0, half, at, :], c[0, 1 - half, at, :]))
        gain_ref[...] = gains[0] + gains[1]
        for j, ref in enumerate((y0, y1, y2)):
            weight = jnp.concatenate([wh0[j], wh1[j]], axis=1)
            ref[...] = dot(h2[...], weight, NT).reshape(s.sectors, s.sec_tokens, s.chan)
        shift_all(s, (y0, y1, y2), home_ref)
        grad_ref[...] = dot(h2[...], cat[...], TN)

    def part(k):
        return (w_head, (3, s.chan, s.db), lambda i, sc: (0, 0, k * s.members + sc[ME]))

    return kernel(
        body,
        "trunk_head",
        scalars,
        (1,),
        [whole(x) for x in hown]
        + [first(x) for x in terms]
        + [part(0), part(1), whole(cot_cat)],
        [
            whole_out((s.sectors, s.sec_tokens, s.chan), BF),
            whole_out((s.dn, 3 * s.chan), F32),
            whole_out((8, s.dn), F32),
        ],
        [pltpu.VMEM((s.tokens, s.dn), BF)]
        + [pltpu.VMEM((s.sectors, s.sec_tokens, s.chan), F32) for _ in range(3)],
    )


def embed_back(s, scalars, g1, own, stats, hidden0, gain, w_embed, in_cat, head_home, head_part, gain2, bias):
    wide = 3 * s.chan
    span = s.dn

    def body(sc, *refs):
        a, b, c, own_ref, st_ref, h0, h1, g, we0, we1, cat, home, head, gain2_ref, bias_ref = refs[:15]
        keep, send = refs[15:17]
        edges = refs[17 : 17 + s.group]
        grad, stat, y0, y1, y2, ours, part, smalls = refs[17 + s.group :]
        lines = slice(s.tokens, s.tokens + 16)
        total = three_terms(a[0, lines, :], b[0, lines, :], c[0, lines, :]) * np.float32(1.0 / s.d)
        for n in range(s.tokens // span):
            pair = [total[n : n + 1, :], total[s.tokens // span + n : s.tokens // span + n + 1, :]]
            pair = jnp.concatenate(pair + [jnp.zeros((LANES - 2, span), F32)], axis=0)
            stat[n * span : (n + 1) * span, :] = jnp.transpose(pair)
        gain_own = jnp.concatenate(
            [
                g[:, pl.ds(pl.multiple_of((k * s.members + sc[ME]) * s.db, s.db), s.db)]
                for k in range(s.teams)
            ],
            axis=1,
        )
        chunk = s.sec_tokens

        def rows_chunk(i, acc):
            at = pl.ds(pl.multiple_of(i * chunk, chunk), chunk)
            mean, rstd = st_ref[at, 0:1], st_ref[at, 1:2]
            one, two = stat[at, 0:1], stat[at, 1:2]
            g1 = three_terms(a[0, at, :], b[0, at, :], c[0, at, :])
            x = (jnp.concatenate([h0[at, :], h1[at, :]], axis=1) - mean) * rstd
            back = g1 * gain_own - one - x * two
            grad[at, :] = (own_ref[at, :].astype(F32) + rstd * back).astype(BF)
            return acc + jnp.sum(g1 * x, axis=0, keepdims=True)

        gain1 = lax.fori_loop(0, s.tokens // chunk, rows_chunk, jnp.zeros((1, s.dn), F32))
        for j, ref in enumerate((y0, y1, y2)):
            weight = jnp.concatenate([we0[j], we1[j]], axis=1)
            ref[...] = dot(grad[...], weight, NT).reshape(s.sectors, s.sec_tokens, s.chan)
        shift_all(s, (y2, y1, y0), ours)
        for odd, ref in ((0, keep), (1, send)):
            for n in range(s.members // 2):
                for team in range(s.teams):
                    sector = team * s.members + (sc[ME] ^ (2 * n + odd))
                    ref[n, team, 0] = home[sector]
                    ref[n, team, 1] = ours[sector]
        part[:, :wide] = head[...]
        part[:, wide : 2 * wide] = dot(grad[...], cat[...], TN)
        size = s.db // s.group
        for k in range(s.teams):
            lines = [
                bias_ref[:, k * s.fb + n * LANES : k * s.fb + (n + 1) * LANES] for n in range(s.fb // LANES)
            ]
            lines += [gain1[:, k * s.db : (k + 1) * s.db], gain2_ref[0:1, k * s.db : (k + 1) * s.db]]
            lines += [jnp.zeros((size - len(lines), LANES), F32)]
            smalls[...] = jnp.concatenate(lines, axis=0).astype(BF)
            for j, ref in enumerate(edges):
                at = pl.ds(pl.multiple_of(k * s.db + (sc[GRP] ^ j) * size, size), size)
                ref[k, :, : 2 * wide] = part[at, :].astype(BF)
                ref[k, :, 2 * wide :] = smalls[...]

    def part_of(k):
        return (w_embed, (3, s.chan, s.db), lambda i, sc: (0, 0, k * s.members + sc[ME]))

    def own_of(k):
        return (hidden0, (s.tokens, s.db), lambda i, sc: (0, k * s.members + sc[ME]))

    goes = (s.members // 2, s.teams, 2, s.sec_tokens, s.chan)
    size = s.db // s.group
    block = (s.teams, size, 2 * wide + LANES)
    return kernel(
        body,
        "embed_back",
        scalars,
        (1,),
        [first(x) for x in g1]
        + [whole(own), whole(stats), own_of(0), own_of(1), whole(gain), part_of(0), part_of(1)]
        + [whole(in_cat), whole(head_home), whole(head_part), whole(gain2), whole(bias)],
        [whole_out(goes, BF), whole_out(goes, BF)] + [whole_out(block, BF)] * s.group,
        [pltpu.VMEM((s.tokens, s.dn), BF), pltpu.VMEM((s.tokens, LANES), F32)]
        + [pltpu.VMEM((s.sectors, s.sec_tokens, s.chan), F32) for _ in range(3)]
        + [pltpu.VMEM((s.sectors, s.sec_tokens, s.chan), BF)]
        + [pltpu.VMEM((s.dn, 2 * wide), F32), pltpu.VMEM((size, LANES), BF)],
    )


def mlp_weight_grads(s, scalars, near, far, grad_mlp):
    sub = s.fb // s.group

    def body(sc, an, pn, nn_ref, af, pf, nf, gn, gf, ka, sa, kb, sb, scr):
        color = pl.program_id(0)
        kind = pl.program_id(1)

        @pl.when(kind == 0)
        def _():
            scr[...] = (dot(an[...], gn[...], TN) + dot(af[...], gf[...], TN)).astype(BF)

        @pl.when(kind == 1)
        def _():
            scr[...] = (dot(pn[...], nn_ref[...], TN) + dot(pf[...], nf[...], TN)).astype(BF)

        for k, refs in enumerate(((ka, sa), (kb, sb))):

            @pl.when(color == k)
            def _():
                def lane_block(c, carry):
                    lanes = pl.ds(pl.multiple_of(c * LANES, LANES), LANES)
                    to = pl.ds(pl.multiple_of(c * sub, sub), sub)
                    for side, slot, q in group_blocks(s, sc, k):
                        rows = pl.ds(pl.multiple_of(q * sub, sub), sub)
                        refs[side][slot, 0, to, :] = scr[rows, lanes]
                    return carry

                lax.fori_loop(0, s.d // LANES, lane_block, 0)

    def out(color):
        shape = (s.group // 2, 2, s.d, LANES)
        block = (s.group // 2, 1, s.d, LANES)
        if color == 0:
            index = lambda k, kind, sc: (0, jnp.where(k == 0, kind, 1), 0, 0)
        else:
            index = lambda k, kind, sc: (0, jnp.where(k == 0, 0, kind), 0, 0)
        return (shape, BF, block, index)

    cols = lambda k, kind, sc: (0, k)
    ins = []
    for activ, grad_pre, normed in (near, far):
        ins += [
            (activ, (s.half, s.fb), cols),
            (grad_pre, (s.half, s.fb), cols),
            whole(normed),
        ]
    ins += [
        (grad_mlp, (s.half, s.d), lambda k, kind, sc: (side_of(s, sc, False), 0)),
        (grad_mlp, (s.half, s.d), lambda k, kind, sc: (side_of(s, sc, True), 0)),
    ]
    return kernel(
        body,
        "mlp_weight_grads",
        scalars,
        (s.teams, 2),
        ins,
        [out(0), out(0), out(1), out(1)],
        [pltpu.VMEM((s.fb, s.d), BF)],
    )


def attention_weight_grads(s, scalars, normed1, dq, dkv, att_near, att_far, own):
    def body(sc, n1, dq_ref, dkv_ref, an, af, own_near, own_far, ka, sa, kb, sb, scr):
        scr[: s.width] = dot(dq_ref[...], n1[...], TN).astype(BF)
        scr[s.width : 3 * s.width] = dot(dkv_ref[...], n1[...], TN).astype(BF)
        scr[3 * s.width :] = (dot(own_near[...], an[...], TN) + dot(own_far[...], af[...], TN)).astype(BF)

        def lane_block(c, carry):
            lanes = pl.ds(pl.multiple_of(c * LANES, LANES), LANES)
            for k, refs in enumerate(((ka, sa), (kb, sb))):
                for side, slot, q in group_blocks(s, sc, k):
                    rows = pl.ds(pl.multiple_of((k * s.group + q) * LANES, LANES), LANES)
                    refs[side][slot, lanes, :] = scr[rows, lanes]
            return carry

        lax.fori_loop(0, s.d // LANES, lane_block, 0)

    shape = (s.group // 2, s.d, LANES)
    return kernel(
        body,
        "attention_weight_grads",
        scalars,
        (1,),
        [
            whole(normed1),
            whole(dq),
            whole(dkv),
            whole(att_near),
            whole(att_far),
            (own, (s.half, s.dn), lambda i, sc: (side_of(s, sc, False), 0)),
            (own, (s.half, s.dn), lambda i, sc: (side_of(s, sc, True), 0)),
        ],
        [whole_out(shape, BF)] * 4,
        [pltpu.VMEM((3 * s.width + s.dn, s.d), BF)],
    )


def add_low(a, b):
    return (a.astype(F32) + b.astype(F32)).astype(BF)


def first(x):
    rank = len(x.shape)
    return (x, (1,) + tuple(x.shape[1:]), lambda *_: (0,) * rank)


def three_terms(keep, got, more):
    return keep.astype(F32) + got.astype(F32) + more.astype(F32)


def group_first(keep_a, send_a, keep_b, send_b):
    got_a = swap(send_a, "grp", 1)
    got_b = swap(send_b, "grp", 2)
    return (keep_a, got_a), (keep_b, got_b), (add_low(keep_a[1], got_a[1]), add_low(keep_b[1], got_b[1]))


def group_second(terms_a, terms_b, sends):
    more_a = swap(sends[0], "grp", 2)
    more_b = swap(sends[1], "grp", 1)
    return terms_a + (more_a[None],), terms_b + (more_b[None],)


def pick_team(s, scalars, terms_a, terms_b, kinds):
    half = s.d // 2

    def body(sc, *refs):
        a, b = refs[:3], refs[3:6]
        keep, send = refs[6:]
        team = sc[TEAM]

        def total(terms, k, rows):
            at = (0, k, rows) if kinds == 2 else (0, rows)
            return three_terms(*[ref[at] for ref in terms]).astype(BF)

        if kinds == 2:
            for side in range(2):

                @pl.when(team == side)
                def _():
                    same, other = (a, b) if side == 0 else (b, a)
                    keep[0] = total(same, 0, slice(None))
                    send[0] = total(other, 0, slice(None))

        mine = pl.ds(pl.multiple_of(team * half, half), half)
        theirs = pl.ds(pl.multiple_of((1 - team) * half, half), half)
        for color, terms in enumerate((a, b)):
            at = slice(color * half, (color + 1) * half)
            keep[kinds - 1, at] = total(terms, 1, mine)
            send[kinds - 1, at] = total(terms, 1, theirs)

    return kernel(
        body,
        "pick_team",
        scalars,
        (1,),
        [first(x) for x in terms_a + terms_b],
        [whole_out((kinds, s.d, LANES), BF)] * 2,
    )


def pick_member(s, scalars, keep, got):
    kinds = keep.shape[0]
    half = s.d // 2

    def body(sc, k_ref, g_ref, *refs):
        for j in range(s.members):
            m = sc[ME] ^ j
            for color in range(2):
                at = pl.ds(pl.multiple_of(color * half + m * s.db, s.db), s.db)
                value = k_ref[kinds - 1, at].astype(F32) + g_ref[kinds - 1, at].astype(F32)
                refs[j][color] = value.astype(BF)
        if kinds == 2:
            refs[s.members][...] = (k_ref[0].astype(F32) + g_ref[0].astype(F32)).astype(BF)

    outs = [whole_out((2, s.db, LANES), BF)] * s.members
    if kinds == 2:
        outs = outs + [whole_out((s.d, LANES), BF)]
    return kernel(body, "pick_member", scalars, (1,), [whole(keep), whole(got)], outs)


def all_of_group(x, x_first):
    near, far = (1, 2) if x_first else (2, 1)
    one = swap(x, "grp", near)
    two = swap(x, "grp", far)
    both = swap(one, "grp", far)
    return [x, one, two, both] if x_first else [x, two, one, both]


def cross(s, pieces):
    got = [pieces[0]] + [swap(pieces[j], "sec", j) for j in range(1, s.members)]
    return jnp.stack(got)


def mlp_grads_out(s, scalars, downs, ups):
    sub = s.fb // s.group

    def body(sc, *refs):
        d_refs, u_refs = refs[: s.group], refs[s.group : 2 * s.group]
        down, up = refs[2 * s.group :]
        for j in range(s.group):
            q = sc[GRP] ^ j
            rows = pl.ds(pl.multiple_of(q * sub, sub), sub)
            for c in range(s.d // LANES):
                down[rows, c * LANES : (c + 1) * LANES] = d_refs[j][c * sub : (c + 1) * sub, :].astype(F32)

            def member(jm, carry):
                m = sc[ME] ^ jm
                for color in range(s.teams):
                    at = ((color * s.members + m) * s.group + q) * LANES
                    up[:, pl.ds(pl.multiple_of(at, LANES), LANES)] = jnp.transpose(u_refs[j][jm, color].astype(F32))
                return carry

            lax.fori_loop(0, s.members, member, 0)

    return kernel(
        body,
        "mlp_grads_out",
        scalars,
        (1,),
        [whole(x) for x in downs + ups],
        [whole_out((s.fb, s.d), F32), whole_out((s.db, s.ff), F32)],
    )


def attention_grads_out(s, scalars, parts):
    def body(sc, *refs):
        u_refs = refs[: s.group]
        qkv, out = refs[s.group :]
        for j in range(s.group):
            q = sc[GRP] ^ j

            def member(jm, carry):
                m = sc[ME] ^ jm
                at = (q // 2) * s.d + m * s.width + lax.rem(q, 2) * LANES
                value = jnp.transpose(u_refs[j][jm, 0].astype(F32))
                qkv[:, pl.ds(pl.multiple_of(at, LANES), LANES)] = value
                other = jnp.transpose(u_refs[j][jm, 1].astype(F32))

                @pl.when(q < 2)
                def _():
                    at = 2 * s.d + m * s.width + q * LANES
                    qkv[:, pl.ds(pl.multiple_of(at, LANES), LANES)] = other

                @pl.when(q >= 2)
                def _():
                    at = ((q - 2) * s.members + m) * s.db
                    out[:, pl.ds(pl.multiple_of(at, LANES), LANES)] = other

                return carry

            lax.fori_loop(0, s.members, member, 0)

    return kernel(
        body,
        "attention_grads_out",
        scalars,
        (1,),
        [whole(x) for x in parts],
        [whole_out((s.db, 3 * s.d), F32), whole_out((s.db, s.d), F32)],
    )


def edge_grads_out(s, scalars, parts):
    wide = 3 * s.chan
    size = s.db // s.group

    def body(sc, *refs):
        ins = refs[: s.group]
        embed, head, small, scr = refs[s.group :]
        for j in range(s.group):
            at = pl.ds(pl.multiple_of((sc[GRP] ^ j) * size, size), size)
            scr[at, :] = ins[j][...].astype(F32)
        head[...] = jnp.transpose(scr[:, :wide])
        embed[...] = jnp.transpose(scr[:, wide : 2 * wide])
        small[...] = ins[0][:16, 2 * wide :].astype(F32)

    return kernel(
        body,
        "edge_grads_out",
        scalars,
        (1,),
        [whole(x) for x in parts],
        [
            whole_out((wide, s.db), F32),
            whole_out((wide, s.db), F32),
            whole_out((16, LANES), F32),
        ],
        [pltpu.VMEM((s.db, 2 * wide + LANES), F32)],
    )


def on_team(
    fields,
    valid_rows,
    w_embed,
    ln1_gain,
    w_qkv,
    w_out,
    ln2_gain,
    w_up,
    b_up,
    w_down,
    w_head,
    cotangent,
):
    s = Sizes(fields, w_qkv, w_up)
    place = lax.axis_index("sec")
    team, me = place // s.members, place % s.members
    core, chip = 1, 2
    first_team = team == 0
    valid = jnp.where(first_team, valid_rows[0], valid_rows[1])
    scalars = (jnp.stack([team, me, lax.axis_index("grp"), valid]).astype(jnp.int32), [])
    gain1 = ln1_gain.astype(F32)[None]
    gain2 = ln2_gain.astype(F32)[None]

    def gather_sample(x):
        flat = x.reshape(s.teams, s.sec_tokens, s.chan)
        mine = jnp.where(first_team, flat[0], flat[1])
        other = swap(jnp.where(first_team, flat[1], flat[0]), "sec", s.members)
        pair = jnp.stack([mine, other])
        across = swap(pair, "sec", chip)
        return [pair, swap(pair, "sec", core), across, swap(across, "sec", core)]

    def go_home(keep, got, far):
        mine = three_terms(keep[0], got[0], far)
        own = jnp.where(first_team, mine[0], mine[1])
        other = jnp.where(first_team, mine[1], mine[0]).astype(BF)
        other = swap(other, "sec", s.members).astype(F32)
        both = [jnp.where(first_team, own, other), jnp.where(first_team, other, own)]
        return [jnp.stack([x[kind] for x in both]).reshape(fields.shape) for kind in range(2)]

    def scatter_features(keep, send):
        got = swap(send, "sec", core)
        return keep, got, swap(add_low(keep[1:2], got[1:2]), "sec", chip)

    w_head_t = jnp.transpose(w_head, (0, 2, 1))
    in_cat, hidden0, normed1, qkv, stats = embed_qkv(
        s, scalars, gather_sample(fields), w_embed.reshape(3 * s.chan, s.d), gain1, w_qkv
    )
    att_near, *rest = attention_fwd(s, scalars, qkv, False)
    saved_near = (att_near, *rest)
    from_chip_far = swap(att_near, "sec", chip)
    att_far, *rest = attention_fwd(s, scalars, qkv, True)
    saved_far = (att_far, *rest)
    from_chip_near = swap(att_far, "sec", chip)
    hold(scalars, from_chip_far)
    cot_cat, grad_mlp = cotangent_grad(
        s, scalars, gather_sample(cotangent), w_head_t.reshape(3 * s.chan, s.d)
    )
    att_pieces_far = [att_far, swap(att_far, "sec", core), from_chip_far, swap(from_chip_far, "sec", core)]
    att_pieces_near = [att_near, swap(att_near, "sec", core), from_chip_near, swap(from_chip_near, "sec", core)]

    def run_mlp(pieces, far):
        return mlp(s, scalars, pieces, hidden0, grad_mlp, w_out, gain2, w_up, b_up, w_down, far)

    attended_far, normed2_far, activ_far, pre_far, gkeep, gsend, gsum, hown_far, bias_far, _ = run_mlp(
        att_pieces_far, True
    )
    hold(scalars, from_chip_near)
    g2_chip = [swap(gkeep, "sec", chip), swap(gsend, "sec", chip + core)]
    attended_near, normed2_near, activ_near, pre_near, gkeep, gsend, gsum_near, hown_near, bias_near, hidden1 = run_mlp(
        att_pieces_near, False
    )
    bias_grad = bias_far + bias_near
    got = swap(gsend, "sec", core)
    pkeep, psend = trunk_part(s, scalars, ((activ_near, gsum_near), (activ_far, gsum)), w_down)
    b0 = norm_two_back(s, scalars, [gkeep, got, *g2_chip], hidden1, grad_mlp, gain2)
    b1 = swap(b0, "sec", core)
    b2 = swap(b0, "sec", chip)
    b3 = swap(b2, "sec", core)
    mlp_blocks = mlp_weight_grads(
        s, scalars, (activ_near, pre_near, normed2_near), (activ_far, pre_far, normed2_far), grad_mlp
    )
    hold(scalars, b2)
    mlp_a, mlp_b, mlp_sends = group_first(*mlp_blocks)
    before = attention_bwd(s, scalars, qkv, saved_near, (b0, b1), w_out, False)
    hold(scalars, b3, *mlp_sends)
    mlp_terms = group_second(mlp_a, mlp_b, mlp_sends)
    trunk_terms = scatter_features(pkeep, psend)
    dq, own, dkv = attention_bwd(s, scalars, qkv, saved_far, (b2, b3), w_out, True, before)
    hold(scalars, *[terms[2] for terms in mlp_terms])
    att_blocks = attention_weight_grads(s, scalars, normed1, dq, dkv, attended_near, attended_far, own)
    att_a, att_b, att_sends = group_first(*att_blocks)
    mlp_kept, send = pick_team(s, scalars, *mlp_terms, 2)
    mlp_swapped = swap(send, "sec", s.members)
    g1_keep, g1_send = norm_one_grad(s, scalars, qkv, dq, dkv, w_qkv, gain1)
    hold(scalars, *att_sends)
    att_terms = group_second(att_a, att_b, att_sends)
    hold(scalars, trunk_terms[2])
    head_home, head_part, gain2_grad = trunk_head(
        s, scalars, (hown_near, hown_far), trunk_terms, w_head_t, cot_cat
    )
    g1 = scatter_features(g1_keep, g1_send)
    hold(scalars, *[terms[2] for terms in att_terms])
    att_kept, send = pick_team(s, scalars, *att_terms, 1)
    att_swapped = swap(send, "sec", s.members)
    *crossed, downs = pick_member(s, scalars, mlp_kept, mlp_swapped)
    mlp_parts = (all_of_group(downs, False), all_of_group(cross(s, crossed), True))
    keep, send, *edges = embed_back(
        s, scalars, g1, own, stats, hidden0, gain1, w_embed, in_cat, head_home, head_part, gain2_grad, bias_grad
    )
    edges = edges[:1] + [swap(edges[j], "grp", j) for j in range(1, s.group)]
    home_got = swap(send, "sec", core)
    hold(scalars, *mlp_parts[0], *mlp_parts[1])
    crossed = pick_member(s, scalars, att_kept, att_swapped)
    att_parts = all_of_group(cross(s, crossed), True)
    home_far = swap(add_low(keep[1], home_got[1]), "sec", chip)
    down_grad, up_grad = mlp_grads_out(s, scalars, *mlp_parts)
    hold(scalars, home_far)
    head_output, input_grad = go_home(keep, home_got, home_far)

    total = edges[0].astype(F32) + edges[1].astype(F32) + edges[2].astype(F32) + edges[3].astype(F32)
    kept = jnp.where(first_team, total[0], total[1])
    given = jnp.where(first_team, total[1], total[0]).astype(BF)
    edges = (kept + swap(given, "sec", s.members).astype(F32)).astype(BF)
    edge_parts = all_of_group(edges, True)
    qkv_grad, out_grad = attention_grads_out(s, scalars, att_parts)
    embed_t, head_t, small = edge_grads_out(s, scalars, edge_parts)
    embed_grad = embed_t.reshape(3, s.chan, s.db)
    head_grad = jnp.transpose(head_t.reshape(3, s.chan, s.db), (0, 2, 1))
    nb = s.fb // LANES
    return (
        head_output,
        input_grad,
        embed_grad,
        small[nb],
        qkv_grad,
        out_grad,
        small[nb + 1],
        up_grad,
        small[:nb].reshape(s.fb),
        down_grad,
        head_grad,
    )

LAT = 32
KCOLS = 8


def extended(cells, sides, width):
    for axis, dim in sides:
        count = lax.axis_size(axis)
        head = lax.slice_in_dim(cells, 0, width, axis=dim)
        tail = lax.slice_in_dim(cells, cells.shape[dim] - width, cells.shape[dim], axis=dim)
        cells = jnp.concatenate(
            [
                lax.ppermute(tail, axis, [(i, (i + 1) % count) for i in range(count)]),
                cells,
                lax.ppermute(head, axis, [((i + 1) % count, i) for i in range(count)]),
            ],
            axis=dim,
        )
    return cells


def normed(hidden, gains):
    center = hidden - jnp.mean(hidden, axis=-1, keepdims=True)
    spread = jnp.mean(center * center, axis=-1, keepdims=True)
    return center * lax.rsqrt(spread + 1e-05) * gains


def gelu_exact(values):
    return jax.nn.gelu(values, approximate=False)


def three_cols(padded, col_count, west_first):
    west_cols = padded[:, :, 0:col_count]
    middle_cols = padded[:, :, 1 : col_count + 1]
    east_cols = padded[:, :, 2 : col_count + 2]
    if west_first:
        return jnp.stack([west_cols, middle_cols, east_cols], axis=3)
    return jnp.stack([east_cols, middle_cols, west_cols], axis=3)


def split_heads(values):
    return values.reshape(values.shape[0], -1, HEADS, HEAD_DIM)


def key_mask(valid_rows, count_cols):
    rows_ok = jnp.arange(LAT)[None, :] < valid_rows[:, None]
    spread_ok = jnp.broadcast_to(rows_ok[:, :, None], (rows_ok.shape[0], LAT, count_cols))
    return spread_ok.reshape(rows_ok.shape[0], LAT * count_cols)


def key_scores(queries, kv_piece, valid_rows):
    d_model = HEADS * HEAD_DIM
    key_part = split_heads(kv_piece[..., :d_model])
    value_part = split_heads(kv_piece[..., d_model:])
    scores = (
        jnp.einsum("sqhd,skhd->shqk", queries, key_part, preferred_element_type=jnp.float32) * 0.125
    )
    allowed = key_mask(valid_rows, kv_piece.shape[2])
    scores = jnp.where(allowed[:, None, None, :], scores, -1e30)
    return (scores, key_part, value_part)


def softmax_fold(queries, valid_rows):

    def fold_piece(run_state, kv_piece, first_col):
        run_max, run_sum, run_acc = run_state
        scores, key_part, value_part = key_scores(queries, kv_piece, valid_rows)
        new_max = jnp.maximum(run_max, jnp.max(scores, axis=-1))
        factor = jnp.exp(run_max - new_max)
        weights = jnp.exp(scores - new_max[..., None])
        new_sum = run_sum * factor + jnp.sum(weights, axis=-1)
        added = jnp.einsum(
            "shqk,skhd->sqhd",
            weights.astype(jnp.bfloat16),
            value_part,
            preferred_element_type=jnp.float32,
        )
        new_acc = run_acc * jnp.transpose(factor, (0, 2, 1))[..., None] + added
        return (new_max, new_sum, new_acc)

    return fold_piece


def on_sectors(
    fields,
    valid_rows,
    w_embed,
    ln1_gain,
    w_qkv,
    w_out,
    ln2_gain,
    w_up,
    b_up,
    w_down,
    w_head,
    cotangent,
):
    samples, lat_rows, col_count, channels = fields.shape
    d_model = w_qkv.shape[0]
    token_count = lat_rows * col_count
    padded_in = extended(fields, (("sec", 2),), 1)
    input_cat = three_cols(padded_in, col_count, True)
    hidden0 = jnp.einsum("slcoi,oid->slcd", input_cat, w_embed, preferred_element_type=jnp.float32)
    normed_one, norm_one_back = jax.vjp(normed, hidden0, ln1_gain.astype(jnp.float32))
    normed_one_low = normed_one.astype(jnp.bfloat16)
    qkv_full = jnp.einsum(
        "slcd,de->slce", normed_one_low, w_qkv, preferred_element_type=jnp.float32
    ).astype(jnp.bfloat16)
    queries = split_heads(qkv_full[..., :d_model])
    key_vals = qkv_full[..., d_model:]
    init_state = (
        jnp.full((samples, HEADS, token_count), -1e30, jnp.float32),
        jnp.zeros((samples, HEADS, token_count), jnp.float32),
        jnp.zeros((samples, token_count, HEADS, HEAD_DIM), jnp.float32),
    )
    fold_piece = softmax_fold(queries, valid_rows)
    all_kv = lax.all_gather(key_vals, "sec", axis=2, tiled=True)

    def forward_block(block_index, run_state):
        kv_block = lax.dynamic_slice_in_dim(all_kv, block_index * KCOLS, KCOLS, 2)
        return fold_piece(run_state, kv_block, block_index * KCOLS)

    run_max, run_sum, run_acc = lax.fori_loop(
        0, all_kv.shape[2] // KCOLS, forward_block, init_state
    )
    attended = run_acc / jnp.transpose(run_sum, (0, 2, 1))[..., None]
    log_total = run_max + jnp.log(run_sum)
    attended_low = attended.reshape(samples, lat_rows, col_count, d_model).astype(jnp.bfloat16)
    hidden1 = hidden0 + jnp.einsum(
        "slcd,de->slce", attended_low, w_out, preferred_element_type=jnp.float32
    )
    normed_two, norm_two_back = jax.vjp(normed, hidden1, ln2_gain.astype(jnp.float32))
    normed_two_low = normed_two.astype(jnp.bfloat16)
    preact = jnp.einsum(
        "slcd,df->slcf", normed_two_low, w_up, preferred_element_type=jnp.float32
    ) + b_up.astype(jnp.float32)
    activ, gelu_back = jax.vjp(gelu_exact, preact)
    activ_low = activ.astype(jnp.bfloat16)
    hidden2 = hidden1 + jnp.einsum(
        "slcf,fd->slcd", activ_low, w_down, preferred_element_type=jnp.float32
    )
    hidden2_low = hidden2.astype(jnp.bfloat16)
    padded_hidden = extended(hidden2_low, (("sec", 2),), 1)
    hidden_cat = three_cols(padded_hidden, col_count, True)
    head_output = jnp.einsum(
        "slcod,odi->slci", hidden_cat, w_head, preferred_element_type=jnp.float32
    )
    padded_cot = extended(cotangent, (("sec", 2),), 1)
    cot_cat = three_cols(padded_cot, col_count, False)
    head_grad = jnp.einsum(
        "slcod,slci->odi", hidden_cat, cotangent, preferred_element_type=jnp.float32
    )
    grad_two = jnp.einsum("slcoi,odi->slcd", cot_cat, w_head, preferred_element_type=jnp.float32)
    grad_mlp = grad_two.astype(jnp.bfloat16)
    down_grad = jnp.einsum("slcf,slcd->fd", activ_low, grad_mlp, preferred_element_type=jnp.float32)
    grad_act = jnp.einsum("slcd,fd->slcf", grad_mlp, w_down, preferred_element_type=jnp.float32)
    grad_pre = gelu_back(grad_act)[0].astype(jnp.bfloat16)
    bias_grad = jnp.sum(grad_pre.astype(jnp.float32), axis=(0, 1, 2))
    up_grad = jnp.einsum(
        "slcd,slcf->df", normed_two_low, grad_pre, preferred_element_type=jnp.float32
    )
    grad_normed_two = jnp.einsum(
        "slcf,df->slcd", grad_pre, w_up, preferred_element_type=jnp.float32
    )
    grad_from_norm, gain_two_grad = norm_two_back(grad_normed_two)
    grad_one = grad_two + grad_from_norm
    grad_att = grad_one.astype(jnp.bfloat16)
    out_grad = jnp.einsum(
        "slcd,slce->de", attended_low, grad_att, preferred_element_type=jnp.float32
    )
    grad_heads = split_heads(
        jnp.einsum("slce,de->slcd", grad_att, w_out, preferred_element_type=jnp.float32).astype(
            jnp.bfloat16
        )
    )
    row_delta = jnp.transpose(
        jnp.sum(grad_heads.astype(jnp.float32) * attended, axis=-1), (0, 2, 1)
    )

    def sample_backward(unused_carry, sample_in):
        one_query, one_grad, one_lse, one_delta, one_valid, one_kv = sample_in
        term_zero = jnp.zeros((1, lat_rows, one_kv.shape[2], 2 * d_model), jnp.bfloat16)
        grad_zero = jnp.zeros(one_query.shape, jnp.float32)

        def backward_block(block_index, run_state):
            grad_query, term = run_state
            kv_block = lax.dynamic_slice_in_dim(one_kv, block_index * KCOLS, KCOLS, 2)
            scores, key_part, value_part = key_scores(one_query, kv_block, one_valid)
            probs = jnp.exp(scores - one_lse[..., None])
            grad_probs = jnp.einsum(
                "sqhd,skhd->shqk", one_grad, value_part, preferred_element_type=jnp.float32
            )
            grad_scores = (probs * (grad_probs - one_delta[..., None])).astype(jnp.bfloat16)
            grad_query = (
                grad_query
                + jnp.einsum(
                    "shqk,skhd->sqhd", grad_scores, key_part, preferred_element_type=jnp.float32
                )
                * 0.125
            )
            grad_keys = (
                jnp.einsum(
                    "shqk,sqhd->skhd", grad_scores, one_query, preferred_element_type=jnp.float32
                )
                * 0.125
            )
            grad_values = jnp.einsum(
                "shqk,sqhd->skhd",
                probs.astype(jnp.bfloat16),
                one_grad,
                preferred_element_type=jnp.float32,
            )
            joined = jnp.concatenate(
                [
                    grad_keys.reshape(1, lat_rows, KCOLS, d_model),
                    grad_values.reshape(1, lat_rows, KCOLS, d_model),
                ],
                axis=-1,
            ).astype(jnp.bfloat16)
            term = lax.dynamic_update_slice_in_dim(term, joined, block_index * KCOLS, 2)
            return (grad_query, term)

        grad_query, term = lax.fori_loop(
            0, one_kv.shape[2] // KCOLS, backward_block, (grad_zero, term_zero)
        )
        summed = lax.psum_scatter(
            term.astype(jnp.float32).astype(jnp.bfloat16), "sec", scatter_dimension=2, tiled=True
        ).astype(jnp.float32)
        return (unused_carry, (grad_query, summed))

    scan_inputs = (
        queries.reshape(samples, 1, token_count, HEADS, HEAD_DIM),
        grad_heads.reshape(samples, 1, token_count, HEADS, HEAD_DIM),
        log_total.reshape(samples, 1, HEADS, token_count),
        row_delta.reshape(samples, 1, HEADS, token_count),
        valid_rows.reshape(samples, 1),
        all_kv.reshape(samples, 1, lat_rows, all_kv.shape[2], 2 * d_model),
    )
    scan_end, (grad_queries, grad_kv) = lax.scan(sample_backward, 0, scan_inputs)
    grad_qkv = jnp.concatenate(
        [
            grad_queries.reshape(samples, lat_rows, col_count, d_model),
            grad_kv.reshape(samples, lat_rows, col_count, 2 * d_model),
        ],
        axis=-1,
    ).astype(jnp.bfloat16)
    qkv_grad = jnp.einsum(
        "slcd,slce->de", normed_one_low, grad_qkv, preferred_element_type=jnp.float32
    )
    grad_normed_one = jnp.einsum(
        "slce,de->slcd", grad_qkv, w_qkv, preferred_element_type=jnp.float32
    )
    grad_from_first, gain_one_grad = norm_one_back(grad_normed_one)
    grad_zero_low = (grad_one + grad_from_first).astype(jnp.bfloat16)
    embed_grad = jnp.einsum(
        "slcoi,slcd->oid", input_cat, grad_zero_low, preferred_element_type=jnp.float32
    )
    padded_grad = extended(grad_zero_low, (("sec", 2),), 1)
    grad_cat = three_cols(padded_grad, col_count, False)
    input_grad = jnp.einsum(
        "slcod,oid->slci", grad_cat, w_embed, preferred_element_type=jnp.float32
    )
    shard_grads = (
        lax.psum_scatter(
            embed_grad.astype(jnp.bfloat16), "sec", scatter_dimension=2, tiled=True
        ).astype(jnp.float32),
        lax.psum_scatter(
            gain_one_grad.astype(jnp.bfloat16), "sec", scatter_dimension=0, tiled=True
        ).astype(jnp.float32),
        lax.psum_scatter(
            qkv_grad.astype(jnp.bfloat16), "sec", scatter_dimension=0, tiled=True
        ).astype(jnp.float32),
        lax.psum_scatter(
            out_grad.astype(jnp.bfloat16), "sec", scatter_dimension=0, tiled=True
        ).astype(jnp.float32),
        lax.psum_scatter(
            gain_two_grad.astype(jnp.bfloat16), "sec", scatter_dimension=0, tiled=True
        ).astype(jnp.float32),
        lax.psum_scatter(
            up_grad.astype(jnp.bfloat16), "sec", scatter_dimension=0, tiled=True
        ).astype(jnp.float32),
        lax.psum_scatter(
            bias_grad.astype(jnp.bfloat16), "sec", scatter_dimension=0, tiled=True
        ).astype(jnp.float32),
        lax.psum_scatter(
            down_grad.astype(jnp.bfloat16), "sec", scatter_dimension=0, tiled=True
        ).astype(jnp.float32),
        lax.psum_scatter(
            head_grad.astype(jnp.bfloat16), "sec", scatter_dimension=1, tiled=True
        ).astype(jnp.float32),
    )
    total_grads = (
        lax.psum(shard_grads[0].astype(jnp.bfloat16), "grp").astype(jnp.float32),
        lax.psum(shard_grads[1].astype(jnp.bfloat16), "grp").astype(jnp.float32),
        lax.psum(shard_grads[2].astype(jnp.bfloat16), "grp").astype(jnp.float32),
        lax.psum(shard_grads[3].astype(jnp.bfloat16), "grp").astype(jnp.float32),
        lax.psum(shard_grads[4].astype(jnp.bfloat16), "grp").astype(jnp.float32),
        lax.psum(shard_grads[5].astype(jnp.bfloat16), "grp").astype(jnp.float32),
        lax.psum(shard_grads[6].astype(jnp.bfloat16), "grp").astype(jnp.float32),
        lax.psum(shard_grads[7].astype(jnp.bfloat16), "grp").astype(jnp.float32),
        lax.psum(shard_grads[8].astype(jnp.bfloat16), "grp").astype(jnp.float32),
    )
    return (
        head_output,
        input_grad,
        total_grads[0],
        total_grads[1],
        total_grads[2],
        total_grads[3],
        total_grads[4],
        total_grads[5],
        total_grads[6],
        total_grads[7],
        total_grads[8],
    )


def on_device(*args):
    fields, w_qkv = args[0], args[4]
    sectors = lax.axis_size("sec")
    fits = (
        fields.shape[0] == 2
        and sectors == 8
        and lax.axis_size("grp") == 4
        and w_qkv.shape[0] == sectors * LANES
    )
    return on_team(*args) if fits else on_sectors(*args)


def solution(mesh):
    tokens_in = P("grp", None, "sec", None)
    return jax.shard_map(
        on_device,
        mesh=mesh,
        in_specs=(tokens_in, P("grp")) + (P(),) * 9 + (tokens_in,),
        out_specs=(
            tokens_in,
            tokens_in,
            P(None, None, "sec"),
            P("sec"),
            P("sec", None),
            P("sec", None),
            P("sec"),
            P("sec", None),
            P("sec"),
            P("sec", None),
            P(None, "sec", None),
        ),
        check_vma=False,
    )
```

profile of v0, /device:TPU:0, one launch (start us, length us, event | category | flops | bytes accessed | tf_op | source)
XLA Modules:
  0.0 296.4 jit_solution(1823471044532661473)
XLA Ops:
  1.8 4.1 %collective-permute-start = (bf16[128,192]{1,0:T(8,128)(2,1)S(1)}, bf16[128,192]{1,0:T(8,128)(2,1)S(1)}, u32[]{:S(2)}, u32[]{:S(2)}) collective-permute-start(bf16[128,192]{1,0:T(8,128)(2,1)S(1)} %select_n.119), channel_id=1, source_target_pairs={{0,4},{1,5},{2,6},{3,7},{4,0},{5,1},{6,2},{7,3},{8,12},{9,13},{10,... | collective-permute-start | bytes 147464 | tf_op jit(solution)/shard_map/ppermute | solution.py:50
  14.9 3.6 %collective-permute-done.2.refs_2_ = bf16[2,128,192]{2,1,0:T(8,128)(2,1)S(1)} collective-permute-done((bf16[2,128,192]{2,1,0:T(8,128)(2,1)S(1)}, bf16[2,128,192]{2,1,0:T(8,128)(2,1)S(1)}, u32[]{:S(2)}, u32[]{:S(2)}) %collective-permute-start.2) | collective-permute-done | bytes 98336 | tf_op jit(solution)/shard_map/ppermute | solution.py:50
  22.1 9.7 %embed_qkv.1 = (bf16[1024,576]{1,0:T(8,128)(2,1)}, f32[1024,1024]{1,0:T(8,128)}, bf16[1024,1024]{1,0:T(8,128)(2,1)}, bf16[1024,768]{1,0:T(8,128)(2,1)}, f32[1024,128]{1,0:T(8,128)}) custom-call(s32[4]{0:T(128)} %pad_add_fusion.sc, bf16[2,128,192]{2,1,0:T(8,128)(2,1)} %copy-done.7, bf16[2,128,192]{2,1,0:T(8,128)(2,1)} %copy-done.13, ...), custom_call_target="tpu_custom_call" | custom-call | flops 11040000000 | bytes 34560000 | tf_op jit(solution)/shard_map/embed_qkv/pallas_call | solution.py:62
  31.8 8.5 %attention_fwd.2 = (bf16[512,256]{1,0:T(8,128)(2,1)}, bf16[4,2,1024,256]{3,2,1,0:T(8,128)(2,1)}, f32[512,128]{1,0:T(8,128)}) custom-call(s32[4]{0:T(128)} %pad_add_fusion.sc, bf16[1024,768]{1,0:T(8,128)(2,1)} %get-tuple-element.113.q_ref.kv_ref.refs_0_.refs_1_.qkv_ref, bf16[1024,768]{1,0:T(8,128)(2,1)} %get-tuple-element.113.q_ref.kv_ref.refs_0_.refs_1_.qkv_ref), custom_call_target="tpu_custom_call" | custom-call | flops 10579999744 | bytes 33120000 | tf_op jit(solution)/shard_map/attention_fwd/pallas_call | solution.py:62
  41.9 8.5 %attention_fwd.3 = (bf16[512,256]{1,0:T(8,128)(2,1)}, bf16[4,2,1024,256]{3,2,1,0:T(8,128)(2,1)}, f32[512,128]{1,0:T(8,128)}) custom-call(s32[4]{0:T(128)} %pad_add_fusion.sc, bf16[1024,768]{1,0:T(8,128)(2,1)} %get-tuple-element.113.q_ref.kv_ref.refs_0_.refs_1_.qkv_ref, bf16[1024,768]{1,0:T(8,128)(2,1)} %get-tuple-element.113.q_ref.kv_ref.refs_0_.refs_1_.qkv_ref), custom_call_target="tpu_custom_call" | custom-call | flops 10579999744 | bytes 33120000 | tf_op jit(solution)/shard_map/attention_fwd/pallas_call | solution.py:62
  51.6 5.7 %cotangent_grad.1 = (bf16[1024,576]{1,0:T(8,128)(2,1)}, bf16[1024,1024]{1,0:T(8,128)(2,1)}) custom-call(s32[4]{0:T(128)} %pad_add_fusion.sc, bf16[2,128,192]{2,1,0:T(8,128)(2,1)} %copy-done.6, bf16[2,128,192]{2,1,0:T(8,128)(2,1)} %collective-permute-done.9.refs_1_, bf16[2,128,192]{2,1,0:T(8,128)(2,1)} %collective-permute-done.10.refs_2_, ...), custom_call_target="tpu_custom_call" | custom-call | flops 7015000064 | bytes 21960000 | tf_op jit(solution)/shard_map/cotangent_grad/pallas_call | solution.py:62
  59.4 17.2 %mlp.3 = (bf16[512,1024]{1,0:T(8,128)(2,1)}, bf16[512,1024]{1,0:T(8,128)(2,1)}, bf16[512,1024]{1,0:T(8,128)(2,1)}, bf16[512,1024]{1,0:T(8,128)(2,1)}, bf16[256,1...) custom-call(s32[4]{0:T(128)} %pad_add_fusion.sc, ...), custom_call_target="tpu_custom_call" | custom-call | flops 19549999104 | bytes 61200000 | tf_op jit(solution)/shard_map/mlp/pallas_call | solution.py:62
  78.5 17.2 %mlp.2 = (bf16[512,1024]{1,0:T(8,128)(2,1)}, bf16[512,1024]{1,0:T(8,128)(2,1)}, bf16[512,1024]{1,0:T(8,128)(2,1)}, bf16[512,1024]{1,0:T(8,128)(2,1)}, bf16[256,1...) custom-call(s32[4]{0:T(128)} %pad_add_fusion.sc, ...), custom_call_target="tpu_custom_call" | custom-call | flops 19549999104 | bytes 61200000 | tf_op jit(solution)/shard_map/mlp/pallas_call | solution.py:62
  96.1 7.4 %trunk_part.1 = (bf16[2,2,528,256]{3,2,1,0:T(8,128)(2,1)}, bf16[2,2,528,256]{3,2,1,0:T(8,128)(2,1)}) custom-call(s32[4]{0:T(128)} %pad_add_fusion.sc, bf16[512,1024]{1,0:T(8,128)(2,1)} %get-tuple-element.125.act0.an, f32[1,1024]{1,0:T(1,128)} %get-tuple-element.126.gs0, bf16[512,1024]{1,0:T(8,128)(2,1)} %get-tuple-element.128.act1.af, ...), custom_call_target="tpu_custom_call" | custom-call | flops 4600000000 | bytes 14400000 | tf_op jit(solution)/shard_map/trunk_part/pallas_call | solution.py:62
  103.7 4.8 %norm_two_back.1.refs_5_ = bf16[256,1024]{1,0:T(8,128)(2,1)} custom-call(s32[4]{0:T(128)} %pad_add_fusion.sc, bf16[256,1024]{1,0:T(8,128)(2,1)} %get-tuple-element.132.refs_0_, bf16[256,1024]{1,0:T(8,128)(2,1)} %collective-permute-done.14.refs_1_, bf16[256,1024]{1,0:T(8,128)(2,1)} %collective-permute-done.15.refs_2_, ...), custom_call_target="tpu_custom_call" | custom-call | flops 5634999808 | bytes 17640000 | tf_op jit(solution)/shard_map/norm_two_back/pallas_call | solution.py:62
  108.9 11.8 %mlp_weight_grads.1 = (bf16[2,2,1024,128]{3,2,1,0:T(8,128)(2,1)}, bf16[2,2,1024,128]{3,2,1,0:T(8,128)(2,1)}, bf16[2,2,1024,128]{3,2,1,0:T(8,128)(2,1)}, bf16[2,2,1024,128]{3,2,1,0:T(8,128)(2,1)}) custom-call(s32[4]{0:T(128)} %pad_add_fusion.sc, bf16[512,1024]{1,0:T(8,128)(2,1)} %get-tuple-element.125.act0.an, bf16[512,1024]{1,0:T(8,128)(2,1)} %get-tuple-element.137.pn, ...), custom_call_target="tpu_custom_call" | custom-call | flops 13224999936 | bytes 41400000 | tf_op jit(solution)/shard_map/mlp_weight_grads/pallas_call | solution.py:62
  123.9 12.5 %attention_bwd.2 = (bf16[1024,256]{1,0:T(8,128)(2,1)}, bf16[1024,256]{1,0:T(8,128)(2,1)}, f32[1024,512]{1,0:T(8,128)}) custom-call(s32[4]{0:T(128)} %pad_add_fusion.sc, bf16[1024,768]{1,0:T(8,128)(2,1)} %get-tuple-element.113.q_ref.kv_ref.refs_0_.refs_1_.qkv_ref, bf16[1024,768]{1,0:T(8,128)(2,1)} %get-tuple-element.113.q_ref.kv_ref.refs_0_.refs_1_.qkv_ref, ...), custom_call_target="tpu_custom_call" | custom-call | flops 15294999552 | bytes 47880000 | tf_op jit(solution)/shard_map/attention_bwd/pallas_call | solution.py:62
  139.5 7.0 %collective-permute-done.21.refs_4_ = bf16[2,2,1024,128]{3,2,1,0:T(8,128)(2,1)} collective-permute-done((bf16[2,2,1024,128]{3,2,1,0:T(8,128)(2,1)}, bf16[2,2,1024,128]{3,2,1,0:T(8,128)(2,1)}, u32[]{:S(2)}, u32[]{:S(2)}) %collective-permute-start.21) | collective-permute-done | bytes 1048608 | tf_op jit(solution)/shard_map/ppermute | solution.py:50
  153.7 12.2 %attention_bwd.3 = (bf16[1024,256]{1,0:T(8,128)(2,1)}, bf16[1024,256]{1,0:T(8,128)(2,1)}, bf16[1024,512]{1,0:T(8,128)(2,1)}) custom-call(s32[4]{0:T(128)} %pad_add_fusion.sc, bf16[1024,768]{1,0:T(8,128)(2,1)} %get-tuple-element.113.q_ref.kv_ref.refs_0_.refs_1_.qkv_ref, ...), custom_call_target="tpu_custom_call", output_to_operand_aliasing={{0}: (9, {}), {1}: (10, {})} | custom-call | flops 15294999552 | bytes 47880000 | tf_op jit(solution)/shard_map/attention_bwd/pallas_call | solution.py:62
  165.8 7.7 %attention_weight_grads.1 = (bf16[2,1024,128]{2,1,0:T(8,128)(2,1)}, bf16[2,1024,128]{2,1,0:T(8,128)(2,1)}, bf16[2,1024,128]{2,1,0:T(8,128)(2,1)}, bf16[2,1024,128]{2,1,0:T(8,128)(2,1)}) custom-call(s32[4]{0:T(128)} %pad_add_fusion.sc, bf16[1024,1024]{1,0:T(8,128)(2,1)} %get-tuple-element.154.n1, bf16[1024,256]{1,0:T(8,128)(2,1)} %get-tuple-element.155.dq_ref, ...), custom_call_target="tpu_custom_call" | custom-call | flops 10350000128 | bytes 32400000 | tf_op jit(solution)/shard_map/attention_weight_grads/pallas_call | solution.py:62
  174.9 3.9 %pick_team.2 = (bf16[2,1024,128]{2,1,0:T(8,128)(2,1)}, bf16[2,1024,128]{2,1,0:T(8,128)(2,1)}) custom-call(s32[4]{0:T(128)} %pad_add_fusion.sc, bf16[2,2,1024,128]{3,2,1,0:T(8,128)(2,1)} %get-tuple-element.145.refs_0_, bf16[2,2,1024,128]{3,2,1,0:T(8,128)(2,1)} %collective-permute-done.20.refs_1_, bf16[1,2,1024,128]{3,2,1,0:T(8,128)(2,1)} %bitcast.15.refs_2_, ...), custom_call_target="tpu_custom_call" | custom-call | flops 3910000128 | bytes 12240000 | tf_op jit(solution)/shard_map/pick_team/pallas_call | solution.py:62
  181.9 7.8 %norm_one_grad.1 = (bf16[2,1040,256]{2,1,0:T(8,128)(2,1)}, bf16[2,1040,256]{2,1,0:T(8,128)(2,1)}) custom-call(s32[4]{0:T(128)} %pad_add_fusion.sc, bf16[1024,768]{1,0:T(8,128)(2,1)} %get-tuple-element.113.q_ref.kv_ref.refs_0_.refs_1_.qkv_ref, bf16[1024,256]{1,0:T(8,128)(2,1)} %get-tuple-element.155.dq_ref, bf16[1024,512]{1,0:T(8,128)(2,1)} %get-tuple-element.152.dkv_ref, ...), custom_call_target="tpu_custom_call" | custom-call | flops 13454999552 | bytes 42120000 | tf_op jit(solution)/shard_map/norm_one_grad/pallas_call | solution.py:62
  196.5 6.1 %trunk_head.1 = (bf16[8,128,192]{2,1,0:T(8,128)(2,1)}, f32[256,576]{1,0:T(8,128)}, f32[8,256]{1,0:T(8,128)}) custom-call(s32[4]{0:T(128)} %pad_add_fusion.sc, f32[512,256]{1,0:T(8,128)} %get-tuple-element.169.near, f32[512,256]{1,0:T(8,128)} %get-tuple-element.170.far, bf16[2,2,528,256]{3,2,1,0:T(8,128)(2,1)} %get-tuple-element.167.a, ...), custom_call_target="tpu_custom_call" | custom-call | flops 8049999872 | bytes 25200000 | tf_op jit(solution)/shard_map/trunk_head/pallas_call | solution.py:62
  215.4 7.1 %collective-permute-done.40 = bf16[2,128,128]{2,1,0:T(8,128)(2,1)S(1)} collective-permute-done((bf16[2,128,128]{2,1,0:T(8,128)(2,1)}, bf16[2,128,128]{2,1,0:T(8,128)(2,1)S(1)}, u32[]{:S(2)}, u32[]{:S(2)}) %collective-permute-start.40) | collective-permute-done | bytes 65568 | tf_op jit(solution)/shard_map/ppermute | solution.py:50
  227.5 5.2 %collective-permute-done.42.refs_5_ = bf16[4,2,128,128]{3,2,1,0:T(8,128)(2,1)} collective-permute-done((bf16[4,2,128,128]{3,2,1,0:T(8,128)(2,1)S(1)}, bf16[4,2,128,128]{3,2,1,0:T(8,128)(2,1)}, u32[]{:S(2)}, u32[]{:S(2)}) %collective-permute-start.42) | collective-permute-done | bytes 262176 | tf_op jit(solution)/shard_map/ppermute | solution.py:50
  234.4 8.2 %embed_back.1 = (bf16[2,2,2,128,192]{4,3,2,1,0:T(8,128)(2,1)}, bf16[2,2,2,128,192]{4,3,2,1,0:T(8,128)(2,1)}, bf16[2,32,1280]{2,1,0:T(8,128)(2,1)}, bf16[2,32,128...) custom-call(s32[4]{0:T(128)} %pad_add_fusion.sc, ...), custom_call_target="tpu_custom_call" | custom-call | flops 10350000128 | bytes 32400000 | tf_op jit(solution)/shard_map/embed_back/pallas_call | solution.py:62
  261.7 3.6 %collective-permute-done.49.refs_1_ = bf16[4,2,128,128]{3,2,1,0:T(8,128)(2,1)} collective-permute-done((bf16[4,2,128,128]{3,2,1,0:T(8,128)(2,1)}, bf16[4,2,128,128]{3,2,1,0:T(8,128)(2,1)}, u32[]{:S(2)}, u32[]{:S(2)}) %collective-permute-start.49) | collective-permute-done | bytes 262176 | tf_op jit(solution)/shard_map/ppermute | solution.py:50
  268.9 6.0 %mlp_grads_out.1 = (f32[512,1024]{1,0:T(8,128)}, f32[128,4096]{1,0:T(8,128)}) custom-call(s32[4]{0:T(128)} %pad_add_fusion.sc, bf16[1024,128]{1,0:T(8,128)(2,1)} %get-tuple-element.177.refs_0_, bf16[1024,128]{1,0:T(8,128)(2,1)} %collective-permute-done.36.refs_1_, bf16[1024,128]{1,0:T(8,128)(2,1)} %collective-permute-done.37.refs_2_, ...), custom_call_target="tpu_custom_call" | custom-call | flops 5405000192 | bytes 16920000 | tf_op jit(solution)/shard_map/mlp_grads_out/pallas_call | solution.py:62
  277.0 5.0 %attention_grads_out.1 = (f32[128,3072]{1,0:T(8,128)}, f32[128,1024]{1,0:T(8,128)}) custom-call(s32[4]{0:T(128)} %pad_add_fusion.sc, bf16[4,2,128,128]{3,2,1,0:T(8,128)(2,1)} %pad_maximum_fusion.3.refs_0_, bf16[4,2,128,128]{3,2,1,0:T(8,128)(2,1)} %collective-permute-done.49.refs_1_, bf16[4,2,128,128]{3,2,1,0:T(8,128)(2,1)} %collective-permute-done.50.refs_2_, ...), custom_call_target="tpu_custom_call" | custom-call | flops 4024999936 | bytes 12600000 | tf_op jit(solution)/shard_map/attention_grads_out/pallas_call | solution.py:62
  (189 shorter events, 103.6 us)
Async XLA Ops:
  19.1 32.1 %collective-permute-start.9 = (bf16[2,128,192]{2,1,0:T(8,128)(2,1)S(1)}, bf16[2,128,192]{2,1,0:T(8,128)(2,1)}, u32[]{:S(2)}, u32[]{:S(2)}) collective-permute-start(bf16[2,128,192]{2,1,0:T(8,128)(2,1)S(1)} %pad_maximum_fusion.5.refs_0_), channel_id=1, source_target_pairs={{0,1},{1,0},{2,3},{3,2},{4,5},{5,4},{6,7},{7,6},{8,9},{9,8},{10,11... | collective-permute-start | bytes 294920 | tf_op jit(solution)/shard_map/ppermute | solution.py:50
  20.8 30.9 %collective-permute-start.11 = (bf16[2,128,192]{2,1,0:T(8,128)(2,1)}, bf16[2,128,192]{2,1,0:T(8,128)(2,1)}, u32[]{:S(2)}, u32[]{:S(2)}) collective-permute-start(bf16[2,128,192]{2,1,0:T(8,128)(2,1)} %collective-permute-done.10.refs_2_), channel_id=1, source_target_pairs={{0,1},{1,0},{2,3},{3,2},{4,5},{5,4},{6,7},{7,6},{8,9},{9,8},{10,11... | collective-permute-start | bytes 294920 | tf_op jit(solution)/shard_map/ppermute | solution.py:50
  51.1 27.4 %collective-permute-start.5 = (bf16[512,256]{1,0:T(8,128)(2,1)S(1)}, bf16[512,256]{1,0:T(8,128)(2,1)}, u32[]{:S(2)}, u32[]{:S(2)}) collective-permute-start(bf16[512,256]{1,0:T(8,128)(2,1)S(1)} %copy-done.11), channel_id=1, source_target_pairs={{0,1},{1,0},{2,3},{3,2},{4,5},{5,4},{6,7},{7,6},{8,9},{9,8},{10,11... | collective-permute-start | bytes 786440 | tf_op jit(solution)/shard_map/ppermute | solution.py:50
  59.4 19.1 %collective-permute-start.6 = (bf16[512,256]{1,0:T(8,128)(2,1)}, bf16[512,256]{1,0:T(8,128)(2,1)}, u32[]{:S(2)}, u32[]{:S(2)}) collective-permute-start(bf16[512,256]{1,0:T(8,128)(2,1)} %collective-permute-done.4.refs_2_), channel_id=1, source_target_pairs={{0,1},{1,0},{2,3},{3,2},{4,5},{5,4},{6,7},{7,6},{8,9},{9,8},{10,11... | collective-permute-start | bytes 786440 | tf_op jit(solution)/shard_map/ppermute | solution.py:50
  76.6 27.1 %collective-permute-start.15 = (bf16[256,1024]{1,0:T(8,128)(2,1)}, bf16[256,1024]{1,0:T(8,128)(2,1)}, u32[]{:S(2)}, u32[]{:S(2)}) collective-permute-start(bf16[256,1024]{1,0:T(8,128)(2,1)} %get-tuple-element.134), channel_id=1, source_target_pairs={{0,2},{1,3},{2,0},{3,1},{4,6},{5,7},{6,4},{7,5},{8,10},{9,11},{10,... | collective-permute-start | bytes 1572872 | tf_op jit(solution)/shard_map/ppermute | solution.py:50
  77.1 26.6 %collective-permute-start.16 = (bf16[256,1024]{1,0:T(8,128)(2,1)}, bf16[256,1024]{1,0:T(8,128)(2,1)}, u32[]{:S(2)}, u32[]{:S(2)}) collective-permute-start(bf16[256,1024]{1,0:T(8,128)(2,1)} %get-tuple-element.135), channel_id=1, source_target_pairs={{0,3},{1,2},{2,1},{3,0},{4,7},{5,6},{6,5},{7,4},{8,11},{9,10},{10,... | collective-permute-start | bytes 1572872 | tf_op jit(solution)/shard_map/ppermute | solution.py:50
  103.5 32.9 %collective-permute-start.26 = (bf16[2,2,528,256]{3,2,1,0:T(8,128)(2,1)}, bf16[2,2,528,256]{3,2,1,0:T(8,128)(2,1)}, u32[]{:S(2)}, u32[]{:S(2)}) collective-permute-start(bf16[2,2,528,256]{3,2,1,0:T(8,128)(2,1)} %get-tuple-element.130), channel_id=1, source_target_pairs={{0,1},{1,0},{2,3},{3,2},{4,5},{5,4},{6,7},{7,6},{8,9},{9,8},{10,11... | collective-permute-start | bytes 3244040 | tf_op jit(solution)/shard_map/ppermute | solution.py:50
  108.5 15.3 %collective-permute-start.17 = (bf16[256,1024]{1,0:T(8,128)(2,1)}, bf16[256,1024]{1,0:T(8,128)(2,1)}, u32[]{:S(2)}, u32[]{:S(2)}) collective-permute-start(bf16[256,1024]{1,0:T(8,128)(2,1)} %norm_two_back.1.refs_5_), channel_id=1, source_target_pairs={{0,2},{1,3},{2,0},{3,1},{4,6},{5,7},{6,4},{7,5},{8,10},{9,11},{10,... | collective-permute-start | bytes 1572872 | tf_op jit(solution)/shard_map/ppermute | solution.py:50
  108.9 15.0 %collective-permute-start.18 = (bf16[256,1024]{1,0:T(8,128)(2,1)}, bf16[256,1024]{1,0:T(8,128)(2,1)}, u32[]{:S(2)}, u32[]{:S(2)}) collective-permute-start(bf16[256,1024]{1,0:T(8,128)(2,1)} %norm_two_back.1.refs_5_), channel_id=1, source_target_pairs={{0,1},{1,0},{2,3},{3,2},{4,5},{5,4},{6,7},{7,6},{8,9},{9,8},{10,11... | collective-permute-start | bytes 1572872 | tf_op jit(solution)/shard_map/ppermute | solution.py:50
  120.7 25.9 %collective-permute-start.21 = (bf16[2,2,1024,128]{3,2,1,0:T(8,128)(2,1)}, bf16[2,2,1024,128]{3,2,1,0:T(8,128)(2,1)}, u32[]{:S(2)}, u32[]{:S(2)}) collective-permute-start(bf16[2,2,1024,128]{3,2,1,0:T(8,128)(2,1)} %get-tuple-element.141), channel_id=1, source_target_pairs={{0,16},{8,24},{16,0},{24,8},{1,17},{9,25},{17,1},{25,9},{2,18},{10... | collective-permute-start | bytes 3145736 | tf_op jit(solution)/shard_map/ppermute | solution.py:50
  122.4 27.8 %collective-permute-start.20 = (bf16[2,2,1024,128]{3,2,1,0:T(8,128)(2,1)}, bf16[2,2,1024,128]{3,2,1,0:T(8,128)(2,1)}, u32[]{:S(2)}, u32[]{:S(2)}) collective-permute-start(bf16[2,2,1024,128]{3,2,1,0:T(8,128)(2,1)} %get-tuple-element.146), channel_id=1, source_target_pairs={{0,8},{8,0},{16,24},{24,16},{1,9},{9,1},{17,25},{25,17},{2,10},{10... | collective-permute-start | bytes 3145736 | tf_op jit(solution)/shard_map/ppermute | solution.py:50
  123.9 29.8 %collective-permute-start.19 = (bf16[256,1024]{1,0:T(8,128)(2,1)}, bf16[256,1024]{1,0:T(8,128)(2,1)}, u32[]{:S(2)}, u32[]{:S(2)}) collective-permute-start(bf16[256,1024]{1,0:T(8,128)(2,1)} %collective-permute-done.17.refs_5_), channel_id=1, source_target_pairs={{0,1},{1,0},{2,3},{3,2},{4,5},{5,4},{6,7},{7,6},{8,9},{9,8},{10,11... | collective-permute-start | bytes 1572872 | tf_op jit(solution)/shard_map/ppermute | solution.py:50
  138.7 57.8 %collective-permute-start.27 = (bf16[1,2,528,256]{3,2,1,0:T(8,128)(2,1)}, bf16[1,2,528,256]{3,2,1,0:T(8,128)(2,1)}, u32[]{:S(2)}, u32[]{:S(2)}) collective-permute-start(bf16[1,2,528,256]{3,2,1,0:T(8,128)(2,1)} %add_convert_fusion), channel_id=1, source_target_pairs={{0,2},{1,3},{2,0},{3,1},{4,6},{5,7},{6,4},{7,5},{8,10},{9,11},{10,... | collective-permute-start | bytes 1622024 | tf_op jit(solution)/shard_map/ppermute | solution.py:50
  148.5 17.3 %collective-permute-start.23 = (bf16[2,1024,128]{2,1,0:T(8,128)(2,1)}, bf16[2,1024,128]{2,1,0:T(8,128)(2,1)}, u32[]{:S(2)}, u32[]{:S(2)}) collective-permute-start(bf16[2,1024,128]{2,1,0:T(8,128)(2,1)} %fusion.1), channel_id=1, source_target_pairs={{0,8},{8,0},{16,24},{24,16},{1,9},{9,1},{17,25},{25,17},{2,10},{10... | collective-permute-start | bytes 1572872 | tf_op jit(solution)/shard_map/ppermute | solution.py:50
  152.1 13.7 %collective-permute-start.22 = (bf16[2,1024,128]{2,1,0:T(8,128)(2,1)}, bf16[2,1024,128]{2,1,0:T(8,128)(2,1)}, u32[]{:S(2)}, u32[]{:S(2)}) collective-permute-start(bf16[2,1024,128]{2,1,0:T(8,128)(2,1)} %fusion), channel_id=1, source_target_pairs={{0,16},{8,24},{16,0},{24,8},{1,17},{9,25},{17,1},{25,9},{2,18},{10... | collective-permute-start | bytes 1572872 | tf_op jit(solution)/shard_map/ppermute | solution.py:50
  173.5 16.2 %collective-permute-start.25 = (bf16[2,1024,128]{2,1,0:T(8,128)(2,1)}, bf16[2,1024,128]{2,1,0:T(8,128)(2,1)}, u32[]{:S(2)}, u32[]{:S(2)}) collective-permute-start(bf16[2,1024,128]{2,1,0:T(8,128)(2,1)} %get-tuple-element.159), channel_id=1, source_target_pairs={{0,16},{8,24},{16,0},{24,8},{1,17},{9,25},{17,1},{25,9},{2,18},{10... | collective-permute-start | bytes 1572872 | tf_op jit(solution)/shard_map/ppermute | solution.py:50
  178.8 30.8 %collective-permute-start.30 = (bf16[2,1024,128]{2,1,0:T(8,128)(2,1)}, bf16[2,1024,128]{2,1,0:T(8,128)(2,1)}, u32[]{:S(2)}, u32[]{:S(2)}) collective-permute-start(bf16[2,1024,128]{2,1,0:T(8,128)(2,1)} %get-tuple-element.161), channel_id=1, source_target_pairs={{0,4},{1,5},{2,6},{3,7},{4,0},{5,1},{6,2},{7,3},{8,12},{9,13},{10,... | collective-permute-start | bytes 1572872 | tf_op jit(solution)/shard_map/ppermute | solution.py:50
  189.7 16.2 %collective-permute-start.31 = (bf16[2,1040,256]{2,1,0:T(8,128)(2,1)}, bf16[2,1040,256]{2,1,0:T(8,128)(2,1)}, u32[]{:S(2)}, u32[]{:S(2)}) collective-permute-start(bf16[2,1040,256]{2,1,0:T(8,128)(2,1)} %get-tuple-element.163), channel_id=1, source_target_pairs={{0,1},{1,0},{2,3},{3,2},{4,5},{5,4},{6,7},{7,6},{8,9},{9,8},{10,11... | collective-permute-start | bytes 3194888 | tf_op jit(solution)/shard_map/ppermute | solution.py:50
  208.0 25.3 %collective-permute-start.32 = (bf16[1,1040,256]{2,1,0:T(8,128)(2,1)}, bf16[1,1040,256]{2,1,0:T(8,128)(2,1)}, u32[]{:S(2)}, u32[]{:S(2)}) collective-permute-start(bf16[1,1040,256]{2,1,0:T(8,128)(2,1)} %add_convert_fusion.1), channel_id=1, source_target_pairs={{0,2},{1,3},{2,0},{3,1},{4,6},{5,7},{6,4},{7,5},{8,10},{9,11},{10,... | collective-permute-start | bytes 1597448 | tf_op jit(solution)/shard_map/ppermute | solution.py:50
  224.7 17.8 %collective-permute-start.36 = (bf16[1024,128]{1,0:T(8,128)(2,1)}, bf16[1024,128]{1,0:T(8,128)(2,1)}, u32[]{:S(2)}, u32[]{:S(2)}) collective-permute-start(bf16[1024,128]{1,0:T(8,128)(2,1)} %get-tuple-element.177.refs_0_), channel_id=1, source_target_pairs={{0,8},{8,0},{16,24},{24,16},{1,9},{9,1},{17,25},{25,17},{2,10},{10... | collective-permute-start | bytes 786440 | tf_op jit(solution)/shard_map/ppermute | solution.py:50
  226.2 19.9 %collective-permute-start.45 = (bf16[1,1024,128]{2,1,0:T(8,128)(2,1)}, bf16[1,1024,128]{2,1,0:T(8,128)(2,1)}, u32[]{:S(2)}, u32[]{:S(2)}) collective-permute-start(bf16[1,1024,128]{2,1,0:T(8,128)(2,1)} %get-tuple-element.174), channel_id=1, source_target_pairs={{0,4},{1,5},{2,6},{3,7},{4,0},{5,1},{6,2},{7,3},{8,12},{9,13},{10,... | collective-permute-start | bytes 786440 | tf_op jit(solution)/shard_map/ppermute | solution.py:50
  226.5 17.6 %collective-permute-start.43 = (bf16[4,2,128,128]{3,2,1,0:T(8,128)(2,1)S(1)}, bf16[4,2,128,128]{3,2,1,0:T(8,128)(2,1)}, u32[]{:S(2)}, u32[]{:S(2)}) collective-permute-start(bf16[4,2,128,128]{3,2,1,0:T(8,128)(2,1)S(1)} %pad_maximum_fusion.2.refs_4_), channel_id=1, source_target_pairs={{0,16},{8,24},{16,0},{24,8},{1,17},{9,25},{17,1},{25,9},{2,18},{10... | collective-permute-start | bytes 786440 | tf_op jit(solution)/shard_map/ppermute | solution.py:50
  257.8 19.1 %collective-permute-start.50 = (bf16[4,2,128,128]{3,2,1,0:T(8,128)(2,1)}, bf16[4,2,128,128]{3,2,1,0:T(8,128)(2,1)}, u32[]{:S(2)}, u32[]{:S(2)}) collective-permute-start(bf16[4,2,128,128]{3,2,1,0:T(8,128)(2,1)} %pad_maximum_fusion.3.refs_0_), channel_id=1, source_target_pairs={{0,16},{8,24},{16,0},{24,8},{1,17},{9,25},{17,1},{25,9},{2,18},{10... | collective-permute-start | bytes 786440 | tf_op jit(solution)/shard_map/ppermute | solution.py:50
  261.6 14.3 %collective-permute-start.56 = (bf16[32,1280]{1,0:T(8,128)(2,1)S(1)}, bf16[32,1280]{1,0:T(8,128)(2,1)S(1)}, u32[]{:S(2)}, u32[]{:S(2)}) collective-permute-start(bf16[32,1280]{1,0:T(8,128)(2,1)S(1)} %fusion.5.refs_0_), channel_id=1, source_target_pairs={{0,8},{8,0},{16,24},{24,16},{1,9},{9,1},{17,25},{25,17},{2,10},{10... | collective-permute-start | bytes 245768 | tf_op jit(solution)/shard_map/ppermute | solution.py:50
  (51 other events, 457.2 us)
where the time goes:
time: 298 us; the launch traced here: 296 us
  Pallas kernels  171 us (57%)
  starting transfers between devices  53.2 us (18%)
  waiting for transfers between devices  39.4 us (13%)
  other arithmetic  22.4 us (8%)
  local copies, waits for them, and re-layouts  8.19 us (3%)
    pallas_call x22, Pallas kernels, kernel(): pl.pallas_call(body, grid_spec=pltpu.PrefetchScalarGridSpec(num_scalar_pr...  171 us
    ppermute x59, starting transfers between devices, swap(): return lax.ppermute(x, axis, [(i, i ^ bit) for i in range(n)])  53.2 us
    ppermute x59, waiting for transfers between devices, swap(): return lax.ppermute(x, axis, [(i, i ^ bit) for i in range(n)])  39.4 us
    convert_element_type x7, other arithmetic, add_low(): return (a.astype(F32) + b.astype(F32)).astype(BF)  12.1 us
  transfers between devices with their start and end apart: 59, of which 14 were waited for; matrix products, arithmetic and copies ran while one was open for 8% of the time, Pallas kernels for 57%

commit v1 on v0

--- a/solution.py
+++ b/solution.py
@@ -10,7 +10,7 @@
 HEADS = 16
 LANES = 128
 KEY_CHUNK = 512
-VMEM_LIMIT = 127 * 512 * 1024
+VMEM_LIMIT = 48 * 1024 * 1024
 BF = jnp.bfloat16
 F32 = jnp.float32
 
@@ -82,6 +82,10 @@
 
 def hold(scalars, *values):
     scalars[1].extend(values)
+
+
+def after(values, *others):
+    return list(lax.optimization_barrier((*values, *others))[: len(values)])
 
 
 def whole(array):
@@ -1232,22 +1236,25 @@
     first_team = team == 0
     valid = jnp.where(first_team, valid_rows[0], valid_rows[1])
     scalars = (jnp.stack([team, me, lax.axis_index("grp"), valid]).astype(jnp.int32), [])
-    gain1 = ln1_gain.astype(F32)[None]
-    gain2 = ln2_gain.astype(F32)[None]
-
-    def gather_sample(x):
+
+    def gather_pair(x):
         flat = x.reshape(s.teams, s.sec_tokens, s.chan)
         mine = jnp.where(first_team, flat[0], flat[1])
         other = swap(jnp.where(first_team, flat[1], flat[0]), "sec", s.members)
-        pair = jnp.stack([mine, other])
+        return jnp.stack([mine, other])
+
+    def gather_sample(pair):
         across = swap(pair, "sec", chip)
         return [pair, swap(pair, "sec", core), across, swap(across, "sec", core)]
 
     def go_home(keep, got, far):
         mine = three_terms(keep[0], got[0], far)
+        other = jnp.where(first_team, mine[1], mine[0]).astype(BF)
+        return mine, swap(other, "sec", s.members)
+
+    def at_home(mine, other):
         own = jnp.where(first_team, mine[0], mine[1])
-        other = jnp.where(first_team, mine[1], mine[0]).astype(BF)
-        other = swap(other, "sec", s.members).astype(F32)
+        other = other.astype(F32)
         both = [jnp.where(first_team, own, other), jnp.where(first_team, other, own)]
         return [jnp.stack([x[kind] for x in both]).reshape(fields.shape) for kind in range(2)]
 
@@ -1256,8 +1263,12 @@
         return keep, got, swap(add_low(keep[1:2], got[1:2]), "sec", chip)
 
     w_head_t = jnp.transpose(w_head, (0, 2, 1))
+    fields_pair = gather_pair(fields)
+    late1, late2, b_up = after([ln1_gain, ln2_gain, b_up], fields_pair)
+    gain1 = late1.astype(F32)[None]
+    gain2 = late2.astype(F32)[None]
     in_cat, hidden0, normed1, qkv, stats = embed_qkv(
-        s, scalars, gather_sample(fields), w_embed.reshape(3 * s.chan, s.d), gain1, w_qkv
+        s, scalars, gather_sample(fields_pair), w_embed.reshape(3 * s.chan, s.d), gain1, w_qkv
     )
     att_near, *rest = attention_fwd(s, scalars, qkv, False)
     saved_near = (att_near, *rest)
@@ -1267,7 +1278,7 @@
     from_chip_near = swap(att_far, "sec", chip)
     hold(scalars, from_chip_far)
     cot_cat, grad_mlp = cotangent_grad(
-        s, scalars, gather_sample(cotangent), w_head_t.reshape(3 * s.chan, s.d)
+        s, scalars, gather_sample(gather_pair(cotangent)), w_head_t.reshape(3 * s.chan, s.d)
     )
     att_pieces_far = [att_far, swap(att_far, "sec", core), from_chip_far, swap(from_chip_far, "sec", core)]
     att_pieces_near = [att_near, swap(att_near, "sec", core), from_chip_near, swap(from_chip_near, "sec", core)]
@@ -1312,24 +1323,31 @@
     head_home, head_part, gain2_grad = trunk_head(
         s, scalars, (hown_near, hown_far), trunk_terms, w_head_t, cot_cat
     )
-    g1 = scatter_features(g1_keep, g1_send)
-    hold(scalars, *[terms[2] for terms in att_terms])
+    g1_got = swap(g1_send, "sec", core)
+    g1_sum = add_low(g1_keep[1:2], g1_got[1:2])
+    g1 = (g1_keep, g1_got, swap(g1_sum, "sec", chip))
+    hold(scalars, g1_sum, *[terms[2] for terms in att_terms])
     att_kept, send = pick_team(s, scalars, *att_terms, 1)
     att_swapped = swap(send, "sec", s.members)
     *crossed, downs = pick_member(s, scalars, mlp_kept, mlp_swapped)
-    mlp_parts = (all_of_group(downs, False), all_of_group(cross(s, crossed), True))
+    ups = cross(s, crossed)
+    downs = [downs, swap(downs, "grp", 1), swap(downs, "grp", 2)]
+    ups = [ups, swap(ups, "grp", 1), swap(ups, "grp", 2)]
     keep, send, *edges = embed_back(
         s, scalars, g1, own, stats, hidden0, gain1, w_embed, in_cat, head_home, head_part, gain2_grad, bias_grad
     )
     edges = edges[:1] + [swap(edges[j], "grp", j) for j in range(1, s.group)]
     home_got = swap(send, "sec", core)
-    hold(scalars, *mlp_parts[0], *mlp_parts[1])
+    mlp_parts = (
+        downs + [swap(after(downs[2:], edges[0])[0], "grp", 1)],
+        ups + [swap(after(ups[1:2], edges[0])[0], "grp", 2)],
+    )
     crossed = pick_member(s, scalars, att_kept, att_swapped)
     att_parts = all_of_group(cross(s, crossed), True)
     home_far = swap(add_low(keep[1], home_got[1]), "sec", chip)
     down_grad, up_grad = mlp_grads_out(s, scalars, *mlp_parts)
     hold(scalars, home_far)
-    head_output, input_grad = go_home(keep, home_got, home_far)
+    home_mine, home_other = go_home(keep, home_got, home_far)
 
     total = edges[0].astype(F32) + edges[1].astype(F32) + edges[2].astype(F32) + edges[3].astype(F32)
     kept = jnp.where(first_team, total[0], total[1])
@@ -1337,6 +1355,8 @@
     edges = (kept + swap(given, "sec", s.members).astype(F32)).astype(BF)
     edge_parts = all_of_group(edges, True)
     qkv_grad, out_grad = attention_grads_out(s, scalars, att_parts)
+    hold(scalars, home_other)
+    head_output, input_grad = at_home(home_mine, home_other)
     embed_t, head_t, small = edge_grads_out(s, scalars, edge_parts)
     embed_grad = embed_t.reshape(3, s.chan, s.db)
     head_grad = jnp.transpose(head_t.reshape(3, s.chan, s.db), (0, 2, 1))

time: 298 us -> 272 us (0.913)
  Pallas kernels: 171 us -> 130 us
  waiting for transfers between devices: 39.4 us -> 61.5 us
  other arithmetic: 22.4 us -> 4.4 us
  local copies, waits for them, and re-layouts: 8.19 us -> 17.9 us
    pallas_call x22, Pallas kernels: 171 us -> 130 us  [kernel(): pl.pallas_call(body, grid_spec=pltpu.PrefetchScalarGridSpec(num_scalar_pr...]
    ppermute x59, waiting for transfers between devices: 39.4 us -> 61.5 us  [swap(): return lax.ppermute(x, axis, [(i, i ^ bit) for i in range(n)])]
    unnamed x34 -> x74, local copies, waits for them, and re-layouts: 2.94 us -> 14.1 us
    convert_element_type x7, other arithmetic: 12.1 us -> 2.71 us  [add_low(): return (a.astype(F32) + b.astype(F32)).astype(BF)]
  transfers between devices with their start and end apart: 59 -> 59, of which waited for: 14 -> 22; matrix products, arithmetic and copies ran while one was open for 8% -> 2% of each run, Pallas kernels for 57% -> 47%
where the time goes in v1:
time: 272 us; the launch traced here: 271 us
  Pallas kernels  130 us (48%)
  waiting for transfers between devices  61.5 us (23%)
  starting transfers between devices  55 us (20%)
  local copies, waits for them, and re-layouts  17.9 us (7%)
  other arithmetic  4.4 us (2%)
    pallas_call x22, Pallas kernels, kernel(): pl.pallas_call(body, grid_spec=pltpu.PrefetchScalarGridSpec(num_scalar_pr...  130 us
    ppermute x59, waiting for transfers between devices, swap(): return lax.ppermute(x, axis, [(i, i ^ bit) for i in range(n)])  61.5 us
    ppermute x59, starting transfers between devices, swap(): return lax.ppermute(x, axis, [(i, i ^ bit) for i in range(n)])  55 us
    unnamed x74, local copies, waits for them, and re-layouts  14.1 us
  transfers between devices with their start and end apart: 59, of which 22 were waited for; matrix products, arithmetic and copies ran while one was open for 2% of the time, Pallas kernels for 47%

profile of v1, /device:TPU:0, one launch (start us, length us, event | category | flops | bytes accessed | tf_op | source)
XLA Modules:
  0.0 271.2 jit_solution(1654246099472978965)
XLA Ops:
  1.9 4.1 %collective-permute-start = (bf16[128,192]{1,0:T(8,128)(2,1)S(1)}, bf16[128,192]{1,0:T(8,128)(2,1)S(1)}, u32[]{:S(2)}, u32[]{:S(2)}) collective-permute-start(bf16[128,192]{1,0:T(8,128)(2,1)S(1)} %select_n.119), channel_id=1, source_target_pairs={{0,4},{1,5},{2,6},{3,7},{4,0},{5,1},{6,2},{7,3},{8,12},{9,13},{10,... | collective-permute-start | bytes 147464 | tf_op jit(solution)/shard_map/ppermute | solution.py:50
  18.2 8.6 %embed_qkv.1 = (bf16[1024,576]{1,0:T(8,128)(2,1)S(1)}, f32[1024,1024]{1,0:T(8,128)}, bf16[1024,1024]{1,0:T(8,128)(2,1)}, bf16[1024,768]{1,0:T(8,128)(2,1)S(1)}, f32[1024,128]{1,0:T(8,128)S(1)}) custom-call(s32[4]{0:T(128)S(1)} %pad_add_fusion.sc, bf16[2,128,192]{2,1,0:T(8,128)(2,1)S(1)} %pad_maximum_fusion.4.refs_0_, ...), custom_call_target="tpu_custom_call" | custom-call | flops 11040000000 | bytes 34560000 | tf_op jit(solution)/shard_map/embed_qkv/pallas_call | solution.py:62
  27.9 6.8 %attention_fwd.2 = (bf16[512,256]{1,0:T(8,128)(2,1)S(1)}, bf16[4,2,1024,256]{3,2,1,0:T(8,128)(2,1)}, f32[512,128]{1,0:T(8,128)S(1)}) custom-call(s32[4]{0:T(128)S(1)} %pad_add_fusion.sc, bf16[1024,768]{1,0:T(8,128)(2,1)S(1)} %get-tuple-element.119.q_ref.kv_ref.refs_0_.refs_1_.qkv_ref, ...), custom_call_target="tpu_custom_call" | custom-call | flops 10579999744 | bytes 33120000 | tf_op jit(solution)/shard_map/attention_fwd/pallas_call | solution.py:62
  36.4 6.8 %attention_fwd.3 = (bf16[512,256]{1,0:T(8,128)(2,1)S(1)}, bf16[4,2,1024,256]{3,2,1,0:T(8,128)(2,1)}, f32[512,128]{1,0:T(8,128)S(1)}) custom-call(s32[4]{0:T(128)S(1)} %pad_add_fusion.sc, bf16[1024,768]{1,0:T(8,128)(2,1)S(1)} %get-tuple-element.119.q_ref.kv_ref.refs_0_.refs_1_.qkv_ref, ...), custom_call_target="tpu_custom_call" | custom-call | flops 10579999744 | bytes 33120000 | tf_op jit(solution)/shard_map/attention_fwd/pallas_call | solution.py:62
  52.6 15.2 %mlp.3 = (bf16[512,1024]{1,0:T(8,128)(2,1)S(1)}, bf16[512,1024]{1,0:T(8,128)(2,1)S(1)}, bf16[512,1024]{1,0:T(8,128)(2,1)S(1)}, bf16[512,1024]{1,0:T(8,128)(2,1)}...) custom-call(s32[4]{0:T(128)S(1)} %pad_add_fusion.sc, ...), custom_call_target="tpu_custom_call" | custom-call | flops 19549999104 | bytes 61200000 | tf_op jit(solution)/shard_map/mlp/pallas_call | solution.py:62
  71.6 15.3 %mlp.2 = (bf16[512,1024]{1,0:T(8,128)(2,1)S(1)}, bf16[512,1024]{1,0:T(8,128)(2,1)S(1)}, bf16[512,1024]{1,0:T(8,128)(2,1)S(1)}, bf16[512,1024]{1,0:T(8,128)(2,1)}...) custom-call(s32[4]{0:T(128)S(1)} %pad_add_fusion.sc, ...), custom_call_target="tpu_custom_call" | custom-call | flops 19549999104 | bytes 61200000 | tf_op jit(solution)/shard_map/mlp/pallas_call | solution.py:62
  90.1 5.4 %trunk_part.1 = (bf16[2,2,528,256]{3,2,1,0:T(8,128)(2,1)S(1)}, bf16[2,2,528,256]{3,2,1,0:T(8,128)(2,1)S(1)}) custom-call(s32[4]{0:T(128)S(1)} %pad_add_fusion.sc, bf16[512,1024]{1,0:T(8,128)(2,1)S(1)} %get-tuple-element.133.act0.an, f32[1,1024]{1,0:T(1,128)S(1)} %get-tuple-element.134.gs0, bf16[512,1024]{1,0:T(8,128)(2,1)S(1)} %get-tuple-element.136.act1.af, ...), custom_call_target="tpu_custom_call" | custom-call | flops 4600000000 | bytes 14400000 | tf_op jit(solution)/shard_map/trunk_part/pallas_call | solution.py:62
  99.2 10.4 %mlp_weight_grads.1 = (bf16[2,2,1024,128]{3,2,1,0:T(8,128)(2,1)S(1)}, bf16[2,2,1024,128]{3,2,1,0:T(8,128)(2,1)S(1)}, bf16[2,2,1024,128]{3,2,1,0:T(8,128)(2,1)S(1)}, bf16[2,2,1024,128]{3,2,1,0:T(8,128)(2,1)S(1)}) custom-call(s32[4]{0:T(128)S(1)} %pad_add_fusion.sc, bf16[512,1024]{1,0:T(8,128)(2,1)S(1)} %get-tuple-element.133.act0.an, ...), custom_call_target="tpu_custom_call" | custom-call | flops 13224999936 | bytes 41400000 | tf_op jit(solution)/shard_map/mlp_weight_grads/pallas_call | solution.py:62
  113.0 10.4 %attention_bwd.2 = (bf16[1024,256]{1,0:T(8,128)(2,1)S(1)}, bf16[1024,256]{1,0:T(8,128)(2,1)S(1)}, f32[1024,512]{1,0:T(8,128)}) custom-call(s32[4]{0:T(128)S(1)} %pad_add_fusion.sc, bf16[1024,768]{1,0:T(8,128)(2,1)S(1)} %copy-done.8, bf16[1024,768]{1,0:T(8,128)(2,1)S(1)} %copy-done.8, bf16[512,256]{1,0:T(8,128)(2,1)S(1)} %get-tuple-element.124.refs_0_.refs_2_, ...), custom_call_target="tpu_custom_call" | custom-call | flops 15294999552 | bytes 47880000 | tf_op jit(solution)/shard_map/attention_bwd/pallas_call | solution.py:62
  125.8 9.5 %collective-permute-done.21.refs_4_ = bf16[2,2,1024,128]{3,2,1,0:T(8,128)(2,1)} collective-permute-done((bf16[2,2,1024,128]{3,2,1,0:T(8,128)(2,1)S(1)}, bf16[2,2,1024,128]{3,2,1,0:T(8,128)(2,1)}, u32[]{:S(2)}, u32[]{:S(2)}) %collective-permute-start.21) | collective-permute-done | bytes 1048608 | tf_op jit(solution)/shard_map/ppermute | solution.py:50
  139.9 9.9 %attention_bwd.3 = (bf16[1024,256]{1,0:T(8,128)(2,1)S(1)}, bf16[1024,256]{1,0:T(8,128)(2,1)S(1)}, bf16[1024,512]{1,0:T(8,128)(2,1)S(1)}) custom-call(s32[4]{0:T(128)S(1)} %pad_add_fusion.sc, bf16[1024,768]{1,0:T(8,128)(2,1)S(1)} %copy-done.8, bf16[1024,768]{1,0:T(8,128)(2,1)S(1)} %copy-done.8, ...), custom_call_target="tpu_custom_call", output_to_operand_aliasing={{0}: (9, {}), {1}: (10, {})} | custom-call | flops 15294999552 | bytes 47880000 | tf_op jit(solution)/shard_map/attention_bwd/pallas_call | solution.py:62
  152.9 5.4 %attention_weight_grads.1 = (bf16[2,1024,128]{2,1,0:T(8,128)(2,1)S(1)}, bf16[2,1024,128]{2,1,0:T(8,128)(2,1)S(1)}, bf16[2,1024,128]{2,1,0:T(8,128)(2,1)S(1)}, bf16[2,1024,128]{2,1,0:T(8,128)(2,1)S(1)}) custom-call(s32[4]{0:T(128)S(1)} %pad_add_fusion.sc, bf16[1024,1024]{1,0:T(8,128)(2,1)} %get-tuple-element.162.n1, ...), custom_call_target="tpu_custom_call" | custom-call | flops 10350000128 | bytes 32400000 | tf_op jit(solution)/shard_map/attention_weight_grads/pallas_call | solution.py:62
  162.9 3.3 %collective-permute-start.31 = (bf16[2,1024,128]{2,1,0:T(8,128)(2,1)S(1)}, bf16[2,1024,128]{2,1,0:T(8,128)(2,1)S(1)}, u32[]{:S(2)}, u32[]{:S(2)}) collective-permute-start(bf16[2,1024,128]{2,1,0:T(8,128)(2,1)S(1)} %get-tuple-element.169), channel_id=1, source_target_pairs={{0,4},{1,5},{2,6},{3,7},{4,0},{5,1},{6,2},{7,3},{8,12},{9,13},{10,... | collective-permute-start | bytes 1572872 | tf_op jit(solution)/shard_map/ppermute | solution.py:50
  168.1 5.6 %norm_one_grad.1 = (bf16[2,1040,256]{2,1,0:T(8,128)(2,1)S(1)}, bf16[2,1040,256]{2,1,0:T(8,128)(2,1)S(1)}) custom-call(s32[4]{0:T(128)S(1)} %pad_add_fusion.sc, bf16[1024,768]{1,0:T(8,128)(2,1)S(1)} %copy-done.9, bf16[1024,256]{1,0:T(8,128)(2,1)S(1)} %copy-done.30, bf16[1024,512]{1,0:T(8,128)(2,1)S(1)} %copy-done.13, bf16[1024,3072]{1,0:T(8,128)(2,1)} %wv.1, ...), custom_call_target="tpu_custom_call" | custom-call | flops 13454999552 | bytes 42120000 | tf_op jit(solution)/shard_map/norm_one_grad/pallas_call | solution.py:62
  175.4 3.2 %collective-permute-done.24.refs_1_ = bf16[2,1024,128]{2,1,0:T(8,128)(2,1)S(1)} collective-permute-done((bf16[2,1024,128]{2,1,0:T(8,128)(2,1)S(1)}, bf16[2,1024,128]{2,1,0:T(8,128)(2,1)S(1)}, u32[]{:S(2)}, u32[]{:S(2)}) %collective-permute-start.24) | collective-permute-done | bytes 524320 | tf_op jit(solution)/shard_map/ppermute | solution.py:50
  179.3 4.2 %trunk_head.1 = (bf16[8,128,192]{2,1,0:T(8,128)(2,1)S(1)}, f32[256,576]{1,0:T(8,128)S(1)}, f32[8,256]{1,0:T(8,128)S(1)}) custom-call(s32[4]{0:T(128)S(1)} %pad_add_fusion.sc, f32[512,256]{1,0:T(8,128)S(1)} %copy-done.24, f32[512,256]{1,0:T(8,128)S(1)} %copy-done.22, bf16[2,2,528,256]{3,2,1,0:T(8,128)(2,1)S(1)} %get-tuple-element.175.a, ...), custom_call_target="tpu_custom_call" | custom-call | flops 8049999872 | bytes 25200000 | tf_op jit(solution)/shard_map/trunk_head/pallas_call | solution.py:62
  193.3 12.9 %collective-permute-done.41 = bf16[2,128,128]{2,1,0:T(8,128)(2,1)S(1)} collective-permute-done((bf16[2,128,128]{2,1,0:T(8,128)(2,1)S(1)}, bf16[2,128,128]{2,1,0:T(8,128)(2,1)S(1)}, u32[]{:S(2)}, u32[]{:S(2)}) %collective-permute-start.41) | collective-permute-done | bytes 65568 | tf_op jit(solution)/shard_map/ppermute | solution.py:50
  209.4 6.1 %embed_back.1 = (bf16[2,2,2,128,192]{4,3,2,1,0:T(8,128)(2,1)S(1)}, bf16[2,2,2,128,192]{4,3,2,1,0:T(8,128)(2,1)S(1)}, bf16[2,32,1280]{2,1,0:T(8,128)(2,1)S(1)}, b...) custom-call(s32[4]{0:T(128)S(1)} %pad_add_fusion.sc, ...), custom_call_target="tpu_custom_call" | custom-call | flops 10350000128 | bytes 32400000 | tf_op jit(solution)/shard_map/embed_back/pallas_call | solution.py:62
  215.5 4.4 %collective-permute-done.43.refs_5_ = bf16[4,2,128,128]{3,2,1,0:T(8,128)(2,1)S(1)} collective-permute-done((bf16[4,2,128,128]{3,2,1,0:T(8,128)(2,1)S(1)}, bf16[4,2,128,128]{3,2,1,0:T(8,128)(2,1)S(1)}, u32[]{:S(2)}, u32[]{:S(2)}) %collective-permute-start.43) | collective-permute-done | bytes 262176 | tf_op jit(solution)/shard_map/ppermute | solution.py:50
  224.0 3.4 %collective-permute-done.52 = bf16[2,32,1280]{2,1,0:T(8,128)(2,1)S(1)} collective-permute-done((bf16[2,32,1280]{2,1,0:T(8,128)(2,1)S(1)}, bf16[2,32,1280]{2,1,0:T(8,128)(2,1)S(1)}, u32[]{:S(2)}, u32[]{:S(2)}) %collective-permute-start.52) | collective-permute-done | bytes 163872 | tf_op jit(solution)/shard_map/ppermute | solution.py:50
  237.6 3.4 %collective-permute-done.55 = bf16[32,1280]{1,0:T(8,128)(2,1)S(1)} collective-permute-done((bf16[32,1280]{1,0:T(8,128)(2,1)S(1)}, bf16[32,1280]{1,0:T(8,128)(2,1)S(1)}, u32[]{:S(2)}, u32[]{:S(2)}) %collective-permute-start.55) | collective-permute-done | bytes 81952 | tf_op jit(solution)/shard_map/ppermute | solution.py:50
  247.6 4.4 %mlp_grads_out.1 = (f32[512,1024]{1,0:T(8,128)}, f32[128,4096]{1,0:T(8,128)}) custom-call(s32[4]{0:T(128)S(1)} %pad_add_fusion.sc, bf16[1024,128]{1,0:T(8,128)(2,1)S(1)} %get-tuple-element.186.refs_0_, bf16[1024,128]{1,0:T(8,128)(2,1)S(1)} %collective-permute-done.37.refs_1_, bf16[1024,128]{1,0:T(8,128)(2,1)S(1)} %collective-permute-done.38.refs_2_, ...), custom_call_target="tpu_custom_call" | custom-call | flops 5405000192 | bytes 16920000 | tf_op jit(solution)/shard_map/mlp_grads_out/pallas_call | solution.py:62
  257.6 5.0 %collective-permute-done.51.refs_3_ = bf16[4,2,128,128]{3,2,1,0:T(8,128)(2,1)S(1)} collective-permute-done((bf16[4,2,128,128]{3,2,1,0:T(8,128)(2,1)S(1)}, bf16[4,2,128,128]{3,2,1,0:T(8,128)(2,1)S(1)}, u32[]{:S(2)}, u32[]{:S(2)}) %collective-permute-start.51) | collective-permute-done | bytes 262176 | tf_op jit(solution)/shard_map/ppermute | solution.py:50
  262.6 3.7 %attention_grads_out.1 = (f32[128,3072]{1,0:T(8,128)}, f32[128,1024]{1,0:T(8,128)}) custom-call(s32[4]{0:T(128)S(1)} %pad_add_fusion.sc, bf16[4,2,128,128]{3,2,1,0:T(8,128)(2,1)S(1)} %pad_maximum_fusion.3.refs_0_, bf16[4,2,128,128]{3,2,1,0:T(8,128)(2,1)S(1)} %collective-permute-done.49.refs_1_, bf16[4,2,128,128]{3,2,1,0:T(8,128)(2,1)S(1)} %collective-permute-done.50.refs_2_, ...), custom_call_target="tpu_custom_call" | custom-call | flops 4024999936 | bytes 12600000 | tf_op jit(solution)/shard_map/attention_grads_out/pallas_call | solution.py:62
  (229 shorter events, 101.3 us)
Async XLA Ops:
  13.1 31.3 %collective-permute-start.9 = (bf16[2,128,192]{2,1,0:T(8,128)(2,1)S(1)}, bf16[2,128,192]{2,1,0:T(8,128)(2,1)S(1)}, u32[]{:S(2)}, u32[]{:S(2)}) collective-permute-start(bf16[2,128,192]{2,1,0:T(8,128)(2,1)S(1)} %pad_maximum_fusion.5.refs_0_), channel_id=1, source_target_pairs={{0,1},{1,0},{2,3},{3,2},{4,5},{5,4},{6,7},{7,6},{8,9},{9,8},{10,11... | collective-permute-start | bytes 294920 | tf_op jit(solution)/shard_map/ppermute | solution.py:50
  18.2 26.7 %collective-permute-start.11 = (bf16[2,128,192]{2,1,0:T(8,128)(2,1)S(1)}, bf16[2,128,192]{2,1,0:T(8,128)(2,1)S(1)}, u32[]{:S(2)}, u32[]{:S(2)}) collective-permute-start(bf16[2,128,192]{2,1,0:T(8,128)(2,1)S(1)} %collective-permute-done.10.refs_2_), channel_id=1, source_target_pairs={{0,1},{1,0},{2,3},{3,2},{4,5},{5,4},{6,7},{7,6},{8,9},{9,8},{10,11... | collective-permute-start | bytes 294920 | tf_op jit(solution)/shard_map/ppermute | solution.py:50
  44.4 27.2 %collective-permute-start.5 = (bf16[512,256]{1,0:T(8,128)(2,1)S(1)}, bf16[512,256]{1,0:T(8,128)(2,1)S(1)}, u32[]{:S(2)}, u32[]{:S(2)}) collective-permute-start(bf16[512,256]{1,0:T(8,128)(2,1)S(1)} %get-tuple-element.124.refs_0_.refs_2_), channel_id=1, source_target_pairs={{0,1},{1,0},{2,3},{3,2},{4,5},{5,4},{6,7},{7,6},{8,9},{9,8},{10,11... | collective-permute-start | bytes 786440 | tf_op jit(solution)/shard_map/ppermute | solution.py:50
  52.6 19.0 %collective-permute-start.6 = (bf16[512,256]{1,0:T(8,128)(2,1)S(1)}, bf16[512,256]{1,0:T(8,128)(2,1)S(1)}, u32[]{:S(2)}, u32[]{:S(2)}) collective-permute-start(bf16[512,256]{1,0:T(8,128)(2,1)S(1)} %collective-permute-done.4.refs_2_), channel_id=1, source_target_pairs={{0,1},{1,0},{2,3},{3,2},{4,5},{5,4},{6,7},{7,6},{8,9},{9,8},{10,11... | collective-permute-start | bytes 786440 | tf_op jit(solution)/shard_map/ppermute | solution.py:50
  69.8 26.1 %collective-permute-start.15 = (bf16[256,1024]{1,0:T(8,128)(2,1)S(1)}, bf16[256,1024]{1,0:T(8,128)(2,1)S(1)}, u32[]{:S(2)}, u32[]{:S(2)}) collective-permute-start(bf16[256,1024]{1,0:T(8,128)(2,1)S(1)} %get-tuple-element.142), channel_id=1, source_target_pairs={{0,2},{1,3},{2,0},{3,1},{4,6},{5,7},{6,4},{7,5},{8,10},{9,11},{10,... | collective-permute-start | bytes 1572872 | tf_op jit(solution)/shard_map/ppermute | solution.py:50
  70.1 25.8 %collective-permute-start.16 = (bf16[256,1024]{1,0:T(8,128)(2,1)S(1)}, bf16[256,1024]{1,0:T(8,128)(2,1)S(1)}, u32[]{:S(2)}, u32[]{:S(2)}) collective-permute-start(bf16[256,1024]{1,0:T(8,128)(2,1)S(1)} %get-tuple-element.143), channel_id=1, source_target_pairs={{0,3},{1,2},{2,1},{3,0},{4,7},{5,6},{6,5},{7,4},{8,11},{9,10},{10,... | collective-permute-start | bytes 1572872 | tf_op jit(solution)/shard_map/ppermute | solution.py:50
  95.6 27.8 %collective-permute-start.26 = (bf16[2,2,528,256]{3,2,1,0:T(8,128)(2,1)S(1)}, bf16[2,2,528,256]{3,2,1,0:T(8,128)(2,1)S(1)}, u32[]{:S(2)}, u32[]{:S(2)}) collective-permute-start(bf16[2,2,528,256]{3,2,1,0:T(8,128)(2,1)S(1)} %get-tuple-element.138), channel_id=1, source_target_pairs={{0,1},{1,0},{2,3},{3,2},{4,5},{5,4},{6,7},{7,6},{8,9},{9,8},{10,11... | collective-permute-start | bytes 3244040 | tf_op jit(solution)/shard_map/ppermute | solution.py:50
  98.8 14.2 %collective-permute-start.17 = (bf16[256,1024]{1,0:T(8,128)(2,1)S(1)}, bf16[256,1024]{1,0:T(8,128)(2,1)S(1)}, u32[]{:S(2)}, u32[]{:S(2)}) collective-permute-start(bf16[256,1024]{1,0:T(8,128)(2,1)S(1)} %norm_two_back.1.refs_5_), channel_id=1, source_target_pairs={{0,2},{1,3},{2,0},{3,1},{4,6},{5,7},{6,4},{7,5},{8,10},{9,11},{10,... | collective-permute-start | bytes 1572872 | tf_op jit(solution)/shard_map/ppermute | solution.py:50
  99.1 13.8 %collective-permute-start.18 = (bf16[256,1024]{1,0:T(8,128)(2,1)S(1)}, bf16[256,1024]{1,0:T(8,128)(2,1)S(1)}, u32[]{:S(2)}, u32[]{:S(2)}) collective-permute-start(bf16[256,1024]{1,0:T(8,128)(2,1)S(1)} %norm_two_back.1.refs_5_), channel_id=1, source_target_pairs={{0,1},{1,0},{2,3},{3,2},{4,5},{5,4},{6,7},{7,6},{8,9},{9,8},{10,11... | collective-permute-start | bytes 1572872 | tf_op jit(solution)/shard_map/ppermute | solution.py:50
  109.6 25.7 %collective-permute-start.21 = (bf16[2,2,1024,128]{3,2,1,0:T(8,128)(2,1)S(1)}, bf16[2,2,1024,128]{3,2,1,0:T(8,128)(2,1)}, u32[]{:S(2)}, u32[]{:S(2)}) collective-permute-start(bf16[2,2,1024,128]{3,2,1,0:T(8,128)(2,1)S(1)} %get-tuple-element.149), channel_id=1, source_target_pairs={{0,16},{8,24},{16,0},{24,8},{1,17},{9,25},{17,1},{25,9},{2,18},{10... | collective-permute-start | bytes 3145736 | tf_op jit(solution)/shard_map/ppermute | solution.py:50
  111.2 26.9 %collective-permute-start.20 = (bf16[2,2,1024,128]{3,2,1,0:T(8,128)(2,1)S(1)}, bf16[2,2,1024,128]{3,2,1,0:T(8,128)(2,1)S(1)}, u32[]{:S(2)}, u32[]{:S(2)}) collective-permute-start(bf16[2,2,1024,128]{3,2,1,0:T(8,128)(2,1)S(1)} %get-tuple-element.154), channel_id=1, source_target_pairs={{0,8},{8,0},{16,24},{24,16},{1,9},{9,1},{17,25},{25,17},{2,10},{10... | collective-permute-start | bytes 3145736 | tf_op jit(solution)/shard_map/ppermute | solution.py:50
  113.0 26.9 %collective-permute-start.19 = (bf16[256,1024]{1,0:T(8,128)(2,1)S(1)}, bf16[256,1024]{1,0:T(8,128)(2,1)S(1)}, u32[]{:S(2)}, u32[]{:S(2)}) collective-permute-start(bf16[256,1024]{1,0:T(8,128)(2,1)S(1)} %collective-permute-done.17.refs_5_), channel_id=1, source_target_pairs={{0,1},{1,0},{2,3},{3,2},{4,5},{5,4},{6,7},{7,6},{8,9},{9,8},{10,11... | collective-permute-start | bytes 1572872 | tf_op jit(solution)/shard_map/ppermute | solution.py:50
  124.3 55.0 %collective-permute-start.27 = (bf16[1,2,528,256]{3,2,1,0:T(8,128)(2,1)}, bf16[1,2,528,256]{3,2,1,0:T(8,128)(2,1)S(1)}, u32[]{:S(2)}, u32[]{:S(2)}) collective-permute-start(bf16[1,2,528,256]{3,2,1,0:T(8,128)(2,1)} %add_convert_fusion), channel_id=1, source_target_pairs={{0,2},{1,3},{2,0},{3,1},{4,6},{5,7},{6,4},{7,5},{8,10},{9,11},{10,... | collective-permute-start | bytes 1622024 | tf_op jit(solution)/shard_map/ppermute | solution.py:50
  158.3 15.5 %collective-permute-start.25 = (bf16[2,1024,128]{2,1,0:T(8,128)(2,1)S(1)}, bf16[2,1024,128]{2,1,0:T(8,128)(2,1)S(1)}, u32[]{:S(2)}, u32[]{:S(2)}) collective-permute-start(bf16[2,1024,128]{2,1,0:T(8,128)(2,1)S(1)} %get-tuple-element.167), channel_id=1, source_target_pairs={{0,16},{8,24},{16,0},{24,8},{1,17},{9,25},{17,1},{25,9},{2,18},{10... | collective-permute-start | bytes 1572872 | tf_op jit(solution)/shard_map/ppermute | solution.py:50
  162.9 24.9 %collective-permute-start.31 = (bf16[2,1024,128]{2,1,0:T(8,128)(2,1)S(1)}, bf16[2,1024,128]{2,1,0:T(8,128)(2,1)S(1)}, u32[]{:S(2)}, u32[]{:S(2)}) collective-permute-start(bf16[2,1024,128]{2,1,0:T(8,128)(2,1)S(1)} %get-tuple-element.169), channel_id=1, source_target_pairs={{0,4},{1,5},{2,6},{3,7},{4,0},{5,1},{6,2},{7,3},{8,12},{9,13},{10,... | collective-permute-start | bytes 1572872 | tf_op jit(solution)/shard_map/ppermute | solution.py:50
  183.7 24.6 %collective-permute-start.32 = (bf16[1,1040,256]{2,1,0:T(8,128)(2,1)S(1)}, bf16[1,1040,256]{2,1,0:T(8,128)(2,1)S(1)}, u32[]{:S(2)}, u32[]{:S(2)}) collective-permute-start(bf16[1,1040,256]{2,1,0:T(8,128)(2,1)S(1)} %add_convert_fusion.1), channel_id=1, source_target_pairs={{0,2},{1,3},{2,0},{3,1},{4,6},{5,7},{6,4},{7,5},{8,10},{9,11},{10,... | collective-permute-start | bytes 1597448 | tf_op jit(solution)/shard_map/ppermute | solution.py:50
  188.5 17.7 %collective-permute-start.41 = (bf16[2,128,128]{2,1,0:T(8,128)(2,1)S(1)}, bf16[2,128,128]{2,1,0:T(8,128)(2,1)S(1)}, u32[]{:S(2)}, u32[]{:S(2)}) collective-permute-start(bf16[2,128,128]{2,1,0:T(8,128)(2,1)S(1)} %get-tuple-element.204), channel_id=1, source_target_pairs={{0,2},{1,3},{2,0},{3,1},{4,6},{5,7},{6,4},{7,5},{8,10},{9,11},{10,... | collective-permute-start | bytes 196616 | tf_op jit(solution)/shard_map/ppermute | solution.py:50
  189.2 18.2 %collective-permute-start.42 = (bf16[2,128,128]{2,1,0:T(8,128)(2,1)S(1)}, bf16[2,128,128]{2,1,0:T(8,128)(2,1)S(1)}, u32[]{:S(2)}, u32[]{:S(2)}) collective-permute-start(bf16[2,128,128]{2,1,0:T(8,128)(2,1)S(1)} %get-tuple-element.205), channel_id=1, source_target_pairs={{0,3},{1,2},{2,1},{3,0},{4,7},{5,6},{6,5},{7,4},{8,11},{9,10},{10,... | collective-permute-start | bytes 196616 | tf_op jit(solution)/shard_map/ppermute | solution.py:50
  190.4 30.3 %collective-permute-start.36 = (bf16[1,1024,128]{2,1,0:T(8,128)(2,1)S(1)}, bf16[1,1024,128]{2,1,0:T(8,128)(2,1)S(1)}, u32[]{:S(2)}, u32[]{:S(2)}) collective-permute-start(bf16[1,1024,128]{2,1,0:T(8,128)(2,1)S(1)} %get-tuple-element.183), channel_id=1, source_target_pairs={{0,4},{1,5},{2,6},{3,7},{4,0},{5,1},{6,2},{7,3},{8,12},{9,13},{10,... | collective-permute-start | bytes 786440 | tf_op jit(solution)/shard_map/ppermute | solution.py:50
  192.8 27.6 %collective-permute-start.38 = (bf16[1024,128]{1,0:T(8,128)(2,1)S(1)}, bf16[1024,128]{1,0:T(8,128)(2,1)S(1)}, u32[]{:S(2)}, u32[]{:S(2)}) collective-permute-start(bf16[1024,128]{1,0:T(8,128)(2,1)S(1)} %get-tuple-element.186.refs_0_), channel_id=1, source_target_pairs={{0,16},{8,24},{16,0},{24,8},{1,17},{9,25},{17,1},{25,9},{2,18},{10... | collective-permute-start | bytes 786440 | tf_op jit(solution)/shard_map/ppermute | solution.py:50
  206.2 38.3 %collective-permute-start.37 = (bf16[1024,128]{1,0:T(8,128)(2,1)S(1)}, bf16[1024,128]{1,0:T(8,128)(2,1)S(1)}, u32[]{:S(2)}, u32[]{:S(2)}) collective-permute-start(bf16[1024,128]{1,0:T(8,128)(2,1)S(1)} %get-tuple-element.186.refs_0_), channel_id=1, source_target_pairs={{0,8},{8,0},{16,24},{24,16},{1,9},{9,1},{17,25},{25,17},{2,10},{10... | collective-permute-start | bytes 786440 | tf_op jit(solution)/shard_map/ppermute | solution.py:50
  208.3 37.8 %collective-permute-start.44 = (bf16[4,2,128,128]{3,2,1,0:T(8,128)(2,1)S(1)}, bf16[4,2,128,128]{3,2,1,0:T(8,128)(2,1)S(1)}, u32[]{:S(2)}, u32[]{:S(2)}) collective-permute-start(bf16[4,2,128,128]{3,2,1,0:T(8,128)(2,1)S(1)} %pad_maximum_fusion.2.refs_4_), channel_id=1, source_target_pairs={{0,16},{8,24},{16,0},{24,8},{1,17},{9,25},{17,1},{25,9},{2,18},{10... | collective-permute-start | bytes 786440 | tf_op jit(solution)/shard_map/ppermute | solution.py:50
  230.8 15.8 %collective-permute-start.45 = (bf16[4,2,128,128]{3,2,1,0:T(8,128)(2,1)S(1)}, bf16[4,2,128,128]{3,2,1,0:T(8,128)(2,1)S(1)}, u32[]{:S(2)}, u32[]{:S(2)}) collective-permute-start(bf16[4,2,128,128]{3,2,1,0:T(8,128)(2,1)S(1)} %collective-permute-done.43.refs_5_), channel_id=1, source_target_pairs={{0,16},{8,24},{16,0},{24,8},{1,17},{9,25},{17,1},{25,9},{2,18},{10... | collective-permute-start | bytes 786440 | tf_op jit(solution)/shard_map/ppermute | solution.py:50
  246.6 19.7 %collective-permute-start.57 = (bf16[32,1280]{1,0:T(8,128)(2,1)S(1)}, bf16[32,1280]{1,0:T(8,128)(2,1)S(1)}, u32[]{:S(2)}, u32[]{:S(2)}) collective-permute-start(bf16[32,1280]{1,0:T(8,128)(2,1)S(1)} %fusion.5.refs_0_), channel_id=1, source_target_pairs={{0,16},{8,24},{16,0},{24,8},{1,17},{9,25},{17,1},{25,9},{2,18},{10... | collective-permute-start | bytes 245768 | tf_op jit(solution)/shard_map/ppermute | solution.py:50
  (71 other events, 552.2 us)

commit v2 on v1

--- a/solution.py
+++ b/solution.py
@@ -1328,19 +1328,20 @@
     g1 = (g1_keep, g1_got, swap(g1_sum, "sec", chip))
     hold(scalars, g1_sum, *[terms[2] for terms in att_terms])
     att_kept, send = pick_team(s, scalars, *att_terms, 1)
-    att_swapped = swap(send, "sec", s.members)
+    att_swapped = swap(after([send], g1[2])[0], "sec", s.members)
     *crossed, downs = pick_member(s, scalars, mlp_kept, mlp_swapped)
-    ups = cross(s, crossed)
+    crossed = [crossed[0]] + [swap(crossed[j], "sec", j) for j in range(1, s.members)]
     downs = [downs, swap(downs, "grp", 1), swap(downs, "grp", 2)]
-    ups = [ups, swap(ups, "grp", 1), swap(ups, "grp", 2)]
     keep, send, *edges = embed_back(
         s, scalars, g1, own, stats, hidden0, gain1, w_embed, in_cat, head_home, head_part, gain2_grad, bias_grad
     )
     edges = edges[:1] + [swap(edges[j], "grp", j) for j in range(1, s.group)]
     home_got = swap(send, "sec", core)
+    ups = jnp.stack(after(crossed, edges[0]))
+    ups = [ups, swap(ups, "grp", 1), swap(ups, "grp", 2)]
     mlp_parts = (
         downs + [swap(after(downs[2:], edges[0])[0], "grp", 1)],
-        ups + [swap(after(ups[1:2], edges[0])[0], "grp", 2)],
+        ups + [swap(ups[1], "grp", 2)],
     )
     crossed = pick_member(s, scalars, att_kept, att_swapped)
     att_parts = all_of_group(cross(s, crossed), True)

time: 272 us -> 266 us (0.978)
  waiting for transfers between devices: 61.5 us -> 56.9 us
    ppermute x59, waiting for transfers between devices: 61.5 us -> 56.9 us  [swap(): return lax.ppermute(x, axis, [(i, i ^ bit) for i in range(n)])]
    unnamed x74 -> x72, local copies, waits for them, and re-layouts: 14.1 us -> 14.1 us
  transfers between devices with their start and end apart: 59 -> 59, of which waited for: 22 -> 22; matrix products, arithmetic and copies ran while one was open for 2% -> 3% of each run, Pallas kernels for 47% -> 48%
where the time goes in v2:
time: 266 us
  Pallas kernels  130 us (49%)
  waiting for transfers between devices  56.9 us (21%)
  starting transfers between devices  53.1 us (20%)
  local copies, waits for them, and re-layouts  17.9 us (7%)
  other arithmetic  5.46 us (2%)
    pallas_call x22, Pallas kernels, kernel(): pl.pallas_call(body, grid_spec=pltpu.PrefetchScalarGridSpec(num_scalar_pr...  130 us
    ppermute x59, waiting for transfers between devices, swap(): return lax.ppermute(x, axis, [(i, i ^ bit) for i in range(n)])  56.9 us
    ppermute x59, starting transfers between devices, swap(): return lax.ppermute(x, axis, [(i, i ^ bit) for i in range(n)])  53.1 us
    unnamed x72, local copies, waits for them, and re-layouts  14.1 us
  transfers between devices with their start and end apart: 59, of which 22 were waited for; matrix products, arithmetic and copies ran while one was open for 3% of the time, Pallas kernels for 48%

profile of v2, /device:TPU:0, one launch (start us, length us, event | category | flops | bytes accessed | tf_op | source)
XLA Modules:
  0.0 265.8 jit_solution(11807323841924436071)
XLA Ops:
  1.9 4.1 %collective-permute-start = (bf16[128,192]{1,0:T(8,128)(2,1)S(1)}, bf16[128,192]{1,0:T(8,128)(2,1)S(1)}, u32[]{:S(2)}, u32[]{:S(2)}) collective-permute-start(bf16[128,192]{1,0:T(8,128)(2,1)S(1)} %select_n.119), channel_id=1, source_target_pairs={{0,4},{1,5},{2,6},{3,7},{4,0},{5,1},{6,2},{7,3},{8,12},{9,13},{10,... | collective-permute-start | bytes 147464 | tf_op jit(solution)/shard_map/ppermute | solution.py:50
  18.2 8.6 %embed_qkv.1 = (bf16[1024,576]{1,0:T(8,128)(2,1)S(1)}, f32[1024,1024]{1,0:T(8,128)}, bf16[1024,1024]{1,0:T(8,128)(2,1)}, bf16[1024,768]{1,0:T(8,128)(2,1)S(1)}, f32[1024,128]{1,0:T(8,128)S(1)}) custom-call(s32[4]{0:T(128)S(1)} %pad_add_fusion.sc, bf16[2,128,192]{2,1,0:T(8,128)(2,1)S(1)} %pad_maximum_fusion.4.refs_0_, ...), custom_call_target="tpu_custom_call" | custom-call | flops 11040000000 | bytes 34560000 | tf_op jit(solution)/shard_map/embed_qkv/pallas_call | solution.py:62
  27.8 6.8 %attention_fwd.2 = (bf16[512,256]{1,0:T(8,128)(2,1)S(1)}, bf16[4,2,1024,256]{3,2,1,0:T(8,128)(2,1)}, f32[512,128]{1,0:T(8,128)S(1)}) custom-call(s32[4]{0:T(128)S(1)} %pad_add_fusion.sc, bf16[1024,768]{1,0:T(8,128)(2,1)S(1)} %get-tuple-element.123.q_ref.kv_ref.refs_0_.refs_1_.qkv_ref, ...), custom_call_target="tpu_custom_call" | custom-call | flops 10579999744 | bytes 33120000 | tf_op jit(solution)/shard_map/attention_fwd/pallas_call | solution.py:62
  36.4 6.8 %attention_fwd.3 = (bf16[512,256]{1,0:T(8,128)(2,1)S(1)}, bf16[4,2,1024,256]{3,2,1,0:T(8,128)(2,1)}, f32[512,128]{1,0:T(8,128)S(1)}) custom-call(s32[4]{0:T(128)S(1)} %pad_add_fusion.sc, bf16[1024,768]{1,0:T(8,128)(2,1)S(1)} %get-tuple-element.123.q_ref.kv_ref.refs_0_.refs_1_.qkv_ref, ...), custom_call_target="tpu_custom_call" | custom-call | flops 10579999744 | bytes 33120000 | tf_op jit(solution)/shard_map/attention_fwd/pallas_call | solution.py:62
  52.7 15.1 %mlp.3 = (bf16[512,1024]{1,0:T(8,128)(2,1)S(1)}, bf16[512,1024]{1,0:T(8,128)(2,1)S(1)}, bf16[512,1024]{1,0:T(8,128)(2,1)S(1)}, bf16[512,1024]{1,0:T(8,128)(2,1)}...) custom-call(s32[4]{0:T(128)S(1)} %pad_add_fusion.sc, ...), custom_call_target="tpu_custom_call" | custom-call | flops 19549999104 | bytes 61200000 | tf_op jit(solution)/shard_map/mlp/pallas_call | solution.py:62
  71.6 15.4 %mlp.2 = (bf16[512,1024]{1,0:T(8,128)(2,1)S(1)}, bf16[512,1024]{1,0:T(8,128)(2,1)S(1)}, bf16[512,1024]{1,0:T(8,128)(2,1)S(1)}, bf16[512,1024]{1,0:T(8,128)(2,1)}...) custom-call(s32[4]{0:T(128)S(1)} %pad_add_fusion.sc, ...), custom_call_target="tpu_custom_call" | custom-call | flops 19549999104 | bytes 61200000 | tf_op jit(solution)/shard_map/mlp/pallas_call | solution.py:62
  90.1 5.4 %trunk_part.1 = (bf16[2,2,528,256]{3,2,1,0:T(8,128)(2,1)S(1)}, bf16[2,2,528,256]{3,2,1,0:T(8,128)(2,1)S(1)}) custom-call(s32[4]{0:T(128)S(1)} %pad_add_fusion.sc, bf16[512,1024]{1,0:T(8,128)(2,1)S(1)} %get-tuple-element.137.act0.an, f32[1,1024]{1,0:T(1,128)S(1)} %get-tuple-element.138.gs0, bf16[512,1024]{1,0:T(8,128)(2,1)S(1)} %get-tuple-element.140.act1.af, ...), custom_call_target="tpu_custom_call" | custom-call | flops 4600000000 | bytes 14400000 | tf_op jit(solution)/shard_map/trunk_part/pallas_call | solution.py:62
  99.2 10.4 %mlp_weight_grads.1 = (bf16[2,2,1024,128]{3,2,1,0:T(8,128)(2,1)S(1)}, bf16[2,2,1024,128]{3,2,1,0:T(8,128)(2,1)S(1)}, bf16[2,2,1024,128]{3,2,1,0:T(8,128)(2,1)S(1)}, bf16[2,2,1024,128]{3,2,1,0:T(8,128)(2,1)S(1)}) custom-call(s32[4]{0:T(128)S(1)} %pad_add_fusion.sc, bf16[512,1024]{1,0:T(8,128)(2,1)S(1)} %get-tuple-element.137.act0.an, ...), custom_call_target="tpu_custom_call" | custom-call | flops 13224999936 | bytes 41400000 | tf_op jit(solution)/shard_map/mlp_weight_grads/pallas_call | solution.py:62
  113.0 10.4 %attention_bwd.2 = (bf16[1024,256]{1,0:T(8,128)(2,1)S(1)}, bf16[1024,256]{1,0:T(8,128)(2,1)S(1)}, f32[1024,512]{1,0:T(8,128)}) custom-call(s32[4]{0:T(128)S(1)} %pad_add_fusion.sc, bf16[1024,768]{1,0:T(8,128)(2,1)S(1)} %copy-done.8, bf16[1024,768]{1,0:T(8,128)(2,1)S(1)} %copy-done.8, bf16[512,256]{1,0:T(8,128)(2,1)S(1)} %get-tuple-element.128.refs_0_.refs_2_, ...), custom_call_target="tpu_custom_call" | custom-call | flops 15294999552 | bytes 47880000 | tf_op jit(solution)/shard_map/attention_bwd/pallas_call | solution.py:62
  125.8 9.5 %collective-permute-done.21.refs_4_ = bf16[2,2,1024,128]{3,2,1,0:T(8,128)(2,1)} collective-permute-done((bf16[2,2,1024,128]{3,2,1,0:T(8,128)(2,1)S(1)}, bf16[2,2,1024,128]{3,2,1,0:T(8,128)(2,1)}, u32[]{:S(2)}, u32[]{:S(2)}) %collective-permute-start.21) | collective-permute-done | bytes 1048608 | tf_op jit(solution)/shard_map/ppermute | solution.py:50
  139.9 9.9 %attention_bwd.3 = (bf16[1024,256]{1,0:T(8,128)(2,1)S(1)}, bf16[1024,256]{1,0:T(8,128)(2,1)S(1)}, bf16[1024,512]{1,0:T(8,128)(2,1)S(1)}) custom-call(s32[4]{0:T(128)S(1)} %pad_add_fusion.sc, bf16[1024,768]{1,0:T(8,128)(2,1)S(1)} %copy-done.8, bf16[1024,768]{1,0:T(8,128)(2,1)S(1)} %copy-done.8, ...), custom_call_target="tpu_custom_call", output_to_operand_aliasing={{0}: (9, {}), {1}: (10, {})} | custom-call | flops 15294999552 | bytes 47880000 | tf_op jit(solution)/shard_map/attention_bwd/pallas_call | solution.py:62
  152.9 5.4 %attention_weight_grads.1 = (bf16[2,1024,128]{2,1,0:T(8,128)(2,1)S(1)}, bf16[2,1024,128]{2,1,0:T(8,128)(2,1)S(1)}, bf16[2,1024,128]{2,1,0:T(8,128)(2,1)S(1)}, bf16[2,1024,128]{2,1,0:T(8,128)(2,1)S(1)}) custom-call(s32[4]{0:T(128)S(1)} %pad_add_fusion.sc, bf16[1024,1024]{1,0:T(8,128)(2,1)} %get-tuple-element.166.n1, ...), custom_call_target="tpu_custom_call" | custom-call | flops 10350000128 | bytes 32400000 | tf_op jit(solution)/shard_map/attention_weight_grads/pallas_call | solution.py:62
  162.9 3.3 %collective-permute-start.31 = (bf16[2,1024,128]{2,1,0:T(8,128)(2,1)S(1)}, bf16[2,1024,128]{2,1,0:T(8,128)(2,1)S(1)}, u32[]{:S(2)}, u32[]{:S(2)}) collective-permute-start(bf16[2,1024,128]{2,1,0:T(8,128)(2,1)S(1)} %get-tuple-element.173), channel_id=1, source_target_pairs={{0,4},{1,5},{2,6},{3,7},{4,0},{5,1},{6,2},{7,3},{8,12},{9,13},{10,... | collective-permute-start | bytes 1572872 | tf_op jit(solution)/shard_map/ppermute | solution.py:50
  168.1 5.6 %norm_one_grad.1 = (bf16[2,1040,256]{2,1,0:T(8,128)(2,1)S(1)}, bf16[2,1040,256]{2,1,0:T(8,128)(2,1)S(1)}) custom-call(s32[4]{0:T(128)S(1)} %pad_add_fusion.sc, bf16[1024,768]{1,0:T(8,128)(2,1)S(1)} %copy-done.9, bf16[1024,256]{1,0:T(8,128)(2,1)S(1)} %copy-done.30, bf16[1024,512]{1,0:T(8,128)(2,1)S(1)} %copy-done.13, bf16[1024,3072]{1,0:T(8,128)(2,1)} %wv.1, ...), custom_call_target="tpu_custom_call" | custom-call | flops 13454999552 | bytes 42120000 | tf_op jit(solution)/shard_map/norm_one_grad/pallas_call | solution.py:62
  175.5 3.2 %collective-permute-done.24.refs_1_ = bf16[2,1024,128]{2,1,0:T(8,128)(2,1)S(1)} collective-permute-done((bf16[2,1024,128]{2,1,0:T(8,128)(2,1)S(1)}, bf16[2,1024,128]{2,1,0:T(8,128)(2,1)S(1)}, u32[]{:S(2)}, u32[]{:S(2)}) %collective-permute-start.24) | collective-permute-done | bytes 524320 | tf_op jit(solution)/shard_map/ppermute | solution.py:50
  179.3 4.2 %trunk_head.1 = (bf16[8,128,192]{2,1,0:T(8,128)(2,1)S(1)}, f32[256,576]{1,0:T(8,128)S(1)}, f32[8,256]{1,0:T(8,128)S(1)}) custom-call(s32[4]{0:T(128)S(1)} %pad_add_fusion.sc, f32[512,256]{1,0:T(8,128)S(1)} %copy-done.24, f32[512,256]{1,0:T(8,128)S(1)} %copy-done.22, bf16[2,2,528,256]{3,2,1,0:T(8,128)(2,1)S(1)} %get-tuple-element.179.a, ...), custom_call_target="tpu_custom_call" | custom-call | flops 8049999872 | bytes 25200000 | tf_op jit(solution)/shard_map/trunk_head/pallas_call | solution.py:62
  191.9 8.0 %collective-permute-done.32.refs_2_ = bf16[1,1040,256]{2,1,0:T(8,128)(2,1)S(1)} collective-permute-done((bf16[1,1040,256]{2,1,0:T(8,128)(2,1)S(1)}, bf16[1,1040,256]{2,1,0:T(8,128)(2,1)S(1)}, u32[]{:S(2)}, u32[]{:S(2)}) %collective-permute-start.32) | collective-permute-done | bytes 532512 | tf_op jit(solution)/shard_map/ppermute | solution.py:50
  199.9 6.1 %embed_back.1 = (bf16[2,2,2,128,192]{4,3,2,1,0:T(8,128)(2,1)S(1)}, bf16[2,2,2,128,192]{4,3,2,1,0:T(8,128)(2,1)S(1)}, bf16[2,32,1280]{2,1,0:T(8,128)(2,1)S(1)}, b...) custom-call(s32[4]{0:T(128)S(1)} %pad_add_fusion.sc, ...), custom_call_target="tpu_custom_call" | custom-call | flops 10350000128 | bytes 32400000 | tf_op jit(solution)/shard_map/embed_back/pallas_call | solution.py:62
  213.4 3.4 %collective-permute-done.54 = bf16[2,32,1280]{2,1,0:T(8,128)(2,1)S(1)} collective-permute-done((bf16[2,32,1280]{2,1,0:T(8,128)(2,1)S(1)}, bf16[2,32,1280]{2,1,0:T(8,128)(2,1)S(1)}, u32[]{:S(2)}, u32[]{:S(2)}) %collective-permute-start.54) | collective-permute-done | bytes 163872 | tf_op jit(solution)/shard_map/ppermute | solution.py:50
  217.7 6.8 %collective-permute-done.36.g_ref = bf16[1,1024,128]{2,1,0:T(8,128)(2,1)S(1)} collective-permute-done((bf16[1,1024,128]{2,1,0:T(8,128)(2,1)S(1)}, bf16[1,1024,128]{2,1,0:T(8,128)(2,1)S(1)}, u32[]{:S(2)}, u32[]{:S(2)}) %collective-permute-start.36) | collective-permute-done | bytes 262176 | tf_op jit(solution)/shard_map/ppermute | solution.py:50
  232.8 3.9 %collective-permute-done.34 = bf16[2,2,128,192]{3,2,1,0:T(8,128)(2,1)S(1)} collective-permute-done((bf16[2,2,128,192]{3,2,1,0:T(8,128)(2,1)S(1)}, bf16[2,2,128,192]{3,2,1,0:T(8,128)(2,1)S(1)}, u32[]{:S(2)}, u32[]{:S(2)}) %collective-permute-start.34) | collective-permute-done | bytes 196640 | tf_op jit(solution)/shard_map/ppermute | solution.py:50
  239.0 4.3 %collective-permute-done.56.refs_1_ = bf16[32,1280]{1,0:T(8,128)(2,1)S(1)} collective-permute-done((bf16[32,1280]{1,0:T(8,128)(2,1)S(1)}, bf16[32,1280]{1,0:T(8,128)(2,1)S(1)}, u32[]{:S(2)}, u32[]{:S(2)}) %collective-permute-start.56) | collective-permute-done | bytes 81952 | tf_op jit(solution)/shard_map/ppermute | solution.py:50
  248.6 4.4 %mlp_grads_out.1 = (f32[512,1024]{1,0:T(8,128)}, f32[128,4096]{1,0:T(8,128)}) custom-call(s32[4]{0:T(128)S(1)} %pad_add_fusion.sc, bf16[1024,128]{1,0:T(8,128)(2,1)S(1)} %get-tuple-element.190.refs_0_, bf16[1024,128]{1,0:T(8,128)(2,1)S(1)} %collective-permute-done.37.refs_1_, bf16[1024,128]{1,0:T(8,128)(2,1)S(1)} %collective-permute-done.38.refs_2_, ...), custom_call_target="tpu_custom_call" | custom-call | flops 5405000192 | bytes 16920000 | tf_op jit(solution)/shard_map/mlp_grads_out/pallas_call | solution.py:62
  259.4 3.7 %attention_grads_out.1 = (f32[128,3072]{1,0:T(8,128)}, f32[128,1024]{1,0:T(8,128)}) custom-call(s32[4]{0:T(128)S(1)} %pad_add_fusion.sc, bf16[4,2,128,128]{3,2,1,0:T(8,128)(2,1)S(1)} %pad_maximum_fusion.3.refs_0_, bf16[4,2,128,128]{3,2,1,0:T(8,128)(2,1)S(1)} %collective-permute-done.49.refs_1_, bf16[4,2,128,128]{3,2,1,0:T(8,128)(2,1)S(1)} %collective-permute-done.50.refs_2_, ...), custom_call_target="tpu_custom_call" | custom-call | flops 4024999936 | bytes 12600000 | tf_op jit(solution)/shard_map/attention_grads_out/pallas_call | solution.py:62
  (227 shorter events, 98.5 us)
Async XLA Ops:
  13.1 31.3 %collective-permute-start.9 = (bf16[2,128,192]{2,1,0:T(8,128)(2,1)S(1)}, bf16[2,128,192]{2,1,0:T(8,128)(2,1)S(1)}, u32[]{:S(2)}, u32[]{:S(2)}) collective-permute-start(bf16[2,128,192]{2,1,0:T(8,128)(2,1)S(1)} %pad_maximum_fusion.5.refs_0_), channel_id=1, source_target_pairs={{0,1},{1,0},{2,3},{3,2},{4,5},{5,4},{6,7},{7,6},{8,9},{9,8},{10,11... | collective-permute-start | bytes 294920 | tf_op jit(solution)/shard_map/ppermute | solution.py:50
  18.2 26.7 %collective-permute-start.11 = (bf16[2,128,192]{2,1,0:T(8,128)(2,1)S(1)}, bf16[2,128,192]{2,1,0:T(8,128)(2,1)S(1)}, u32[]{:S(2)}, u32[]{:S(2)}) collective-permute-start(bf16[2,128,192]{2,1,0:T(8,128)(2,1)S(1)} %collective-permute-done.10.refs_2_), channel_id=1, source_target_pairs={{0,1},{1,0},{2,3},{3,2},{4,5},{5,4},{6,7},{7,6},{8,9},{9,8},{10,11... | collective-permute-start | bytes 294920 | tf_op jit(solution)/shard_map/ppermute | solution.py:50
  44.4 27.2 %collective-permute-start.5 = (bf16[512,256]{1,0:T(8,128)(2,1)S(1)}, bf16[512,256]{1,0:T(8,128)(2,1)S(1)}, u32[]{:S(2)}, u32[]{:S(2)}) collective-permute-start(bf16[512,256]{1,0:T(8,128)(2,1)S(1)} %get-tuple-element.128.refs_0_.refs_2_), channel_id=1, source_target_pairs={{0,1},{1,0},{2,3},{3,2},{4,5},{5,4},{6,7},{7,6},{8,9},{9,8},{10,11... | collective-permute-start | bytes 786440 | tf_op jit(solution)/shard_map/ppermute | solution.py:50
  52.6 19.0 %collective-permute-start.6 = (bf16[512,256]{1,0:T(8,128)(2,1)S(1)}, bf16[512,256]{1,0:T(8,128)(2,1)S(1)}, u32[]{:S(2)}, u32[]{:S(2)}) collective-permute-start(bf16[512,256]{1,0:T(8,128)(2,1)S(1)} %collective-permute-done.4.refs_2_), channel_id=1, source_target_pairs={{0,1},{1,0},{2,3},{3,2},{4,5},{5,4},{6,7},{7,6},{8,9},{9,8},{10,11... | collective-permute-start | bytes 786440 | tf_op jit(solution)/shard_map/ppermute | solution.py:50
  69.8 26.1 %collective-permute-start.15 = (bf16[256,1024]{1,0:T(8,128)(2,1)S(1)}, bf16[256,1024]{1,0:T(8,128)(2,1)S(1)}, u32[]{:S(2)}, u32[]{:S(2)}) collective-permute-start(bf16[256,1024]{1,0:T(8,128)(2,1)S(1)} %get-tuple-element.146), channel_id=1, source_target_pairs={{0,2},{1,3},{2,0},{3,1},{4,6},{5,7},{6,4},{7,5},{8,10},{9,11},{10,... | collective-permute-start | bytes 1572872 | tf_op jit(solution)/shard_map/ppermute | solution.py:50
  70.1 25.8 %collective-permute-start.16 = (bf16[256,1024]{1,0:T(8,128)(2,1)S(1)}, bf16[256,1024]{1,0:T(8,128)(2,1)S(1)}, u32[]{:S(2)}, u32[]{:S(2)}) collective-permute-start(bf16[256,1024]{1,0:T(8,128)(2,1)S(1)} %get-tuple-element.147), channel_id=1, source_target_pairs={{0,3},{1,2},{2,1},{3,0},{4,7},{5,6},{6,5},{7,4},{8,11},{9,10},{10,... | collective-permute-start | bytes 1572872 | tf_op jit(solution)/shard_map/ppermute | solution.py:50
  95.6 27.8 %collective-permute-start.26 = (bf16[2,2,528,256]{3,2,1,0:T(8,128)(2,1)S(1)}, bf16[2,2,528,256]{3,2,1,0:T(8,128)(2,1)S(1)}, u32[]{:S(2)}, u32[]{:S(2)}) collective-permute-start(bf16[2,2,528,256]{3,2,1,0:T(8,128)(2,1)S(1)} %get-tuple-element.142), channel_id=1, source_target_pairs={{0,1},{1,0},{2,3},{3,2},{4,5},{5,4},{6,7},{7,6},{8,9},{9,8},{10,11... | collective-permute-start | bytes 3244040 | tf_op jit(solution)/shard_map/ppermute | solution.py:50
  98.8 14.2 %collective-permute-start.17 = (bf16[256,1024]{1,0:T(8,128)(2,1)S(1)}, bf16[256,1024]{1,0:T(8,128)(2,1)S(1)}, u32[]{:S(2)}, u32[]{:S(2)}) collective-permute-start(bf16[256,1024]{1,0:T(8,128)(2,1)S(1)} %norm_two_back.1.refs_5_), channel_id=1, source_target_pairs={{0,2},{1,3},{2,0},{3,1},{4,6},{5,7},{6,4},{7,5},{8,10},{9,11},{10,... | collective-permute-start | bytes 1572872 | tf_op jit(solution)/shard_map/ppermute | solution.py:50
  109.6 25.7 %collective-permute-start.21 = (bf16[2,2,1024,128]{3,2,1,0:T(8,128)(2,1)S(1)}, bf16[2,2,1024,128]{3,2,1,0:T(8,128)(2,1)}, u32[]{:S(2)}, u32[]{:S(2)}) collective-permute-start(bf16[2,2,1024,128]{3,2,1,0:T(8,128)(2,1)S(1)} %get-tuple-element.153), channel_id=1, source_target_pairs={{0,16},{8,24},{16,0},{24,8},{1,17},{9,25},{17,1},{25,9},{2,18},{10... | collective-permute-start | bytes 3145736 | tf_op jit(solution)/shard_map/ppermute | solution.py:50
  111.2 26.9 %collective-permute-start.20 = (bf16[2,2,1024,128]{3,2,1,0:T(8,128)(2,1)S(1)}, bf16[2,2,1024,128]{3,2,1,0:T(8,128)(2,1)S(1)}, u32[]{:S(2)}, u32[]{:S(2)}) collective-permute-start(bf16[2,2,1024,128]{3,2,1,0:T(8,128)(2,1)S(1)} %get-tuple-element.158), channel_id=1, source_target_pairs={{0,8},{8,0},{16,24},{24,16},{1,9},{9,1},{17,25},{25,17},{2,10},{10... | collective-permute-start | bytes 3145736 | tf_op jit(solution)/shard_map/ppermute | solution.py:50
  113.0 27.0 %collective-permute-start.19 = (bf16[256,1024]{1,0:T(8,128)(2,1)S(1)}, bf16[256,1024]{1,0:T(8,128)(2,1)S(1)}, u32[]{:S(2)}, u32[]{:S(2)}) collective-permute-start(bf16[256,1024]{1,0:T(8,128)(2,1)S(1)} %collective-permute-done.17.refs_5_), channel_id=1, source_target_pairs={{0,1},{1,0},{2,3},{3,2},{4,5},{5,4},{6,7},{7,6},{8,9},{9,8},{10,11... | collective-permute-start | bytes 1572872 | tf_op jit(solution)/shard_map/ppermute | solution.py:50
  124.4 55.0 %collective-permute-start.27 = (bf16[1,2,528,256]{3,2,1,0:T(8,128)(2,1)}, bf16[1,2,528,256]{3,2,1,0:T(8,128)(2,1)S(1)}, u32[]{:S(2)}, u32[]{:S(2)}) collective-permute-start(bf16[1,2,528,256]{3,2,1,0:T(8,128)(2,1)} %add_convert_fusion), channel_id=1, source_target_pairs={{0,2},{1,3},{2,0},{3,1},{4,6},{5,7},{6,4},{7,5},{8,10},{9,11},{10,... | collective-permute-start | bytes 1622024 | tf_op jit(solution)/shard_map/ppermute | solution.py:50
  158.3 15.5 %collective-permute-start.25 = (bf16[2,1024,128]{2,1,0:T(8,128)(2,1)S(1)}, bf16[2,1024,128]{2,1,0:T(8,128)(2,1)S(1)}, u32[]{:S(2)}, u32[]{:S(2)}) collective-permute-start(bf16[2,1024,128]{2,1,0:T(8,128)(2,1)S(1)} %get-tuple-element.171), channel_id=1, source_target_pairs={{0,16},{8,24},{16,0},{24,8},{1,17},{9,25},{17,1},{25,9},{2,18},{10... | collective-permute-start | bytes 1572872 | tf_op jit(solution)/shard_map/ppermute | solution.py:50
  162.9 24.9 %collective-permute-start.31 = (bf16[2,1024,128]{2,1,0:T(8,128)(2,1)S(1)}, bf16[2,1024,128]{2,1,0:T(8,128)(2,1)S(1)}, u32[]{:S(2)}, u32[]{:S(2)}) collective-permute-start(bf16[2,1024,128]{2,1,0:T(8,128)(2,1)S(1)} %get-tuple-element.173), channel_id=1, source_target_pairs={{0,4},{1,5},{2,6},{3,7},{4,0},{5,1},{6,2},{7,3},{8,12},{9,13},{10,... | collective-permute-start | bytes 1572872 | tf_op jit(solution)/shard_map/ppermute | solution.py:50
  184.8 15.1 %collective-permute-start.32 = (bf16[1,1040,256]{2,1,0:T(8,128)(2,1)S(1)}, bf16[1,1040,256]{2,1,0:T(8,128)(2,1)S(1)}, u32[]{:S(2)}, u32[]{:S(2)}) collective-permute-start(bf16[1,1040,256]{2,1,0:T(8,128)(2,1)S(1)} %add_convert_fusion.1), channel_id=1, source_target_pairs={{0,2},{1,3},{2,0},{3,1},{4,6},{5,7},{6,4},{7,5},{8,10},{9,11},{10,... | collective-permute-start | bytes 1597448 | tf_op jit(solution)/shard_map/ppermute | solution.py:50
  188.5 22.0 %collective-permute-start.38 = (bf16[1024,128]{1,0:T(8,128)(2,1)S(1)}, bf16[1024,128]{1,0:T(8,128)(2,1)S(1)}, u32[]{:S(2)}, u32[]{:S(2)}) collective-permute-start(bf16[1024,128]{1,0:T(8,128)(2,1)S(1)} %get-tuple-element.190.refs_0_), channel_id=1, source_target_pairs={{0,16},{8,24},{16,0},{24,8},{1,17},{9,25},{17,1},{25,9},{2,18},{10... | collective-permute-start | bytes 786440 | tf_op jit(solution)/shard_map/ppermute | solution.py:50
  190.1 16.0 %collective-permute-start.40 = (bf16[2,128,128]{2,1,0:T(8,128)(2,1)S(1)}, bf16[2,128,128]{2,1,0:T(8,128)(2,1)S(1)}, u32[]{:S(2)}, u32[]{:S(2)}) collective-permute-start(bf16[2,128,128]{2,1,0:T(8,128)(2,1)S(1)} %get-tuple-element.208), channel_id=1, source_target_pairs={{0,1},{1,0},{2,3},{3,2},{4,5},{5,4},{6,7},{7,6},{8,9},{9,8},{10,11... | collective-permute-start | bytes 196616 | tf_op jit(solution)/shard_map/ppermute | solution.py:50
  190.1 17.3 %collective-permute-start.41 = (bf16[2,128,128]{2,1,0:T(8,128)(2,1)S(1)}, bf16[2,128,128]{2,1,0:T(8,128)(2,1)S(1)}, u32[]{:S(2)}, u32[]{:S(2)}) collective-permute-start(bf16[2,128,128]{2,1,0:T(8,128)(2,1)S(1)} %get-tuple-element.209), channel_id=1, source_target_pairs={{0,2},{1,3},{2,0},{3,1},{4,6},{5,7},{6,4},{7,5},{8,10},{9,11},{10,... | collective-permute-start | bytes 196616 | tf_op jit(solution)/shard_map/ppermute | solution.py:50
  190.2 19.4 %collective-permute-start.42 = (bf16[2,128,128]{2,1,0:T(8,128)(2,1)S(1)}, bf16[2,128,128]{2,1,0:T(8,128)(2,1)S(1)}, u32[]{:S(2)}, u32[]{:S(2)}) collective-permute-start(bf16[2,128,128]{2,1,0:T(8,128)(2,1)S(1)} %get-tuple-element.210), channel_id=1, source_target_pairs={{0,3},{1,2},{2,1},{3,0},{4,7},{5,6},{6,5},{7,4},{8,11},{9,10},{10,... | collective-permute-start | bytes 196616 | tf_op jit(solution)/shard_map/ppermute | solution.py:50
  209.6 15.0 %collective-permute-start.36 = (bf16[1,1024,128]{2,1,0:T(8,128)(2,1)S(1)}, bf16[1,1024,128]{2,1,0:T(8,128)(2,1)S(1)}, u32[]{:S(2)}, u32[]{:S(2)}) collective-permute-start(bf16[1,1024,128]{2,1,0:T(8,128)(2,1)S(1)} %get-tuple-element.202), channel_id=1, source_target_pairs={{0,4},{1,5},{2,6},{3,7},{4,0},{5,1},{6,2},{7,3},{8,12},{9,13},{10,... | collective-permute-start | bytes 786440 | tf_op jit(solution)/shard_map/ppermute | solution.py:50
  210.5 21.5 %collective-permute-start.43 = (bf16[4,2,128,128]{3,2,1,0:T(8,128)(2,1)S(1)}, bf16[4,2,128,128]{3,2,1,0:T(8,128)(2,1)S(1)}, u32[]{:S(2)}, u32[]{:S(2)}) collective-permute-start(bf16[4,2,128,128]{3,2,1,0:T(8,128)(2,1)S(1)} %pad_maximum_fusion.2.refs_4_), channel_id=1, source_target_pairs={{0,8},{8,0},{16,24},{24,16},{1,9},{9,1},{17,25},{25,17},{2,10},{10... | collective-permute-start | bytes 786440 | tf_op jit(solution)/shard_map/ppermute | solution.py:50
  230.7 14.2 %collective-permute-start.39 = (bf16[1024,128]{1,0:T(8,128)(2,1)S(1)}, bf16[1024,128]{1,0:T(8,128)(2,1)S(1)}, u32[]{:S(2)}, u32[]{:S(2)}) collective-permute-start(bf16[1024,128]{1,0:T(8,128)(2,1)S(1)} %collective-permute-done.38.refs_2_), channel_id=1, source_target_pairs={{0,8},{8,0},{16,24},{24,16},{1,9},{9,1},{17,25},{25,17},{2,10},{10... | collective-permute-start | bytes 786440 | tf_op jit(solution)/shard_map/ppermute | solution.py:50
  237.2 25.8 %collective-permute-start.57 = (bf16[32,1280]{1,0:T(8,128)(2,1)S(1)}, bf16[32,1280]{1,0:T(8,128)(2,1)S(1)}, u32[]{:S(2)}, u32[]{:S(2)}) collective-permute-start(bf16[32,1280]{1,0:T(8,128)(2,1)S(1)} %fusion.5.refs_0_), channel_id=1, source_target_pairs={{0,16},{8,24},{16,0},{24,8},{1,17},{9,25},{17,1},{25,9},{2,18},{10... | collective-permute-start | bytes 245768 | tf_op jit(solution)/shard_map/ppermute | solution.py:50
  243.3 19.8 %collective-permute-start.58 = (bf16[32,1280]{1,0:T(8,128)(2,1)S(1)}, bf16[32,1280]{1,0:T(8,128)(2,1)S(1)}, u32[]{:S(2)}, u32[]{:S(2)}) collective-permute-start(bf16[32,1280]{1,0:T(8,128)(2,1)S(1)} %collective-permute-done.56.refs_1_), channel_id=1, source_target_pairs={{0,16},{8,24},{16,0},{24,8},{1,17},{9,25},{17,1},{25,9},{2,18},{10... | collective-permute-start | bytes 245768 | tf_op jit(solution)/shard_map/ppermute | solution.py:50
  (70 other events, 544.1 us)

commit v3 on v2

--- a/solution.py
+++ b/solution.py
@@ -539,7 +539,7 @@
 
 
 def norm_two_back(s, scalars, parts, hidden1, grad_mlp, gain):
-    chunk = 64
+    chunk = 128
     count = len(parts)
 
     def body(sc, *refs):
@@ -587,6 +587,7 @@
             dq_ref, own_ref, out_ref, gh, acc, keys = refs[11:]
         else:
             dq_ref, own_ref, out_ref, gh, acc, keys = refs[8:]
+            acc = out_ref
         i = pl.program_id(0)
 
         @pl.when(i == 0)
@@ -658,8 +659,6 @@
             if last:
                 out_ref[:, : s.width] = (acc[:, : s.width] * 0.125).astype(BF)
                 out_ref[:, s.width :] = acc[:, s.width :].astype(BF)
-            else:
-                out_ref[...] = acc[...]
 
     member = lambda i, sc: (sc[ME] ^ (base + i), 0)
     side = lambda i, sc: lax.rem(sc[ME] ^ i, s.members // 2)

time: 266 us -> 266 us (level)
  no operation moved by 1% of the time
where the time goes in v3:
time: 266 us; the launch traced here: 265 us
  Pallas kernels  129 us (48%)
  waiting for transfers between devices  57.1 us (21%)
  starting transfers between devices  52.8 us (20%)
  local copies, waits for them, and re-layouts  17.9 us (7%)
  other arithmetic  5.46 us (2%)
    pallas_call x22, Pallas kernels, kernel(): pl.pallas_call(body, grid_spec=pltpu.PrefetchScalarGridSpec(num_scalar_pr...  129 us
    ppermute x59, waiting for transfers between devices, swap(): return lax.ppermute(x, axis, [(i, i ^ bit) for i in range(n)])  57.1 us
    ppermute x59, starting transfers between devices, swap(): return lax.ppermute(x, axis, [(i, i ^ bit) for i in range(n)])  52.8 us
    unnamed x72, local copies, waits for them, and re-layouts  14 us
  transfers between devices with their start and end apart: 59, of which 22 were waited for; matrix products, arithmetic and copies ran while one was open for 3% of the time, Pallas kernels for 48%

profile of v3, /device:TPU:0, one launch (start us, length us, event | category | flops | bytes accessed | tf_op | source)
XLA Modules:
  0.0 265.3 jit_solution(16233204268227613594)
XLA Ops:
  1.9 4.1 %collective-permute-start = (bf16[128,192]{1,0:T(8,128)(2,1)S(1)}, bf16[128,192]{1,0:T(8,128)(2,1)S(1)}, u32[]{:S(2)}, u32[]{:S(2)}) collective-permute-start(bf16[128,192]{1,0:T(8,128)(2,1)S(1)} %select_n.119), channel_id=1, source_target_pairs={{0,4},{1,5},{2,6},{3,7},{4,0},{5,1},{6,2},{7,3},{8,12},{9,13},{10,... | collective-permute-start | bytes 147464 | tf_op jit(solution)/shard_map/ppermute | solution.py:50
  18.2 8.6 %embed_qkv.1 = (bf16[1024,576]{1,0:T(8,128)(2,1)S(1)}, f32[1024,1024]{1,0:T(8,128)}, bf16[1024,1024]{1,0:T(8,128)(2,1)}, bf16[1024,768]{1,0:T(8,128)(2,1)S(1)}, f32[1024,128]{1,0:T(8,128)S(1)}) custom-call(s32[4]{0:T(128)S(1)} %pad_add_fusion.sc, bf16[2,128,192]{2,1,0:T(8,128)(2,1)S(1)} %pad_maximum_fusion.4.refs_0_, ...), custom_call_target="tpu_custom_call" | custom-call | flops 11040000000 | bytes 34560000 | tf_op jit(solution)/shard_map/embed_qkv/pallas_call | solution.py:62
  27.8 6.8 %attention_fwd.2 = (bf16[512,256]{1,0:T(8,128)(2,1)S(1)}, bf16[4,2,1024,256]{3,2,1,0:T(8,128)(2,1)}, f32[512,128]{1,0:T(8,128)S(1)}) custom-call(s32[4]{0:T(128)S(1)} %pad_add_fusion.sc, bf16[1024,768]{1,0:T(8,128)(2,1)S(1)} %get-tuple-element.123.q_ref.kv_ref.refs_0_.refs_1_.qkv_ref, ...), custom_call_target="tpu_custom_call" | custom-call | flops 10579999744 | bytes 33120000 | tf_op jit(solution)/shard_map/attention_fwd/pallas_call | solution.py:62
  36.4 6.8 %attention_fwd.3 = (bf16[512,256]{1,0:T(8,128)(2,1)S(1)}, bf16[4,2,1024,256]{3,2,1,0:T(8,128)(2,1)}, f32[512,128]{1,0:T(8,128)S(1)}) custom-call(s32[4]{0:T(128)S(1)} %pad_add_fusion.sc, bf16[1024,768]{1,0:T(8,128)(2,1)S(1)} %get-tuple-element.123.q_ref.kv_ref.refs_0_.refs_1_.qkv_ref, ...), custom_call_target="tpu_custom_call" | custom-call | flops 10579999744 | bytes 33120000 | tf_op jit(solution)/shard_map/attention_fwd/pallas_call | solution.py:62
  52.7 15.1 %mlp.3 = (bf16[512,1024]{1,0:T(8,128)(2,1)S(1)}, bf16[512,1024]{1,0:T(8,128)(2,1)S(1)}, bf16[512,1024]{1,0:T(8,128)(2,1)S(1)}, bf16[512,1024]{1,0:T(8,128)(2,1)}...) custom-call(s32[4]{0:T(128)S(1)} %pad_add_fusion.sc, ...), custom_call_target="tpu_custom_call" | custom-call | flops 19549999104 | bytes 61200000 | tf_op jit(solution)/shard_map/mlp/pallas_call | solution.py:62
  71.6 15.4 %mlp.2 = (bf16[512,1024]{1,0:T(8,128)(2,1)S(1)}, bf16[512,1024]{1,0:T(8,128)(2,1)S(1)}, bf16[512,1024]{1,0:T(8,128)(2,1)S(1)}, bf16[512,1024]{1,0:T(8,128)(2,1)}...) custom-call(s32[4]{0:T(128)S(1)} %pad_add_fusion.sc, ...), custom_call_target="tpu_custom_call" | custom-call | flops 19549999104 | bytes 61200000 | tf_op jit(solution)/shard_map/mlp/pallas_call | solution.py:62
  90.1 5.4 %trunk_part.1 = (bf16[2,2,528,256]{3,2,1,0:T(8,128)(2,1)S(1)}, bf16[2,2,528,256]{3,2,1,0:T(8,128)(2,1)S(1)}) custom-call(s32[4]{0:T(128)S(1)} %pad_add_fusion.sc, bf16[512,1024]{1,0:T(8,128)(2,1)S(1)} %get-tuple-element.137.act0.an, f32[1,1024]{1,0:T(1,128)S(1)} %get-tuple-element.138.gs0, bf16[512,1024]{1,0:T(8,128)(2,1)S(1)} %get-tuple-element.140.act1.af, ...), custom_call_target="tpu_custom_call" | custom-call | flops 4600000000 | bytes 14400000 | tf_op jit(solution)/shard_map/trunk_part/pallas_call | solution.py:62
  98.9 10.4 %mlp_weight_grads.1 = (bf16[2,2,1024,128]{3,2,1,0:T(8,128)(2,1)S(1)}, bf16[2,2,1024,128]{3,2,1,0:T(8,128)(2,1)S(1)}, bf16[2,2,1024,128]{3,2,1,0:T(8,128)(2,1)S(1)}, bf16[2,2,1024,128]{3,2,1,0:T(8,128)(2,1)S(1)}) custom-call(s32[4]{0:T(128)S(1)} %pad_add_fusion.sc, bf16[512,1024]{1,0:T(8,128)(2,1)S(1)} %get-tuple-element.137.act0.an, ...), custom_call_target="tpu_custom_call" | custom-call | flops 13224999936 | bytes 41400000 | tf_op jit(solution)/shard_map/mlp_weight_grads/pallas_call | solution.py:62
  112.7 10.3 %attention_bwd.2 = (bf16[1024,256]{1,0:T(8,128)(2,1)S(1)}, bf16[1024,256]{1,0:T(8,128)(2,1)S(1)}, f32[1024,512]{1,0:T(8,128)}) custom-call(s32[4]{0:T(128)S(1)} %pad_add_fusion.sc, bf16[1024,768]{1,0:T(8,128)(2,1)S(1)} %copy-done.8, bf16[1024,768]{1,0:T(8,128)(2,1)S(1)} %copy-done.8, bf16[512,256]{1,0:T(8,128)(2,1)S(1)} %get-tuple-element.128.refs_0_.refs_2_, ...), custom_call_target="tpu_custom_call" | custom-call | flops 15294999552 | bytes 47880000 | tf_op jit(solution)/shard_map/attention_bwd/pallas_call | solution.py:62
  125.4 9.7 %collective-permute-done.21.refs_4_ = bf16[2,2,1024,128]{3,2,1,0:T(8,128)(2,1)} collective-permute-done((bf16[2,2,1024,128]{3,2,1,0:T(8,128)(2,1)S(1)}, bf16[2,2,1024,128]{3,2,1,0:T(8,128)(2,1)}, u32[]{:S(2)}, u32[]{:S(2)}) %collective-permute-start.21) | collective-permute-done | bytes 1048608 | tf_op jit(solution)/shard_map/ppermute | solution.py:50
  139.6 9.9 %attention_bwd.3 = (bf16[1024,256]{1,0:T(8,128)(2,1)S(1)}, bf16[1024,256]{1,0:T(8,128)(2,1)S(1)}, bf16[1024,512]{1,0:T(8,128)(2,1)S(1)}) custom-call(s32[4]{0:T(128)S(1)} %pad_add_fusion.sc, bf16[1024,768]{1,0:T(8,128)(2,1)S(1)} %copy-done.8, bf16[1024,768]{1,0:T(8,128)(2,1)S(1)} %copy-done.8, ...), custom_call_target="tpu_custom_call", output_to_operand_aliasing={{0}: (9, {}), {1}: (10, {})} | custom-call | flops 15294999552 | bytes 47880000 | tf_op jit(solution)/shard_map/attention_bwd/pallas_call | solution.py:62
  152.6 5.4 %attention_weight_grads.1 = (bf16[2,1024,128]{2,1,0:T(8,128)(2,1)S(1)}, bf16[2,1024,128]{2,1,0:T(8,128)(2,1)S(1)}, bf16[2,1024,128]{2,1,0:T(8,128)(2,1)S(1)}, bf16[2,1024,128]{2,1,0:T(8,128)(2,1)S(1)}) custom-call(s32[4]{0:T(128)S(1)} %pad_add_fusion.sc, bf16[1024,1024]{1,0:T(8,128)(2,1)} %get-tuple-element.166.n1, ...), custom_call_target="tpu_custom_call" | custom-call | flops 10350000128 | bytes 32400000 | tf_op jit(solution)/shard_map/attention_weight_grads/pallas_call | solution.py:62
  167.6 5.6 %norm_one_grad.1 = (bf16[2,1040,256]{2,1,0:T(8,128)(2,1)S(1)}, bf16[2,1040,256]{2,1,0:T(8,128)(2,1)S(1)}) custom-call(s32[4]{0:T(128)S(1)} %pad_add_fusion.sc, bf16[1024,768]{1,0:T(8,128)(2,1)S(1)} %copy-done.9, bf16[1024,256]{1,0:T(8,128)(2,1)S(1)} %copy-done.30, bf16[1024,512]{1,0:T(8,128)(2,1)S(1)} %copy-done.13, bf16[1024,3072]{1,0:T(8,128)(2,1)} %wv.1, ...), custom_call_target="tpu_custom_call" | custom-call | flops 13454999552 | bytes 42120000 | tf_op jit(solution)/shard_map/norm_one_grad/pallas_call | solution.py:62
  175.0 3.3 %collective-permute-done.24.refs_1_ = bf16[2,1024,128]{2,1,0:T(8,128)(2,1)S(1)} collective-permute-done((bf16[2,1024,128]{2,1,0:T(8,128)(2,1)S(1)}, bf16[2,1024,128]{2,1,0:T(8,128)(2,1)S(1)}, u32[]{:S(2)}, u32[]{:S(2)}) %collective-permute-start.24) | collective-permute-done | bytes 524320 | tf_op jit(solution)/shard_map/ppermute | solution.py:50
  178.9 4.2 %trunk_head.1 = (bf16[8,128,192]{2,1,0:T(8,128)(2,1)S(1)}, f32[256,576]{1,0:T(8,128)S(1)}, f32[8,256]{1,0:T(8,128)S(1)}) custom-call(s32[4]{0:T(128)S(1)} %pad_add_fusion.sc, f32[512,256]{1,0:T(8,128)S(1)} %copy-done.24, f32[512,256]{1,0:T(8,128)S(1)} %copy-done.22, bf16[2,2,528,256]{3,2,1,0:T(8,128)(2,1)S(1)} %get-tuple-element.179.a, ...), custom_call_target="tpu_custom_call" | custom-call | flops 8049999872 | bytes 25200000 | tf_op jit(solution)/shard_map/trunk_head/pallas_call | solution.py:62
  191.4 8.1 %collective-permute-done.32.refs_2_ = bf16[1,1040,256]{2,1,0:T(8,128)(2,1)S(1)} collective-permute-done((bf16[1,1040,256]{2,1,0:T(8,128)(2,1)S(1)}, bf16[1,1040,256]{2,1,0:T(8,128)(2,1)S(1)}, u32[]{:S(2)}, u32[]{:S(2)}) %collective-permute-start.32) | collective-permute-done | bytes 532512 | tf_op jit(solution)/shard_map/ppermute | solution.py:50
  199.5 6.1 %embed_back.1 = (bf16[2,2,2,128,192]{4,3,2,1,0:T(8,128)(2,1)S(1)}, bf16[2,2,2,128,192]{4,3,2,1,0:T(8,128)(2,1)S(1)}, bf16[2,32,1280]{2,1,0:T(8,128)(2,1)S(1)}, b...) custom-call(s32[4]{0:T(128)S(1)} %pad_add_fusion.sc, ...), custom_call_target="tpu_custom_call" | custom-call | flops 10350000128 | bytes 32400000 | tf_op jit(solution)/shard_map/embed_back/pallas_call | solution.py:62
  213.0 3.4 %collective-permute-done.54 = bf16[2,32,1280]{2,1,0:T(8,128)(2,1)S(1)} collective-permute-done((bf16[2,32,1280]{2,1,0:T(8,128)(2,1)S(1)}, bf16[2,32,1280]{2,1,0:T(8,128)(2,1)S(1)}, u32[]{:S(2)}, u32[]{:S(2)}) %collective-permute-start.54) | collective-permute-done | bytes 163872 | tf_op jit(solution)/shard_map/ppermute | solution.py:50
  217.2 6.8 %collective-permute-done.36.g_ref = bf16[1,1024,128]{2,1,0:T(8,128)(2,1)S(1)} collective-permute-done((bf16[1,1024,128]{2,1,0:T(8,128)(2,1)S(1)}, bf16[1,1024,128]{2,1,0:T(8,128)(2,1)S(1)}, u32[]{:S(2)}, u32[]{:S(2)}) %collective-permute-start.36) | collective-permute-done | bytes 262176 | tf_op jit(solution)/shard_map/ppermute | solution.py:50
  232.3 3.9 %collective-permute-done.34 = bf16[2,2,128,192]{3,2,1,0:T(8,128)(2,1)S(1)} collective-permute-done((bf16[2,2,128,192]{3,2,1,0:T(8,128)(2,1)S(1)}, bf16[2,2,128,192]{3,2,1,0:T(8,128)(2,1)S(1)}, u32[]{:S(2)}, u32[]{:S(2)}) %collective-permute-start.34) | collective-permute-done | bytes 196640 | tf_op jit(solution)/shard_map/ppermute | solution.py:50
  238.5 4.3 %collective-permute-done.56.refs_1_ = bf16[32,1280]{1,0:T(8,128)(2,1)S(1)} collective-permute-done((bf16[32,1280]{1,0:T(8,128)(2,1)S(1)}, bf16[32,1280]{1,0:T(8,128)(2,1)S(1)}, u32[]{:S(2)}, u32[]{:S(2)}) %collective-permute-start.56) | collective-permute-done | bytes 81952 | tf_op jit(solution)/shard_map/ppermute | solution.py:50
  248.1 4.4 %mlp_grads_out.1 = (f32[512,1024]{1,0:T(8,128)}, f32[128,4096]{1,0:T(8,128)}) custom-call(s32[4]{0:T(128)S(1)} %pad_add_fusion.sc, bf16[1024,128]{1,0:T(8,128)(2,1)S(1)} %get-tuple-element.190.refs_0_, bf16[1024,128]{1,0:T(8,128)(2,1)S(1)} %collective-permute-done.37.refs_1_, bf16[1024,128]{1,0:T(8,128)(2,1)S(1)} %collective-permute-done.38.refs_2_, ...), custom_call_target="tpu_custom_call" | custom-call | flops 5405000192 | bytes 16920000 | tf_op jit(solution)/shard_map/mlp_grads_out/pallas_call | solution.py:62
  255.8 3.1 %collective-permute-done.51.refs_3_ = bf16[4,2,128,128]{3,2,1,0:T(8,128)(2,1)S(1)} collective-permute-done((bf16[4,2,128,128]{3,2,1,0:T(8,128)(2,1)S(1)}, bf16[4,2,128,128]{3,2,1,0:T(8,128)(2,1)S(1)}, u32[]{:S(2)}, u32[]{:S(2)}) %collective-permute-start.51) | collective-permute-done | bytes 262176 | tf_op jit(solution)/shard_map/ppermute | solution.py:50
  258.9 3.7 %attention_grads_out.1 = (f32[128,3072]{1,0:T(8,128)}, f32[128,1024]{1,0:T(8,128)}) custom-call(s32[4]{0:T(128)S(1)} %pad_add_fusion.sc, bf16[4,2,128,128]{3,2,1,0:T(8,128)(2,1)S(1)} %pad_maximum_fusion.3.refs_0_, bf16[4,2,128,128]{3,2,1,0:T(8,128)(2,1)S(1)} %collective-permute-done.49.refs_1_, bf16[4,2,128,128]{3,2,1,0:T(8,128)(2,1)S(1)} %collective-permute-done.50.refs_2_, ...), custom_call_target="tpu_custom_call" | custom-call | flops 4024999936 | bytes 12600000 | tf_op jit(solution)/shard_map/attention_grads_out/pallas_call | solution.py:62
  (227 shorter events, 98.1 us)
Async XLA Ops:
  13.1 31.3 %collective-permute-start.9 = (bf16[2,128,192]{2,1,0:T(8,128)(2,1)S(1)}, bf16[2,128,192]{2,1,0:T(8,128)(2,1)S(1)}, u32[]{:S(2)}, u32[]{:S(2)}) collective-permute-start(bf16[2,128,192]{2,1,0:T(8,128)(2,1)S(1)} %pad_maximum_fusion.5.refs_0_), channel_id=1, source_target_pairs={{0,1},{1,0},{2,3},{3,2},{4,5},{5,4},{6,7},{7,6},{8,9},{9,8},{10,11... | collective-permute-start | bytes 294920 | tf_op jit(solution)/shard_map/ppermute | solution.py:50
  18.2 26.7 %collective-permute-start.11 = (bf16[2,128,192]{2,1,0:T(8,128)(2,1)S(1)}, bf16[2,128,192]{2,1,0:T(8,128)(2,1)S(1)}, u32[]{:S(2)}, u32[]{:S(2)}) collective-permute-start(bf16[2,128,192]{2,1,0:T(8,128)(2,1)S(1)} %collective-permute-done.10.refs_2_), channel_id=1, source_target_pairs={{0,1},{1,0},{2,3},{3,2},{4,5},{5,4},{6,7},{7,6},{8,9},{9,8},{10,11... | collective-permute-start | bytes 294920 | tf_op jit(solution)/shard_map/ppermute | solution.py:50
  44.4 27.2 %collective-permute-start.5 = (bf16[512,256]{1,0:T(8,128)(2,1)S(1)}, bf16[512,256]{1,0:T(8,128)(2,1)S(1)}, u32[]{:S(2)}, u32[]{:S(2)}) collective-permute-start(bf16[512,256]{1,0:T(8,128)(2,1)S(1)} %get-tuple-element.128.refs_0_.refs_2_), channel_id=1, source_target_pairs={{0,1},{1,0},{2,3},{3,2},{4,5},{5,4},{6,7},{7,6},{8,9},{9,8},{10,11... | collective-permute-start | bytes 786440 | tf_op jit(solution)/shard_map/ppermute | solution.py:50
  52.6 19.0 %collective-permute-start.6 = (bf16[512,256]{1,0:T(8,128)(2,1)S(1)}, bf16[512,256]{1,0:T(8,128)(2,1)S(1)}, u32[]{:S(2)}, u32[]{:S(2)}) collective-permute-start(bf16[512,256]{1,0:T(8,128)(2,1)S(1)} %collective-permute-done.4.refs_2_), channel_id=1, source_target_pairs={{0,1},{1,0},{2,3},{3,2},{4,5},{5,4},{6,7},{7,6},{8,9},{9,8},{10,11... | collective-permute-start | bytes 786440 | tf_op jit(solution)/shard_map/ppermute | solution.py:50
  69.8 26.1 %collective-permute-start.15 = (bf16[256,1024]{1,0:T(8,128)(2,1)S(1)}, bf16[256,1024]{1,0:T(8,128)(2,1)S(1)}, u32[]{:S(2)}, u32[]{:S(2)}) collective-permute-start(bf16[256,1024]{1,0:T(8,128)(2,1)S(1)} %get-tuple-element.146), channel_id=1, source_target_pairs={{0,2},{1,3},{2,0},{3,1},{4,6},{5,7},{6,4},{7,5},{8,10},{9,11},{10,... | collective-permute-start | bytes 1572872 | tf_op jit(solution)/shard_map/ppermute | solution.py:50
  70.1 25.8 %collective-permute-start.16 = (bf16[256,1024]{1,0:T(8,128)(2,1)S(1)}, bf16[256,1024]{1,0:T(8,128)(2,1)S(1)}, u32[]{:S(2)}, u32[]{:S(2)}) collective-permute-start(bf16[256,1024]{1,0:T(8,128)(2,1)S(1)} %get-tuple-element.147), channel_id=1, source_target_pairs={{0,3},{1,2},{2,1},{3,0},{4,7},{5,6},{6,5},{7,4},{8,11},{9,10},{10,... | collective-permute-start | bytes 1572872 | tf_op jit(solution)/shard_map/ppermute | solution.py:50
  95.6 27.4 %collective-permute-start.26 = (bf16[2,2,528,256]{3,2,1,0:T(8,128)(2,1)S(1)}, bf16[2,2,528,256]{3,2,1,0:T(8,128)(2,1)S(1)}, u32[]{:S(2)}, u32[]{:S(2)}) collective-permute-start(bf16[2,2,528,256]{3,2,1,0:T(8,128)(2,1)S(1)} %get-tuple-element.142), channel_id=1, source_target_pairs={{0,1},{1,0},{2,3},{3,2},{4,5},{5,4},{6,7},{7,6},{8,9},{9,8},{10,11... | collective-permute-start | bytes 3244040 | tf_op jit(solution)/shard_map/ppermute | solution.py:50
  98.5 14.2 %collective-permute-start.17 = (bf16[256,1024]{1,0:T(8,128)(2,1)S(1)}, bf16[256,1024]{1,0:T(8,128)(2,1)S(1)}, u32[]{:S(2)}, u32[]{:S(2)}) collective-permute-start(bf16[256,1024]{1,0:T(8,128)(2,1)S(1)} %norm_two_back.1.refs_5_), channel_id=1, source_target_pairs={{0,2},{1,3},{2,0},{3,1},{4,6},{5,7},{6,4},{7,5},{8,10},{9,11},{10,... | collective-permute-start | bytes 1572872 | tf_op jit(solution)/shard_map/ppermute | solution.py:50
  109.3 25.7 %collective-permute-start.21 = (bf16[2,2,1024,128]{3,2,1,0:T(8,128)(2,1)S(1)}, bf16[2,2,1024,128]{3,2,1,0:T(8,128)(2,1)}, u32[]{:S(2)}, u32[]{:S(2)}) collective-permute-start(bf16[2,2,1024,128]{3,2,1,0:T(8,128)(2,1)S(1)} %get-tuple-element.153), channel_id=1, source_target_pairs={{0,16},{8,24},{16,0},{24,8},{1,17},{9,25},{17,1},{25,9},{2,18},{10... | collective-permute-start | bytes 3145736 | tf_op jit(solution)/shard_map/ppermute | solution.py:50
  111.0 26.9 %collective-permute-start.20 = (bf16[2,2,1024,128]{3,2,1,0:T(8,128)(2,1)S(1)}, bf16[2,2,1024,128]{3,2,1,0:T(8,128)(2,1)S(1)}, u32[]{:S(2)}, u32[]{:S(2)}) collective-permute-start(bf16[2,2,1024,128]{3,2,1,0:T(8,128)(2,1)S(1)} %get-tuple-element.158), channel_id=1, source_target_pairs={{0,8},{8,0},{16,24},{24,16},{1,9},{9,1},{17,25},{25,17},{2,10},{10... | collective-permute-start | bytes 3145736 | tf_op jit(solution)/shard_map/ppermute | solution.py:50
  112.7 26.9 %collective-permute-start.19 = (bf16[256,1024]{1,0:T(8,128)(2,1)S(1)}, bf16[256,1024]{1,0:T(8,128)(2,1)S(1)}, u32[]{:S(2)}, u32[]{:S(2)}) collective-permute-start(bf16[256,1024]{1,0:T(8,128)(2,1)S(1)} %collective-permute-done.17.refs_5_), channel_id=1, source_target_pairs={{0,1},{1,0},{2,3},{3,2},{4,5},{5,4},{6,7},{7,6},{8,9},{9,8},{10,11... | collective-permute-start | bytes 1572872 | tf_op jit(solution)/shard_map/ppermute | solution.py:50
  123.9 55.0 %collective-permute-start.27 = (bf16[1,2,528,256]{3,2,1,0:T(8,128)(2,1)}, bf16[1,2,528,256]{3,2,1,0:T(8,128)(2,1)S(1)}, u32[]{:S(2)}, u32[]{:S(2)}) collective-permute-start(bf16[1,2,528,256]{3,2,1,0:T(8,128)(2,1)} %add_convert_fusion), channel_id=1, source_target_pairs={{0,2},{1,3},{2,0},{3,1},{4,6},{5,7},{6,4},{7,5},{8,10},{9,11},{10,... | collective-permute-start | bytes 1622024 | tf_op jit(solution)/shard_map/ppermute | solution.py:50
  158.0 15.3 %collective-permute-start.25 = (bf16[2,1024,128]{2,1,0:T(8,128)(2,1)S(1)}, bf16[2,1024,128]{2,1,0:T(8,128)(2,1)S(1)}, u32[]{:S(2)}, u32[]{:S(2)}) collective-permute-start(bf16[2,1024,128]{2,1,0:T(8,128)(2,1)S(1)} %get-tuple-element.171), channel_id=1, source_target_pairs={{0,16},{8,24},{16,0},{24,8},{1,17},{9,25},{17,1},{25,9},{2,18},{10... | collective-permute-start | bytes 1572872 | tf_op jit(solution)/shard_map/ppermute | solution.py:50
  162.6 24.7 %collective-permute-start.31 = (bf16[2,1024,128]{2,1,0:T(8,128)(2,1)S(1)}, bf16[2,1024,128]{2,1,0:T(8,128)(2,1)S(1)}, u32[]{:S(2)}, u32[]{:S(2)}) collective-permute-start(bf16[2,1024,128]{2,1,0:T(8,128)(2,1)S(1)} %get-tuple-element.173), channel_id=1, source_target_pairs={{0,4},{1,5},{2,6},{3,7},{4,0},{5,1},{6,2},{7,3},{8,12},{9,13},{10,... | collective-permute-start | bytes 1572872 | tf_op jit(solution)/shard_map/ppermute | solution.py:50
  184.4 15.1 %collective-permute-start.32 = (bf16[1,1040,256]{2,1,0:T(8,128)(2,1)S(1)}, bf16[1,1040,256]{2,1,0:T(8,128)(2,1)S(1)}, u32[]{:S(2)}, u32[]{:S(2)}) collective-permute-start(bf16[1,1040,256]{2,1,0:T(8,128)(2,1)S(1)} %add_convert_fusion.1), channel_id=1, source_target_pairs={{0,2},{1,3},{2,0},{3,1},{4,6},{5,7},{6,4},{7,5},{8,10},{9,11},{10,... | collective-permute-start | bytes 1597448 | tf_op jit(solution)/shard_map/ppermute | solution.py:50
  188.0 22.0 %collective-permute-start.38 = (bf16[1024,128]{1,0:T(8,128)(2,1)S(1)}, bf16[1024,128]{1,0:T(8,128)(2,1)S(1)}, u32[]{:S(2)}, u32[]{:S(2)}) collective-permute-start(bf16[1024,128]{1,0:T(8,128)(2,1)S(1)} %get-tuple-element.190.refs_0_), channel_id=1, source_target_pairs={{0,16},{8,24},{16,0},{24,8},{1,17},{9,25},{17,1},{25,9},{2,18},{10... | collective-permute-start | bytes 786440 | tf_op jit(solution)/shard_map/ppermute | solution.py:50
  189.6 16.1 %collective-permute-start.40 = (bf16[2,128,128]{2,1,0:T(8,128)(2,1)S(1)}, bf16[2,128,128]{2,1,0:T(8,128)(2,1)S(1)}, u32[]{:S(2)}, u32[]{:S(2)}) collective-permute-start(bf16[2,128,128]{2,1,0:T(8,128)(2,1)S(1)} %get-tuple-element.208), channel_id=1, source_target_pairs={{0,1},{1,0},{2,3},{3,2},{4,5},{5,4},{6,7},{7,6},{8,9},{9,8},{10,11... | collective-permute-start | bytes 196616 | tf_op jit(solution)/shard_map/ppermute | solution.py:50
  189.6 17.3 %collective-permute-start.41 = (bf16[2,128,128]{2,1,0:T(8,128)(2,1)S(1)}, bf16[2,128,128]{2,1,0:T(8,128)(2,1)S(1)}, u32[]{:S(2)}, u32[]{:S(2)}) collective-permute-start(bf16[2,128,128]{2,1,0:T(8,128)(2,1)S(1)} %get-tuple-element.209), channel_id=1, source_target_pairs={{0,2},{1,3},{2,0},{3,1},{4,6},{5,7},{6,4},{7,5},{8,10},{9,11},{10,... | collective-permute-start | bytes 196616 | tf_op jit(solution)/shard_map/ppermute | solution.py:50
  189.8 19.4 %collective-permute-start.42 = (bf16[2,128,128]{2,1,0:T(8,128)(2,1)S(1)}, bf16[2,128,128]{2,1,0:T(8,128)(2,1)S(1)}, u32[]{:S(2)}, u32[]{:S(2)}) collective-permute-start(bf16[2,128,128]{2,1,0:T(8,128)(2,1)S(1)} %get-tuple-element.210), channel_id=1, source_target_pairs={{0,3},{1,2},{2,1},{3,0},{4,7},{5,6},{6,5},{7,4},{8,11},{9,10},{10,... | collective-permute-start | bytes 196616 | tf_op jit(solution)/shard_map/ppermute | solution.py:50
  209.1 14.9 %collective-permute-start.36 = (bf16[1,1024,128]{2,1,0:T(8,128)(2,1)S(1)}, bf16[1,1024,128]{2,1,0:T(8,128)(2,1)S(1)}, u32[]{:S(2)}, u32[]{:S(2)}) collective-permute-start(bf16[1,1024,128]{2,1,0:T(8,128)(2,1)S(1)} %get-tuple-element.202), channel_id=1, source_target_pairs={{0,4},{1,5},{2,6},{3,7},{4,0},{5,1},{6,2},{7,3},{8,12},{9,13},{10,... | collective-permute-start | bytes 786440 | tf_op jit(solution)/shard_map/ppermute | solution.py:50
  210.0 21.5 %collective-permute-start.43 = (bf16[4,2,128,128]{3,2,1,0:T(8,128)(2,1)S(1)}, bf16[4,2,128,128]{3,2,1,0:T(8,128)(2,1)S(1)}, u32[]{:S(2)}, u32[]{:S(2)}) collective-permute-start(bf16[4,2,128,128]{3,2,1,0:T(8,128)(2,1)S(1)} %pad_maximum_fusion.2.refs_4_), channel_id=1, source_target_pairs={{0,8},{8,0},{16,24},{24,16},{1,9},{9,1},{17,25},{25,17},{2,10},{10... | collective-permute-start | bytes 786440 | tf_op jit(solution)/shard_map/ppermute | solution.py:50
  230.2 14.3 %collective-permute-start.39 = (bf16[1024,128]{1,0:T(8,128)(2,1)S(1)}, bf16[1024,128]{1,0:T(8,128)(2,1)S(1)}, u32[]{:S(2)}, u32[]{:S(2)}) collective-permute-start(bf16[1024,128]{1,0:T(8,128)(2,1)S(1)} %collective-permute-done.38.refs_2_), channel_id=1, source_target_pairs={{0,8},{8,0},{16,24},{24,16},{1,9},{9,1},{17,25},{25,17},{2,10},{10... | collective-permute-start | bytes 786440 | tf_op jit(solution)/shard_map/ppermute | solution.py:50
  236.7 25.9 %collective-permute-start.57 = (bf16[32,1280]{1,0:T(8,128)(2,1)S(1)}, bf16[32,1280]{1,0:T(8,128)(2,1)S(1)}, u32[]{:S(2)}, u32[]{:S(2)}) collective-permute-start(bf16[32,1280]{1,0:T(8,128)(2,1)S(1)} %fusion.5.refs_0_), channel_id=1, source_target_pairs={{0,16},{8,24},{16,0},{24,8},{1,17},{9,25},{17,1},{25,9},{2,18},{10... | collective-permute-start | bytes 245768 | tf_op jit(solution)/shard_map/ppermute | solution.py:50
  242.8 19.8 %collective-permute-start.58 = (bf16[32,1280]{1,0:T(8,128)(2,1)S(1)}, bf16[32,1280]{1,0:T(8,128)(2,1)S(1)}, u32[]{:S(2)}, u32[]{:S(2)}) collective-permute-start(bf16[32,1280]{1,0:T(8,128)(2,1)S(1)} %collective-permute-done.56.refs_1_), channel_id=1, source_target_pairs={{0,16},{8,24},{16,0},{24,8},{1,17},{9,25},{17,1},{25,9},{2,18},{10... | collective-permute-start | bytes 245768 | tf_op jit(solution)/shard_map/ppermute | solution.py:50
  (70 other events, 544.1 us)
